TPU v7x, 32 devices: a whole 2x2x4 slice. The times are simulated.
32 devices in a mesh: row: 8 (over z, core), col: 4 (over y, x).
Axes of the slice: x: 2, y: 2, z: 4, core: 2. Of those that a mesh axis runs over, the one named last changes fastest.
Arguments:
- spins_up: int32 [5120, 8192], P('row', 'col'), may hold values from 0 to 1
- uniforms: float32 [2, 5120, 8192], P(None, 'row', 'col'), may hold values from 0 to 1
- moments: bfloat16 [5120, 8192], P('row', 'col'), may hold values from 0.5 to 2
- accept_bar: float32 [2], replicated, may hold values from 0.06 to 0.6, as said below
Outputs:
- spins_out: float32 [5120, 8192], P('row', 'col')
- corr: float32 [2048], P(('row', 'col'))
Inputs may be any that keep to these rules, and one draw needn't show every extreme that they name: accept_bar[1] equals accept_bar[0] squared, as exp(-8 beta) and exp(-4 beta) for one inverse temperature beta of the draw.
All inputs are finite; a program needn't handle non-finite values.
Results may differ from a plain program's by a relative error of at most 0.0003.
Values may be sent and summed in bfloat16 or wider, within the bound.
No kernel may reach another device: no remote copies, remote signals or barrier semaphores. Data moves between devices by JAX's collectives and lax.ppermute only.
A program may use at most 128 MiB of HBM per device.

v0:
```python
import math

import jax
import jax.numpy as jnp
from jax import lax
from jax.sharding import PartitionSpec as P

R = 2048
SWEEPS = 2


def with_halo(value, sides, width):
    for axis, dim in sides:
        count, length = (lax.axis_size(axis), value.shape[dim])
        up = [(i, (i + 1) % count) for i in range(count)]
        down = [(j, i) for i, j in up]
        last = lax.slice_in_dim(value, length - width, length, axis=dim)
        leading = lax.slice_in_dim(value, 0, width, axis=dim)
        before = lax.ppermute(last, axis, up)
        after = lax.ppermute(leading, axis, down)
        value = jnp.concatenate([before, value, after], axis=dim)
    return value


def shifted_2(block, axis, distance):
    devices = range(lax.axis_size(axis))
    route = [((i - distance) % len(devices), i) for i in devices]
    return lax.ppermute(block, axis, route)


def update_colour(padded, uniform_draws, accept_bar, colour):
    centre = padded[1:-1, 1:-1]
    neighbours = padded[2:, 1:-1] + padded[:-2, 1:-1] + padded[1:-1, 2:] + padded[1:-1, :-2]
    alignment = centre * neighbours
    threshold = jnp.where(alignment > 3.0, accept_bar[1], accept_bar[0])
    row_ids = lax.broadcasted_iota(jnp.int32, centre.shape, 0)
    col_ids = lax.broadcasted_iota(jnp.int32, centre.shape, 1)
    coloured = (row_ids + col_ids) % 2 == colour
    flipped = coloured & ((alignment <= 0.0) | (uniform_draws < threshold))
    return jnp.where(flipped, -centre, centre)


def correlate(left_cells, right_cells, max_distance, tile_width):
    row_count = left_cells.shape[0]
    tile_count = left_cells.shape[1] // tile_width
    offsets = max_distance // tile_width
    left_tiles = left_cells.reshape(row_count, tile_count, tile_width)
    right_tiles = right_cells.reshape(row_count, tile_count + offsets, tile_width)

    def product(offset):
        shifted = lax.dynamic_slice_in_dim(right_tiles, offset, tile_count, 1)
        return jnp.einsum("itp,itq->pq", left_tiles, shifted, preferred_element_type=jnp.float32)

    products = lax.map(product, jnp.arange(offsets + 1, dtype=jnp.int32))
    paired = jnp.concatenate([products[:-1], products[1:]], axis=2)
    flattened = paired.reshape(offsets, tile_width * 2 * tile_width)
    flattened = jnp.pad(flattened, ((0, 0), (0, tile_width)))
    skewed = flattened.reshape(offsets, tile_width, 2 * tile_width + 1)[:, :, :tile_width]
    return jnp.sum(skewed, axis=1).reshape(max_distance)


def on_device(spins_up, uniforms, moments, accept_bar):
    lattice = (2 * spins_up - 1).astype(jnp.float32)
    wide_draws = with_halo(uniforms, (("row", 1), ("col", 2)), 1)
    for sweep_index in range(SWEEPS):
        padded = with_halo(lattice.astype(jnp.bfloat16), (("row", 0), ("col", 1)), 2).astype(
            lattice.dtype
        )
        middle = update_colour(padded, wide_draws[sweep_index], accept_bar, 0)
        lattice = update_colour(middle, uniforms[sweep_index], accept_bar, 1)
    weighted = moments * lattice.astype(jnp.bfloat16)
    columns = weighted.shape[1]
    tile_width = 128
    following = shifted_2(weighted, "col", -1)
    extended = jnp.concatenate([weighted, following], axis=1)
    partial_sums = correlate(weighted, extended, R, tile_width)
    row_devices = lax.axis_size("row")
    col_devices = lax.axis_size("col")
    normaliser = 1.0 / math.sqrt(lattice.shape[0] * row_devices * columns * col_devices)
    owned_sums = lax.psum_scatter(partial_sums, ("row", "col"), scatter_dimension=0, tiled=True)
    return (lattice, owned_sums * normaliser)


def solution(mesh):
    placed = (P("row", "col"), P(None, "row", "col"), P("row", "col"), P())
    return jax.shard_map(
        on_device,
        mesh=mesh,
        in_specs=placed,
        out_specs=(P("row", "col"), P(("row", "col"))),
        check_vma=False,
    )
```

profile of v0, /device:TPU:0, one launch (start us, length us, event | category | flops | bytes accessed | tf_op | source)
XLA Modules:
  0.0 348.8 jit_solution(6484806380018169895)
XLA Ops:
  0.6 3.2 convert_convert_fusion
  3.9 4.6 %collective-permute-start.1 = (bf16[2,2048]{1,0:T(2,128)(2,1)S(1)}, bf16[2,2048]{1,0:T(2,128)(2,1)S(1)}, u32[]{:S(2)}, u32[]{:S(2)}) collective-permute-start(bf16[2,2048]{1,0:T(2,128)(2,1)S(1)} %get-tuple-element.75), channel_id=1, source_target_pairs={{4,0},{8,4},{12,8},{16,12},{20,16},{24,20},{28,24},{0,28},{5,1},{9... | collective-permute-start | bytes 24584 | tf_op jit(solution)/shard_map/ppermute | solution.py:20
  9.5 3.6 %collective-permute-start.5 = (f32[2,1,2048]{2,1,0:T(1,128)S(1)}, f32[2,1,2048]{2,1,0:T(1,128)S(1)}, u32[]{:S(2)}, u32[]{:S(2)}) collective-permute-start(f32[2,1,2048]{2,1,0:T(1,128)S(1)} %get-tuple-element.67), channel_id=1, source_target_pairs={{4,0},{8,4},{12,8},{16,12},{20,16},{24,20},{28,24},{0,28},{5,1},{9... | collective-permute-start | bytes 49160 | tf_op jit(solution)/shard_map/ppermute | solution.py:20
  18.0 5.3 %pad_maximum_fusion = f32[2,642,2048]{2,1,0:T(8,128)S(1)} fusion(f32[2,1,2048]{2,1,0:T(1,128)S(1)} %collective-permute-done.5, f32[2,640,2048]{2,1,0:T(8,128)} %param.7, f32[2,1,2048]{2,1,0:T(1,128)S(1)} %collective-permute-done.4), kind=kLoop, calls=%fused_computation.5 | loop fusion | flops 5259264 | bytes 21037056 | tf_op jit(solution)/shard_map/concatenate | solution.py:21
  23.3 3.9 %copy-done = f32[2,642,2048]{2,1,0:T(8,128)} copy-done((f32[2,642,2048]{2,1,0:T(8,128)}, f32[2,642,2048]{2,1,0:T(8,128)S(1)}, u32[]{:S(2)}) %copy-start) | copy-done | bytes 10518552
  31.7 6.1 %concatenate.25 = bf16[644,2052]{1,0:T(8,128)(2,1)} concatenate(bf16[644,2]{1,0:T(8,128)(2,1)S(1)} %collective-permute-done.2, bf16[644,2048]{1,0:T(8,128)(2,1)} %copy-done.1, bf16[644,2]{1,0:T(8,128)(2,1)S(1)} %collective-permute-done.3), dimensions={1} | concatenate | bytes 5285952 | tf_op jit(solution)/shard_map/concatenate | solution.py:21
  37.8 4.7 %convert_element_type.22 = f32[644,2052]{1,0:T(8,128)} convert(bf16[644,2052]{1,0:T(8,128)(2,1)} %concatenate.25) | non-fusion elementwise | flops 1321488 | bytes 7928928 | tf_op jit(solution)/shard_map/convert_element_type | solution.py:66
  43.0 13.9 %concatenate.27 = f32[2,642,2050]{2,1,0:T(8,128)} concatenate(f32[2,642,1]{2,1,0:T(8,128)S(1)} %copy.24, f32[2,642,2048]{2,1,0:T(8,128)} %copy-done, f32[2,642,1]{2,1,0:T(8,128)S(1)} %copy.25), dimensions={2} | concatenate | bytes 21057600 | tf_op jit(solution)/shard_map/concatenate | solution.py:21
  56.9 19.9 %negate_select_fusion.1 = f32[642,2050]{1,0:T(8,128)S(1)} fusion(f32[2,642,2050]{2,1,0:T(8,128)} %concatenate.27, f32[644,2052]{1,0:T(8,128)} %convert_element_type.22, f32[]{:T(128)} %bitcast.6, f32[]{:T(128)} %bitcast.5), kind=kLoop, calls=%fused_computation.7 | loop fusion | flops 32902500 | bytes 36850808 | tf_op jit(solution)/shard_map/jit(_where)/select_n | solution.py:40
  76.9 10.0 %fusion.24 = bf16[640,2048]{1,0:T(8,128)(2,1)S(1)} fusion(f32[2,640,2048]{2,1,0:T(8,128)} %param.7, f32[642,2050]{1,0:T(8,128)S(1)} %negate_select_fusion.1, f32[]{:T(128)} %bitcast.6, f32[]{:T(128)} %bitcast.5), kind=kLoop, calls=%fused_computation.39 | loop fusion | flops 34078720 | bytes 34078728 | tf_op jit(solution)/shard_map/convert_element_type | solution.py:66
  89.6 3.5 %collective-permute-done.8 = bf16[2,2048]{1,0:T(2,128)(2,1)S(1)} collective-permute-done((bf16[2,2048]{1,0:T(2,128)(2,1)S(1)}, bf16[2,2048]{1,0:T(2,128)(2,1)S(1)}, u32[]{:S(2)}, u32[]{:S(2)}) %collective-permute-start.8) | collective-permute-done | bytes 8224 | tf_op jit(solution)/shard_map/ppermute | solution.py:19
  98.5 3.3 collective-permute-done.10
  103.7 6.0 %concatenate.29 = bf16[644,2052]{1,0:T(8,128)(2,1)} concatenate(bf16[644,2]{1,0:T(8,128)(2,1)S(1)} %collective-permute-done.10, bf16[644,2048]{1,0:T(8,128)(2,1)} %copy-done.2, bf16[644,2]{1,0:T(8,128)(2,1)S(1)} %collective-permute-done.11), dimensions={1} | concatenate | bytes 5285952 | tf_op jit(solution)/shard_map/concatenate | solution.py:21
  111.9 10.1 %negate_select_fusion = f32[642,2050]{1,0:T(8,128)S(1)} fusion(f32[2,642,2050]{2,1,0:T(8,128)} %concatenate.27, f32[644,2052]{1,0:T(8,128)S(1)} %convert_element_type.24, f32[]{:T(128)} %bitcast.6, f32[]{:T(128)} %bitcast.5), kind=kLoop, calls=%fused_computation.6 | loop fusion | flops 32902500 | bytes 36850808 | tf_op jit(solution)/shard_map/jit(_where)/select_n | solution.py:40
  122.0 12.3 %convert_multiply_fusion = (bf16[640,2048]{1,0:T(8,128)(2,1)}, f32[640,2048]{1,0:T(8,128)}) fusion(bf16[640,2048]{1,0:T(8,128)(2,1)S(1)} %copy-done.3, f32[]{:T(128)} %bitcast.6, f32[]{:T(128)} %bitcast.5, f32[2,640,2048]{2,1,0:T(8,128)} %param.7, f32[642,2050]{1,0:T(8,128)S(1)} %negate_select_fusion), kind=kLoop, calls=%fused_computation.62 | loop fusion | flops 39321600 | bytes 41943048 | tf_op jit(solution)/shard_map/mul | solution.py:71
  137.8 50.7 %collective-permute-done.12 = bf16[640,2048]{1,0:T(8,128)(2,1)} collective-permute-done((bf16[640,2048]{1,0:T(8,128)(2,1)}, bf16[640,2048]{1,0:T(8,128)(2,1)}, u32[]{:S(2)}, u32[]{:S(2)}) %collective-permute-start.12) | collective-permute-done | bytes 2621472 | tf_op jit(solution)/shard_map/ppermute | solution.py:28
  188.5 5.5 %pad_maximum_fusion.1 = bf16[640,4096]{1,0:T(8,128)(2,1)} fusion(bf16[640,2048]{1,0:T(8,128)(2,1)} %collective-permute-done.12, bf16[640,2048]{1,0:T(8,128)(2,1)} %get-tuple-element.62), kind=kLoop, calls=%fused_computation.48 | loop fusion | flops 10485760 | bytes 10485760 | tf_op jit(solution)/shard_map/concatenate | solution.py:75
  194.1 7.8 %copy.29 = bf16[640,4096]{0,1:T(8,128)(2,1)} copy(bf16[640,4096]{1,0:T(8,128)(2,1)} %pad_maximum_fusion.1) | data formatting | bytes 10485760 | tf_op jit(solution)/shard_map/while | solution.py:54
  201.9 96.2 %while.10 = (s32[]{:T(128)}, f32[17,128,128]{1,2,0:T(8,128)}, s32[17]{0:T(128)S(1)}, bf16[640,32,128]{0,2,1:T(8,128)(2,1)}, bf16[640,16,128]{2,0,1:T(8,128)(2,1)S(1)}, /*index=5*/s32[]{:T(128)}, s32[]{:T(128)}, s32[]{:T(128)}) while((s32[]{:T(128)}, f32[17,128,128]{1,2,0:T(8,128)}, s32[17]{0:T(128)S(1)}, bf16[640,32,128]{0,2,1:T(8,128)(2,1)}, ...), condition=%wide.region_1.2_spmd, body=%wide.region_0.1_spmd.sunk | while | flops 335544320 | bytes 5308563 | solution.py:54
  227.0 3.2 fusion.49
  289.2 3.2 fusion.49
  294.9 3.2 fusion.49
  303.6 3.6 %reshape.22 = f32[16,128,257]{2,1,0:T(8,128)} reshape(f32[16,32896]{1,0:T(8,128)S(1)} %pad.4) | data formatting | bytes 4210688 | tf_op jit(solution)/shard_map/reshape | solution.py:58
  308.6 39.7 %all-reduce.1 = f32[2048]{0:T(1024)S(1)} all-reduce(f32[2048]{0:T(1024)S(1)} %bitcast.68), channel_id=2, replica_groups=mesh['row'=8,'col'=4] {'row','col'}, use_global_device_ids=true, to_apply=%region_3.4.clone | all-reduce | flops 2048 | bytes 16384
  (84 shorter events, 89.0 us)
Async XLA Ops:
  3.9 9.2 %collective-permute-start.1 = (bf16[2,2048]{1,0:T(2,128)(2,1)S(1)}, bf16[2,2048]{1,0:T(2,128)(2,1)S(1)}, u32[]{:S(2)}, u32[]{:S(2)}) collective-permute-start(bf16[2,2048]{1,0:T(2,128)(2,1)S(1)} %get-tuple-element.75), channel_id=1, source_target_pairs={{4,0},{8,4},{12,8},{16,12},{20,16},{24,20},{28,24},{0,28},{5,1},{9... | collective-permute-start | bytes 24584 | tf_op jit(solution)/shard_map/ppermute | solution.py:20
  8.5 4.9 %collective-permute-start = (bf16[2,2048]{1,0:T(2,128)(2,1)S(1)}, bf16[2,2048]{1,0:T(2,128)(2,1)S(1)}, u32[]{:S(2)}, u32[]{:S(2)}) collective-permute-start(bf16[2,2048]{1,0:T(2,128)(2,1)S(1)} %get-tuple-element.74), channel_id=1, source_target_pairs={{0,4},{4,8},{8,12},{12,16},{16,20},{20,24},{24,28},{28,0},{1,5},{5... | collective-permute-start | bytes 24584 | tf_op jit(solution)/shard_map/ppermute | solution.py:19
  9.5 7.7 %collective-permute-start.5 = (f32[2,1,2048]{2,1,0:T(1,128)S(1)}, f32[2,1,2048]{2,1,0:T(1,128)S(1)}, u32[]{:S(2)}, u32[]{:S(2)}) collective-permute-start(f32[2,1,2048]{2,1,0:T(1,128)S(1)} %get-tuple-element.67), channel_id=1, source_target_pairs={{4,0},{8,4},{12,8},{16,12},{20,16},{24,20},{28,24},{0,28},{5,1},{9... | collective-permute-start | bytes 49160 | tf_op jit(solution)/shard_map/ppermute | solution.py:20
  13.1 5.0 %collective-permute-start.4 = (f32[2,1,2048]{2,1,0:T(1,128)S(1)}, f32[2,1,2048]{2,1,0:T(1,128)S(1)}, u32[]{:S(2)}, u32[]{:S(2)}) collective-permute-start(f32[2,1,2048]{2,1,0:T(1,128)S(1)} %get-tuple-element.66), channel_id=1, source_target_pairs={{0,4},{4,8},{8,12},{12,16},{16,20},{20,24},{24,28},{28,0},{1,5},{5... | collective-permute-start | bytes 49160 | tf_op jit(solution)/shard_map/ppermute | solution.py:19
  14.0 3.1 copy-start.1
  14.2 17.6 %collective-permute-start.2 = (bf16[644,2]{1,0:T(8,128)(2,1)S(1)}, bf16[644,2]{1,0:T(8,128)(2,1)S(1)}, u32[]{:S(2)}, u32[]{:S(2)}) collective-permute-start(bf16[644,2]{1,0:T(8,128)(2,1)S(1)} %get-tuple-element.71), channel_id=1, source_target_pairs={{0,1},{1,2},{2,3},{3,0},{4,5},{5,6},{6,7},{7,4},{8,9},{9,10},{10,1... | collective-permute-start | bytes 7736 | tf_op jit(solution)/shard_map/ppermute | solution.py:19
  15.7 15.4 %copy-start.4 = (f32[2]{0:T(128)S(1)}, f32[2]{0:T(128)}, u32[]{:S(2)}) copy-start(f32[2]{0:T(128)} %param.9) | copy-start | bytes 28
  15.7 16.0 %collective-permute-start.3 = (bf16[644,2]{1,0:T(8,128)(2,1)S(1)}, bf16[644,2]{1,0:T(8,128)(2,1)S(1)}, u32[]{:S(2)}, u32[]{:S(2)}) collective-permute-start(bf16[644,2]{1,0:T(8,128)(2,1)S(1)} %get-tuple-element.70), channel_id=1, source_target_pairs={{1,0},{2,1},{3,2},{0,3},{5,4},{6,5},{7,6},{4,7},{9,8},{10,9},{11,1... | collective-permute-start | bytes 7736 | tf_op jit(solution)/shard_map/ppermute | solution.py:20
  23.3 3.9 %copy-start = (f32[2,642,2048]{2,1,0:T(8,128)}, f32[2,642,2048]{2,1,0:T(8,128)S(1)}, u32[]{:S(2)}) copy-start(f32[2,642,2048]{2,1,0:T(8,128)S(1)} %pad_maximum_fusion) | copy-start | bytes 31555588
  27.7 14.8 %collective-permute-start.6 = (f32[2,642,1]{1,0,2:T(2,128)S(1)}, f32[2,642,1]{1,0,2:T(2,128)S(1)}, u32[]{:S(2)}, u32[]{:S(2)}) collective-permute-start(f32[2,642,1]{1,0,2:T(2,128)S(1)} %copy.22), channel_id=1, source_target_pairs={{0,1},{1,2},{2,3},{3,0},{4,5},{5,6},{6,7},{7,4},{8,9},{9,10},{10,1... | collective-permute-start | bytes 15416 | tf_op jit(solution)/shard_map/ppermute | solution.py:19
  29.5 13.3 %collective-permute-start.7 = (f32[2,642,1]{1,0,2:T(2,128)S(1)}, f32[2,642,1]{1,0,2:T(2,128)S(1)}, u32[]{:S(2)}, u32[]{:S(2)}) collective-permute-start(f32[2,642,1]{1,0,2:T(2,128)S(1)} %copy.23), channel_id=1, source_target_pairs={{1,0},{2,1},{3,2},{0,3},{5,4},{6,5},{7,6},{4,7},{9,8},{10,9},{11,1... | collective-permute-start | bytes 15416 | tf_op jit(solution)/shard_map/ppermute | solution.py:20
  86.9 2.7 collective-permute-start.9
  88.3 4.9 %collective-permute-start.8 = (bf16[2,2048]{1,0:T(2,128)(2,1)S(1)}, bf16[2,2048]{1,0:T(2,128)(2,1)S(1)}, u32[]{:S(2)}, u32[]{:S(2)}) collective-permute-start(bf16[2,2048]{1,0:T(2,128)(2,1)S(1)} %get-tuple-element.72), channel_id=1, source_target_pairs={{0,4},{4,8},{8,12},{12,16},{16,20},{20,24},{24,28},{28,0},{1,5},{5... | collective-permute-start | bytes 24584 | tf_op jit(solution)/shard_map/ppermute | solution.py:19
  93.8 1.6 copy-start.2
  95.5 6.3 %collective-permute-start.10 = (bf16[644,2]{1,0:T(8,128)(2,1)S(1)}, bf16[644,2]{1,0:T(8,128)(2,1)S(1)}, u32[]{:S(2)}, u32[]{:S(2)}) collective-permute-start(bf16[644,2]{1,0:T(8,128)(2,1)S(1)} %get-tuple-element.69), channel_id=1, source_target_pairs={{0,1},{1,2},{2,3},{3,0},{4,5},{5,6},{6,7},{7,4},{8,9},{9,10},{10,1... | collective-permute-start | bytes 7736 | tf_op jit(solution)/shard_map/ppermute | solution.py:19
  95.9 7.7 %collective-permute-start.11 = (bf16[644,2]{1,0:T(8,128)(2,1)S(1)}, bf16[644,2]{1,0:T(8,128)(2,1)S(1)}, u32[]{:S(2)}, u32[]{:S(2)}) collective-permute-start(bf16[644,2]{1,0:T(8,128)(2,1)S(1)} %get-tuple-element.68), channel_id=1, source_target_pairs={{1,0},{2,1},{3,2},{0,3},{5,4},{6,5},{7,6},{4,7},{9,8},{10,9},{11,1... | collective-permute-start | bytes 7736 | tf_op jit(solution)/shard_map/ppermute | solution.py:20
  111.9 10.1 %copy-start.3 = (bf16[640,2048]{1,0:T(8,128)(2,1)S(1)}, bf16[640,2048]{1,0:T(8,128)(2,1)}, u32[]{:S(2)}) copy-start(bf16[640,2048]{1,0:T(8,128)(2,1)} %param.8) | copy-start | bytes 7864324
  134.3 54.2 %collective-permute-start.12 = (bf16[640,2048]{1,0:T(8,128)(2,1)}, bf16[640,2048]{1,0:T(8,128)(2,1)}, u32[]{:S(2)}, u32[]{:S(2)}) collective-permute-start(bf16[640,2048]{1,0:T(8,128)(2,1)} %get-tuple-element.62), channel_id=1, source_target_pairs={{1,0},{2,1},{3,2},{0,3},{5,4},{6,5},{7,6},{4,7},{9,8},{10,9},{11,1... | collective-permute-start | bytes 7864328 | tf_op jit(solution)/shard_map/ppermute | solution.py:28
where the time goes:
time: 351 us; the launch traced here: 349 us
  other arithmetic  76.6 us (22%)
  local copies, waits for them, and re-layouts  63.9 us (18%)
  waiting for transfers between devices  61.9 us (18%)
  matrix products  54.5 us (16%)
  blocking collectives  39.7 us (11%)
  loops' own time  31.6 us (9%)
  starting transfers between devices  19.7 us (6%)
    dot_general x17, matrix products, product(): jnp.einsum('itp,itq->pq', left_tiles, shifted, preferred_element_type=jnp...  54.5 us
    ppermute x1, waiting for transfers between devices, shifted_2(): return lax.ppermute(block, axis, route)  50.7 us
    unnamed x1, blocking collectives  39.7 us
    another operation x1, loops' own time, correlate(): products = lax.map(product, jnp.arange(offsets + 1, dtype=jnp.int32))  31.6 us
    select_n x2, other arithmetic, update_colour(): return jnp.where(flipped, -centre, centre)  30 us
    concatenate x3, local copies, waits for them, and re-layouts, with_halo(): value = jnp.concatenate([before, value, after], axis=dim)  26 us
    ppermute x6, starting transfers between devices, with_halo(): after = lax.ppermute(leading, axis, down)  15.1 us
    convert_element_type x2, other arithmetic, on_device(): lattice.astype(jnp.bfloat16)  13.3 us
  transfers between devices with their start and end apart: 13, of which 7 were waited for; matrix products, arithmetic and copies ran while one was open for 6% of the time, Pallas kernels for 0%

commit v1 on v0

v1 whole, which is shorter than its diff:
```python
import functools
import math

import jax
import jax.numpy as jnp
from jax import lax
from jax.experimental import pallas as pl
from jax.experimental.pallas import tpu as pltpu
from jax.sharding import PartitionSpec as P

R = 2048
SWEEPS = 2
DEPTH = 32
LANES = 128
TILE = 256
PER_STEP = 2


def params(**more):
    return pltpu.CompilerParams(vmem_limit_bytes=48 << 20, **more)


def pack_kernel(bar_ref, spins_ref, draws_ref, words_ref, last_ref, first_ref):
    step = pl.program_id(0)
    planes = pl.num_programs(0) * PER_STEP
    columns = words_ref.shape[2]

    @pl.when(step == 0)
    def _():
        words_ref[...] = jnp.zeros_like(words_ref)

    for left in range(0, columns, TILE):
        lanes = pl.ds(left, TILE)
        words = [words_ref[w, :, lanes] for w in range(1 + 2 * SWEEPS)]
        for plane in range(PER_STEP):
            place = step * PER_STEP + plane + 1
            bit = jnp.int32(1) << place
            rows = pl.ds(plane * DEPTH, DEPTH)
            words[0] = words[0] | (spins_ref[rows, lanes] << place)
            for k in range(SWEEPS):
                draw = draws_ref[k, rows, lanes]
                for c in range(2):
                    word = words[1 + 2 * k + c]
                    words[1 + 2 * k + c] = jnp.where(draw < bar_ref[c], word | bit, word)
        for w, word in enumerate(words):
            words_ref[w, :, lanes] = word

    @pl.when(step == pl.num_programs(0) - 1)
    def _():
        for ref, top, place in ((last_ref, DEPTH - 8, planes), (first_ref, 0, 1)):
            bits = [
                (words_ref[w, top : top + 8, :] >> place) & 1 for w in range(1 + 2 * SWEEPS)
            ]
            ref[...] = strips(bits, True)


def strips(bits, pad):
    parts = [bits[0]] + [bits[1 + 2 * k] + 2 * bits[2 + 2 * k] for k in range(SWEEPS)]
    if pad:
        parts.append(jnp.zeros_like(parts[0]))
    return jnp.concatenate(parts, axis=0).astype(jnp.float32).astype(jnp.bfloat16)


def unstrips(ref, height):
    parts = [
        ref[k * height : (k + 1) * height, :].astype(jnp.float32).astype(jnp.int32)
        for k in range(1 + SWEEPS)
    ]
    bits = [parts[0]]
    for code in parts[1:]:
        bits += [code & 1, code >> 1]
    return bits


def spread(word):
    for shift in (4, 8, 16, 32, 64):
        word = word | pltpu.roll(word, shift, 1)
    return word


def rows_kernel(words_ref, above_ref, below_ref, joined_ref, right_ref, left_ref, *, planes):
    columns = words_ref.shape[2]
    joined_ref[...] = words_ref[...]
    above, below = unstrips(above_ref, 8), unstrips(below_ref, 8)
    for w in range(1 + 2 * SWEEPS):
        joined_ref[w, DEPTH - 8 :, :] = words_ref[w, DEPTH - 8 :, :] | above[w]
        joined_ref[w, :8, :] = words_ref[w, :8, :] | (below[w] << (planes + 1))
    lane = lax.broadcasted_iota(jnp.int32, (DEPTH, LANES), 1)
    for ref, at, held in (
        (right_ref, columns - LANES, lane >= LANES - 4),
        (left_ref, 0, lane < 4),
    ):
        bits = []
        for w in range(1 + 2 * SWEEPS):
            edge = jnp.where(held, joined_ref[w, :, at : at + LANES], 0)
            bits.append((spread(edge) >> (lane // 4)) & 1)
        ref[...] = strips(bits, False)


def sweeps_of(words):
    spins = words[0]
    width = spins.shape[1]
    row = lax.broadcasted_iota(jnp.int32, spins.shape, 0)
    parity = (row + lax.broadcasted_iota(jnp.int32, spins.shape, 1)) & 1
    for k in range(SWEEPS):
        for colour in range(2):
            up = pltpu.roll(spins, 1, 0)
            up = jnp.where(row == 0, up << 1, up)
            down = pltpu.roll(spins, DEPTH - 1, 0)
            down = jnp.where(row == DEPTH - 1, down >> 1, down)
            a, b = up ^ spins, down ^ spins
            c, d = pltpu.roll(spins, 1, 1) ^ spins, pltpu.roll(spins, width - 1, 1) ^ spins
            either, other = a | b, c | d
            some = either | other
            several = (a & b) | (c & d) | (either & other)
            flips = several | (some & words[1 + 2 * k]) | (words[2 + 2 * k] & ~some)
            spins = jnp.where(parity == colour, spins ^ flips, spins)
    return spins


def sweep_kernel(words_ref, before_ref, after_ref, spins_ref):
    columns = words_ref.shape[2]
    lane = lax.broadcasted_iota(jnp.int32, (DEPTH, LANES), 1)
    before, after = unstrips(before_ref, DEPTH), unstrips(after_ref, DEPTH)
    words = [
        jnp.concatenate(
            [
                spread(before[w] << (lane // 4)),
                words_ref[w],
                spread(after[w] << (lane // 4)),
            ],
            axis=1,
        )
        for w in range(1 + 2 * SWEEPS)
    ]
    spins_ref[...] = sweeps_of(words)[:, LANES : LANES + columns]


def weigh_kernel(half_ref, spins_ref, moments_ref, out_ref):
    first = (half_ref[0] * pl.num_programs(0) + pl.program_id(0)) * PER_STEP + 1
    for plane in range(PER_STEP):
        bit = jnp.int32(1) << (first + plane)
        rows = pl.ds(plane * DEPTH, DEPTH)
        for t in range(out_ref.shape[0]):
            lanes = pl.ds(t * TILE, TILE)
            size = moments_ref[rows, lanes].astype(jnp.float32)
            up = (spins_ref[:, lanes] & bit) != 0
            out_ref[t, rows, :] = jnp.where(up, size, -size).astype(jnp.bfloat16)


def spell_kernel(spins_ref, out_ref):
    first = pl.program_id(0) * PER_STEP + 1
    for plane in range(PER_STEP):
        bit = jnp.int32(1) << (first + plane)
        rows = pl.ds(plane * DEPTH, DEPTH)
        out_ref[rows, :] = jnp.where((spins_ref[...] & bit) != 0, 1.0, -1.0)


def gram(left, right):
    depth = left.shape[0] * left.shape[1]
    return lax.dot_general(
        left.reshape(depth, TILE),
        right.reshape(depth, TILE),
        (((0,), (0,)), ((), ())),
        preferred_element_type=jnp.float32,
    )


def fold(sums_ref):
    width = R + LANES
    value = sums_ref[:LANES, :width] + sums_ref[LANES:, LANES : LANES + width]
    height = LANES // 2
    while height >= 8:
        value = value[:height] + pltpu.roll(value[height:], width - height, 1)
        height //= 2
    return value


def own_kernel(first_ref, second_ref, out_ref, sums_ref):
    tiles = first_ref.shape[0]
    for n in range(tiles):
        sums_ref[:, n * TILE : (n + 1) * TILE] = gram(
            first_ref[: tiles - n], first_ref[n:]
        ) + gram(second_ref[: tiles - n], second_ref[n:])
    sums_ref[:, tiles * TILE :] = jnp.zeros((TILE, TILE), jnp.float32)
    out_ref[...] = fold(sums_ref)


def next_kernel(odd_ref, own_ref, mid_ref, far_ref, base_ref, out_ref, sums_ref, ends_ref, sems):
    odd = odd_ref[0]
    copies = (
        pltpu.make_async_copy(own_ref, ends_ref.at[odd], sems.at[0]),
        pltpu.make_async_copy(far_ref, ends_ref.at[1 - odd], sems.at[1]),
    )
    for copy in copies:
        copy.start()
    for copy in copies:
        copy.wait()
    tiles = mid_ref.shape[0]
    sums_ref[:, :TILE] = jnp.zeros((TILE, TILE), jnp.float32)
    for n in range(1, tiles + 1):
        sums_ref[:, n * TILE : (n + 1) * TILE] = gram(
            ends_ref[0, tiles - n :], mid_ref[:n]
        ) + gram(mid_ref[tiles - n :], ends_ref[1, :n])
    value = fold(sums_ref) + base_ref[...]
    for height in (4, 2, 1):
        value = value + pltpu.roll(pltpu.roll(value, value.shape[1] - height, 1), 8 - height, 0)
    out_ref[...] = value[:1, :R]


def on_device(spins_up, uniforms, moments, accept_bar):
    rows, columns = spins_up.shape
    planes, tiles = rows // DEPTH, columns // TILE
    half_rows = rows // 2
    row_devices, col_devices = lax.axis_size("row"), lax.axis_size("col")
    assert columns == R and col_devices % 2 == 0 and planes + 2 <= 26
    count = 1 + 2 * SWEEPS
    block = PER_STEP * DEPTH
    vmem = pl.BlockSpec(memory_space=pltpu.VMEM)
    smem = pl.BlockSpec(memory_space=pltpu.SMEM)
    anywhere = pl.BlockSpec(memory_space=pl.ANY)
    strip_shape = jax.ShapeDtypeStruct((8 * (2 + SWEEPS), columns), jnp.bfloat16)
    edge_shape = jax.ShapeDtypeStruct((DEPTH * (1 + SWEEPS), LANES), jnp.bfloat16)
    words_shape = jax.ShapeDtypeStruct((count, DEPTH, columns), jnp.int32)

    words, last, leading = pl.pallas_call(
        pack_kernel,
        grid=(rows // block,),
        in_specs=[
            smem,
            pl.BlockSpec((block, columns), lambda i: (i, 0)),
            pl.BlockSpec((SWEEPS, block, columns), lambda i: (0, i, 0)),
        ],
        out_specs=[
            pl.BlockSpec(words_shape.shape, lambda i: (0, 0, 0)),
            pl.BlockSpec(strip_shape.shape, lambda i: (0, 0)),
            pl.BlockSpec(strip_shape.shape, lambda i: (0, 0)),
        ],
        out_shape=[words_shape, strip_shape, strip_shape],
        compiler_params=params(),
        name="pack",
    )(accept_bar, spins_up, uniforms)

    def ring(size, step):
        return [(i, (i + step) % size) for i in range(size)]

    above = lax.ppermute(last, "row", ring(row_devices, 1))
    below = lax.ppermute(leading, "row", ring(row_devices, -1))
    joined, right, left = pl.pallas_call(
        functools.partial(rows_kernel, planes=planes),
        in_specs=[vmem] * 3,
        out_specs=[vmem] * 3,
        out_shape=[words_shape, edge_shape, edge_shape],
        compiler_params=params(),
        name="rows",
    )(words, above, below)
    before = lax.ppermute(right, "col", ring(col_devices, 1))
    after = lax.ppermute(left, "col", ring(col_devices, -1))
    spins = pl.pallas_call(
        sweep_kernel,
        in_specs=[vmem] * 3,
        out_specs=vmem,
        out_shape=jax.ShapeDtypeStruct((DEPTH, columns), jnp.int32),
        compiler_params=params(),
        name="sweep",
    )(joined, before, after)

    odd = lax.axis_index("col") % 2

    def weigh(half):
        steps = half_rows // block
        return pl.pallas_call(
            weigh_kernel,
            grid_spec=pltpu.PrefetchScalarGridSpec(
                num_scalar_prefetch=1,
                grid=(steps,),
                in_specs=[
                    pl.BlockSpec((DEPTH, columns), lambda i, h: (0, 0)),
                    pl.BlockSpec((block, columns), lambda i, h: (h[0] * steps + i, 0)),
                ],
                out_specs=pl.BlockSpec((tiles, block, TILE), lambda i, h: (0, i, 0)),
            ),
            out_shape=jax.ShapeDtypeStruct((tiles, half_rows, TILE), jnp.bfloat16),
            compiler_params=params(),
            name="weigh",
        )(half.reshape(1), spins, moments)

    given, kept = weigh(1 - odd), weigh(odd)
    mid = lax.ppermute(given, "col", [(i, i ^ 1) for i in range(col_devices)])
    far = lax.ppermute(
        kept, "col", [(i, (i - 2 + 4 * (i % 2)) % col_devices) for i in range(col_devices)]
    )
    spins_out = pl.pallas_call(
        spell_kernel,
        grid=(rows // block,),
        in_specs=[pl.BlockSpec((DEPTH, columns), lambda i: (0, 0))],
        out_specs=pl.BlockSpec((block, columns), lambda i: (i, 0)),
        out_shape=jax.ShapeDtypeStruct((rows, columns), jnp.float32),
        compiler_params=params(),
        cost_estimate=pl.CostEstimate(
            flops=rows * columns, bytes_accessed=4 * rows * columns, transcendentals=0
        ),
        name="spell",
    )(spins)
    sums = pltpu.VMEM((TILE, R + TILE), jnp.float32)
    base = pl.pallas_call(
        own_kernel,
        in_specs=[vmem] * 2,
        out_specs=vmem,
        out_shape=jax.ShapeDtypeStruct((8, R + LANES), jnp.float32),
        scratch_shapes=[sums],
        compiler_params=params(),
        cost_estimate=pl.CostEstimate(
            flops=rows * columns * columns, bytes_accessed=2 * rows * columns, transcendentals=0
        ),
        name="own",
    )(given, kept)
    partial_sums = pl.pallas_call(
        next_kernel,
        in_specs=[smem, anywhere, vmem, anywhere, vmem],
        out_specs=vmem,
        out_shape=jax.ShapeDtypeStruct((1, R), jnp.float32),
        scratch_shapes=[
            sums,
            pltpu.VMEM((2, tiles, half_rows, TILE), jnp.bfloat16),
            pltpu.SemaphoreType.DMA((2,)),
        ],
        compiler_params=params(),
        name="next",
    )(odd.reshape(1), kept, mid, far, base)
    normaliser = 1.0 / math.sqrt(rows * row_devices * columns * col_devices)
    devices = row_devices * col_devices
    shares = lax.all_to_all(
        partial_sums.reshape(devices, R // devices), ("row", "col"), 0, 0, tiled=True
    )
    return spins_out, jnp.sum(shares, axis=0) * normaliser


def solution(mesh):
    placed = (P("row", "col"), P(None, "row", "col"), P("row", "col"), P())
    return jax.shard_map(
        on_device,
        mesh=mesh,
        in_specs=placed,
        out_specs=(P("row", "col"), P(("row", "col"))),
        check_vma=False,
    )
```

time: 351 us -> 79.4 us (0.23)
  other arithmetic: 76.6 us -> 1.23 us
  local copies, waits for them, and re-layouts: 63.9 us -> 4.2 us
  matrix products: 54.5 us -> 0 us
  blocking collectives: 39.7 us -> 0 us
  loops' own time: 31.6 us -> 0 us
  waiting for transfers between devices: 61.9 us -> 35.1 us
  Pallas kernels: 0 us -> 25.1 us
  starting transfers between devices: 19.7 us -> 12.6 us
    dot_general x17 -> x0, matrix products: 54.5 us -> none  [product(): jnp.einsum('itp,itq->pq', left_tiles, shifted, preferred_element_type=jnp...]
    unnamed x1 -> x0, blocking collectives: 39.7 us -> none
    another operation x1 -> x0, loops' own time: 31.6 us -> none  [correlate(): products = lax.map(product, jnp.arange(offsets + 1, dtype=jnp.int32))]
    select_n x2 -> x0, other arithmetic: 30 us -> none  [update_colour(): return jnp.where(flipped, -centre, centre)]
    ppermute x13 -> x6, waiting for transfers between devices: 61.9 us -> 32.4 us  [the longest x1 25.1 us: on_device(): mid = lax.ppermute(given, 'col', [(i, i ^ 1) for i in range(col_devices)])]
    concatenate x3 -> x0, local copies, waits for them, and re-layouts: 26 us -> none  [with_halo(): value = jnp.concatenate([before, value, after], axis=dim)]
    pallas_call x0 -> x8, Pallas kernels: none -> 25.1 us  [the longest x1 9.35 us: on_device(): pl.pallas_call(pack_kernel, grid=(rows // block,), in_specs=[smem, pl.Blo...]
    convert_element_type x4 -> x0, other arithmetic: 20.2 us -> none  [the longest x2 13.3 us: on_device(): lattice.astype(jnp.bfloat16)]
  transfers between devices with their start and end apart: 13 -> 7, of which waited for: 7 -> 6; matrix products, arithmetic and copies ran while one was open for 6% -> 0% of each run, Pallas kernels for 0% -> 10%
where the time goes in v1:
time: 79.4 us; the launch traced here: 79 us
  waiting for transfers between devices  35.1 us (44%)
  Pallas kernels  25.1 us (32%)
  starting transfers between devices  12.6 us (16%)
  local copies, waits for them, and re-layouts  4.2 us (5%)
  other arithmetic  1.23 us (2%)
    ppermute x1, waiting for transfers between devices, on_device(): mid = lax.ppermute(given, 'col', [(i, i ^ 1) for i in range(col_devices)])  25.1 us
    pallas_call x1, Pallas kernels, on_device(): pl.pallas_call(pack_kernel, grid=(rows // block,), in_specs=[smem, pl.Blo...  9.35 us
    pallas_call x1, Pallas kernels, on_device(): pl.pallas_call(spell_kernel, grid=(rows // block,), in_specs=[pl.BlockSpe...  4.44 us
    pallas_call x1, Pallas kernels, on_device(): pl.pallas_call(next_kernel, in_specs=[smem, anywhere, vmem, anywhere, vme...  4.18 us
    ppermute x1, starting transfers between devices, on_device(): below = lax.ppermute(leading, 'row', ring(row_devices, -1))  4.09 us
    pallas_call x1, Pallas kernels, on_device(): pl.pallas_call(own_kernel, in_specs=[vmem] * 2, out_specs=vmem, out_shape...  3.78 us
    unnamed x8, local copies, waits for them, and re-layouts  3.02 us
    all_to_all x1, waiting for transfers between devices, on_device(): lax.all_to_all(partial_sums.reshape(devices, R // devices), ('row', 'col'...  2.76 us
  transfers between devices with their start and end apart: 7, of which 6 were waited for; matrix products, arithmetic and copies ran while one was open for 0% of the time, Pallas kernels for 10%

profile of v1, /device:TPU:0, one launch (start us, length us, event | category | flops | bytes accessed | tf_op | source)
XLA Modules:
  0.0 79.0 jit_solution(4092869179102371158)
XLA Ops:
  0.6 0.6 copy-done.3
  1.3 9.3 %pack.1 = (s32[5,32,2048]{2,1,0:T(8,128)S(1)}, bf16[32,2048]{1,0:T(8,128)(2,1)S(1)}, bf16[32,2048]{1,0:T(8,128)(2,1)S(1)}) custom-call(f32[2]{0:T(128)S(1)} %copy-done.3, s32[640,2048]{1,0:T(8,128)} %spins_ref.1, f32[2,640,2048]{2,1,0:T(8,128)} %draws_ref.1), custom_call_target="tpu_custom_call" | custom-call | tf_op jit(solution)/shard_map/pack/pallas_call | solution.py:226
  10.6 0.5 collective-permute-start
  11.2 4.1 %collective-permute-start.1 = (bf16[32,2048]{1,0:T(8,128)(2,1)S(1)}, bf16[32,2048]{1,0:T(8,128)(2,1)S(1)}, u32[]{:S(2)}, u32[]{:S(2)}) collective-permute-start(bf16[32,2048]{1,0:T(8,128)(2,1)S(1)} %get-tuple-element.10), channel_id=1, source_target_pairs={{0,28},{4,0},{8,4},{12,8},{16,12},{20,16},{24,20},{28,24},{1,29},{... | collective-permute-start | bytes 393224 | tf_op jit(solution)/shard_map/ppermute | solution.py:248
  15.3 2.7 %collective-permute-done.above_ref = bf16[32,2048]{1,0:T(8,128)(2,1)S(1)} collective-permute-done((bf16[32,2048]{1,0:T(8,128)(2,1)S(1)}, bf16[32,2048]{1,0:T(8,128)(2,1)S(1)}, u32[]{:S(2)}, u32[]{:S(2)}) %collective-permute-start) | collective-permute-done | bytes 131104 | tf_op jit(solution)/shard_map/ppermute | solution.py:247
  18.5 1.0 %copy-done.1 = s32[5,32,2048]{2,1,0:T(8,128)} copy-done((s32[5,32,2048]{2,1,0:T(8,128)}, s32[5,32,2048]{2,1,0:T(8,128)S(1)}, u32[]{:S(2)}) %copy-start.1) | copy-done | bytes 1310744
  19.5 2.0 %collective-permute-start.2 = (bf16[96,128]{1,0:T(8,128)(2,1)S(1)}, bf16[96,128]{1,0:T(8,128)(2,1)S(1)}, u32[]{:S(2)}, u32[]{:S(2)}) collective-permute-start(bf16[96,128]{1,0:T(8,128)(2,1)S(1)} %get-tuple-element.12), channel_id=1, source_target_pairs={{0,1},{1,2},{2,3},{3,0},{4,5},{5,6},{6,7},{7,4},{8,9},{9,10},{10,1... | collective-permute-start | bytes 73736 | tf_op jit(solution)/shard_map/ppermute | solution.py:257
  21.5 1.0 %collective-permute-start.3 = (bf16[96,128]{1,0:T(8,128)(2,1)S(1)}, bf16[96,128]{1,0:T(8,128)(2,1)S(1)}, u32[]{:S(2)}, u32[]{:S(2)}) collective-permute-start(bf16[96,128]{1,0:T(8,128)(2,1)S(1)} %get-tuple-element.13), channel_id=1, source_target_pairs={{0,3},{1,0},{2,1},{3,2},{4,7},{5,4},{6,5},{7,6},{8,11},{9,8},{10,9... | collective-permute-start | bytes 73736 | tf_op jit(solution)/shard_map/ppermute | solution.py:258
  22.5 1.8 %collective-permute-done.2.before_ref = bf16[96,128]{1,0:T(8,128)(2,1)S(1)} collective-permute-done((bf16[96,128]{1,0:T(8,128)(2,1)S(1)}, bf16[96,128]{1,0:T(8,128)(2,1)S(1)}, u32[]{:S(2)}, u32[]{:S(2)}) %collective-permute-start.2) | collective-permute-done | bytes 24608 | tf_op jit(solution)/shard_map/ppermute | solution.py:257
  24.3 1.3 %collective-permute-done.3.after_ref = bf16[96,128]{1,0:T(8,128)(2,1)S(1)} collective-permute-done((bf16[96,128]{1,0:T(8,128)(2,1)S(1)}, bf16[96,128]{1,0:T(8,128)(2,1)S(1)}, u32[]{:S(2)}, u32[]{:S(2)}) %collective-permute-start.3) | collective-permute-done | bytes 24608 | tf_op jit(solution)/shard_map/ppermute | solution.py:258
  25.6 1.3 %copy-done.2 = s32[5,32,2048]{2,1,0:T(8,128)S(1)} copy-done((s32[5,32,2048]{2,1,0:T(8,128)S(1)}, s32[5,32,2048]{2,1,0:T(8,128)}, u32[]{:S(2)}) %copy-start.2) | copy-done | bytes 1310744
  26.9 1.6 %sweep.1.spins_ref = s32[32,2048]{1,0:T(8,128)S(1)} custom-call(s32[5,32,2048]{2,1,0:T(8,128)S(1)} %copy-done.2, bf16[96,128]{1,0:T(8,128)(2,1)S(1)} %collective-permute-done.2.before_ref, bf16[96,128]{1,0:T(8,128)(2,1)S(1)} %collective-permute-done.3.after_ref), custom_call_target="tpu_custom_call" | custom-call | tf_op jit(solution)/shard_map/sweep/pallas_call | solution.py:259
  28.5 0.6 weigh.3.first_ref
  29.2 0.6 weigh.2.second_ref.own_ref
  29.8 2.3 %collective-permute-start.4 = (bf16[8,320,256]{2,1,0:T(8,128)(2,1)S(1)}, bf16[8,320,256]{2,1,0:T(8,128)(2,1)S(1)}, u32[]{:S(2)}, u32[]{:S(2)}) collective-permute-start(bf16[8,320,256]{2,1,0:T(8,128)(2,1)S(1)} %weigh.3.first_ref), channel_id=1, source_target_pairs={{0,1},{1,0},{2,3},{3,2},{4,5},{5,4},{6,7},{7,6},{8,9},{9,8},{10,11... | collective-permute-start | bytes 3932168 | tf_op jit(solution)/shard_map/ppermute | solution.py:289
  32.2 3.8 %own.1.base_ref = f32[8,2176]{1,0:T(8,128)S(1)} custom-call(bf16[8,320,256]{2,1,0:T(8,128)(2,1)S(1)} %weigh.3.first_ref, bf16[8,320,256]{2,1,0:T(8,128)(2,1)S(1)} %weigh.2.second_ref.own_ref), custom_call_target="tpu_custom_call" | custom-call | flops 2684354560 | bytes 2621440 | tf_op jit(solution)/shard_map/own/pallas_call | solution.py:306
  36.0 25.1 %collective-permute-done.4.mid_ref = bf16[8,320,256]{2,1,0:T(8,128)(2,1)S(1)} collective-permute-done((bf16[8,320,256]{2,1,0:T(8,128)(2,1)S(1)}, bf16[8,320,256]{2,1,0:T(8,128)(2,1)S(1)}, u32[]{:S(2)}, u32[]{:S(2)}) %collective-permute-start.4) | collective-permute-done | bytes 1310752 | tf_op jit(solution)/shard_map/ppermute | solution.py:289
  61.1 1.5 %collective-permute-done.5.far_ref = bf16[8,320,256]{2,1,0:T(8,128)(2,1)S(1)} collective-permute-done((bf16[8,320,256]{2,1,0:T(8,128)(2,1)S(1)}, bf16[8,320,256]{2,1,0:T(8,128)(2,1)S(1)}, u32[]{:S(2)}, u32[]{:S(2)}) %collective-permute-start.5) | collective-permute-done | bytes 1310752 | tf_op jit(solution)/shard_map/ppermute | solution.py:290
  62.6 4.2 %next.1 = f32[1,2048]{1,0:T(1,128)S(1)} custom-call(s32[1]{0:T(128)} %bitcast.half_ref.odd_ref, bf16[8,320,256]{2,1,0:T(8,128)(2,1)S(1)} %weigh.2.second_ref.own_ref, bf16[8,320,256]{2,1,0:T(8,128)(2,1)S(1)} %collective-permute-done.4.mid_ref, bf16[8,320,256]{2,1,0:T(8,128)(2,1)S(1)} %collective-permute-done.5.far_ref, f32[8,2176]{1,0:T(8,128)S(1)} %own.1.base_ref), custom_call_target="tpu_custom_call" | custom-call | tf_op jit(solution)/shard_map/next/pallas_call | solution.py:318
  67.3 0.7 reduce.4
  67.9 0.7 all_to_all.6
  68.6 2.7 %all-to-all-start = ((f32[32,1,64]{2,1,0:T(1,128)}), f32[32,1,64]{2,1,0:T(1,128)S(1)}, u32[]{:S(2)}, u32[]{:S(2)}) async-start(f32[32,1,64]{2,1,0:T(1,128)} %bitcast.2), calls=%async_computation | async-start | bytes 32768 | tf_op jit(solution)/shard_map/all_to_all | solution.py:333
  71.3 4.4 %spell.1 = f32[640,2048]{1,0:T(8,128)} custom-call(s32[32,2048]{1,0:T(8,128)S(1)} %sweep.1.spins_ref), custom_call_target="tpu_custom_call" | custom-call | flops 1310720 | bytes 5242880 | tf_op jit(solution)/shard_map/spell/pallas_call | solution.py:293
  75.7 2.8 %all-to-all-done = f32[32,1,64]{2,1,0:T(1,128)S(1)} async-done(((f32[32,1,64]{2,1,0:T(1,128)}), f32[32,1,64]{2,1,0:T(1,128)S(1)}, u32[]{:S(2)}, u32[]{:S(2)}) %all-to-all-start) | async-done | bytes 8224 | tf_op jit(solution)/shard_map/all_to_all | solution.py:333
  (11 shorter events, 1.6 us)
Async XLA Ops:
  0.6 0.7 copy-start.3
  10.6 7.3 %collective-permute-start = (bf16[32,2048]{1,0:T(8,128)(2,1)S(1)}, bf16[32,2048]{1,0:T(8,128)(2,1)S(1)}, u32[]{:S(2)}, u32[]{:S(2)}) collective-permute-start(bf16[32,2048]{1,0:T(8,128)(2,1)S(1)} %get-tuple-element.9), channel_id=1, source_target_pairs={{0,4},{4,8},{8,12},{12,16},{16,20},{20,24},{24,28},{28,0},{1,5},{5... | collective-permute-start | bytes 393224 | tf_op jit(solution)/shard_map/ppermute | solution.py:247
  11.2 6.8 %collective-permute-start.1 = (bf16[32,2048]{1,0:T(8,128)(2,1)S(1)}, bf16[32,2048]{1,0:T(8,128)(2,1)S(1)}, u32[]{:S(2)}, u32[]{:S(2)}) collective-permute-start(bf16[32,2048]{1,0:T(8,128)(2,1)S(1)} %get-tuple-element.10), channel_id=1, source_target_pairs={{0,28},{4,0},{8,4},{12,8},{16,12},{20,16},{24,20},{28,24},{1,29},{... | collective-permute-start | bytes 393224 | tf_op jit(solution)/shard_map/ppermute | solution.py:248
  18.0 10.6 %copy-start = (bf16[640,2048]{1,0:T(8,128)(2,1)S(1)}, bf16[640,2048]{1,0:T(8,128)(2,1)}, u32[]{:S(2)}) copy-start(bf16[640,2048]{1,0:T(8,128)(2,1)} %moments_ref.3) | copy-start | bytes 7864324
  18.5 1.1 %copy-start.1 = (s32[5,32,2048]{2,1,0:T(8,128)}, s32[5,32,2048]{2,1,0:T(8,128)S(1)}, u32[]{:S(2)}) copy-start(s32[5,32,2048]{2,1,0:T(8,128)S(1)} %get-tuple-element.11.words_ref) | copy-start | bytes 3932164
  19.5 4.8 %collective-permute-start.2 = (bf16[96,128]{1,0:T(8,128)(2,1)S(1)}, bf16[96,128]{1,0:T(8,128)(2,1)S(1)}, u32[]{:S(2)}, u32[]{:S(2)}) collective-permute-start(bf16[96,128]{1,0:T(8,128)(2,1)S(1)} %get-tuple-element.12), channel_id=1, source_target_pairs={{0,1},{1,2},{2,3},{3,0},{4,5},{5,6},{6,7},{7,4},{8,9},{9,10},{10,1... | collective-permute-start | bytes 73736 | tf_op jit(solution)/shard_map/ppermute | solution.py:257
  21.5 4.1 %collective-permute-start.3 = (bf16[96,128]{1,0:T(8,128)(2,1)S(1)}, bf16[96,128]{1,0:T(8,128)(2,1)S(1)}, u32[]{:S(2)}, u32[]{:S(2)}) collective-permute-start(bf16[96,128]{1,0:T(8,128)(2,1)S(1)} %get-tuple-element.13), channel_id=1, source_target_pairs={{0,3},{1,0},{2,1},{3,2},{4,7},{5,4},{6,5},{7,6},{8,11},{9,8},{10,9... | collective-permute-start | bytes 73736 | tf_op jit(solution)/shard_map/ppermute | solution.py:258
  25.6 1.3 %copy-start.2 = (s32[5,32,2048]{2,1,0:T(8,128)S(1)}, s32[5,32,2048]{2,1,0:T(8,128)}, u32[]{:S(2)}) copy-start(s32[5,32,2048]{2,1,0:T(8,128)} %copy-done.1) | copy-start | bytes 3932164
  29.8 31.3 %collective-permute-start.4 = (bf16[8,320,256]{2,1,0:T(8,128)(2,1)S(1)}, bf16[8,320,256]{2,1,0:T(8,128)(2,1)S(1)}, u32[]{:S(2)}, u32[]{:S(2)}) collective-permute-start(bf16[8,320,256]{2,1,0:T(8,128)(2,1)S(1)} %weigh.3.first_ref), channel_id=1, source_target_pairs={{0,1},{1,0},{2,3},{3,2},{4,5},{5,4},{6,7},{7,6},{8,9},{9,8},{10,11... | collective-permute-start | bytes 3932168 | tf_op jit(solution)/shard_map/ppermute | solution.py:289
  32.2 30.4 %collective-permute-start.5 = (bf16[8,320,256]{2,1,0:T(8,128)(2,1)S(1)}, bf16[8,320,256]{2,1,0:T(8,128)(2,1)S(1)}, u32[]{:S(2)}, u32[]{:S(2)}) collective-permute-start(bf16[8,320,256]{2,1,0:T(8,128)(2,1)S(1)} %weigh.2.second_ref.own_ref), channel_id=1, source_target_pairs={{0,2},{1,3},{2,0},{3,1},{4,6},{5,7},{6,4},{7,5},{8,10},{9,11},{10,... | collective-permute-start | bytes 3932168 | tf_op jit(solution)/shard_map/ppermute | solution.py:290
  68.6 9.9 %all-to-all-start = ((f32[32,1,64]{2,1,0:T(1,128)}), f32[32,1,64]{2,1,0:T(1,128)S(1)}, u32[]{:S(2)}, u32[]{:S(2)}) async-start(f32[32,1,64]{2,1,0:T(1,128)} %bitcast.2), calls=%async_computation | async-start | bytes 32768 | tf_op jit(solution)/shard_map/all_to_all | solution.py:333

commit v2 on v0

v2 whole, which is shorter than its diff:
```python
import functools
import math

import jax
import jax.numpy as jnp
from jax import lax
from jax.experimental import pallas as pl
from jax.experimental.pallas import tpu as pltpu
from jax.sharding import PartitionSpec as P

R = 2048
SWEEPS = 2
DEPTH = 32
LANES = 128
TILE = 256
PER_STEP = 2
MIDDLE = 4
WORDS = 1 + 2 * SWEEPS


def params(**more):
    return pltpu.CompilerParams(vmem_limit_bytes=48 << 20, **more)


def fetch(step, spins_hbm, draws_hbm, spins_buf, draws_buf, sems, row, at, count):
    copies = [
        pltpu.make_async_copy(
            spins_hbm.at[pl.ds(row, count)], spins_buf.at[pl.ds(at, count)], sems.at[step, 0]
        )
    ]
    for k in range(SWEEPS):
        copies.append(
            pltpu.make_async_copy(
                draws_hbm.at[k, pl.ds(row, count)],
                draws_buf.at[k, pl.ds(at, count)],
                sems.at[step, 1 + k],
            )
        )
    return copies


def pack(bar_ref, words_ref, spins_buf, draws_buf, planes, at, fresh):
    columns = words_ref.shape[2]
    for left in range(0, columns, TILE):
        lanes = pl.ds(left, TILE)
        if fresh:
            words = [jnp.zeros((DEPTH, TILE), jnp.int32)] * WORDS
        else:
            words = [words_ref[w, :, lanes] for w in range(WORDS)]
        for i, plane in enumerate(planes):
            bit = 1 << (plane + 1)
            rows = pl.ds(at + i * DEPTH, DEPTH)
            words[0] = words[0] | (spins_buf[rows, lanes] << (plane + 1))
            for k in range(SWEEPS):
                draw = draws_buf[k, rows, lanes]
                for c in range(2):
                    word = words[1 + 2 * k + c]
                    words[1 + 2 * k + c] = jnp.where(draw < bar_ref[c], word | bit, word)
        for w, word in enumerate(words):
            words_ref[w, :, lanes] = word


def groups_of(planes, size):
    return [planes[i : i + size] for i in range(0, len(planes), size)]


def strips(parts):
    return jnp.concatenate(parts, axis=0).astype(jnp.float32).astype(jnp.bfloat16)


def codes(bits):
    return [bits[0]] + [bits[1 + 2 * k] + 2 * bits[2 + 2 * k] for k in range(SWEEPS)]


def unstrips(ref, height):
    parts = [
        ref[k * height : (k + 1) * height, :].astype(jnp.float32).astype(jnp.int32)
        for k in range(1 + SWEEPS)
    ]
    bits = [parts[0]]
    for code in parts[1:]:
        bits += [code & 1, code >> 1]
    return bits


def spread(word):
    for shift in (4, 8, 16, 32, 64):
        word = word | pltpu.roll(word, shift, 1)
    return word


def sweeps_of(words):
    spins = words[0]
    width = spins.shape[1]
    row = lax.broadcasted_iota(jnp.int32, spins.shape, 0)
    parity = (row + lax.broadcasted_iota(jnp.int32, spins.shape, 1)) & 1
    for k in range(SWEEPS):
        for colour in range(2):
            up = pltpu.roll(spins, 1, 0)
            up = jnp.where(row == 0, up << 1, up)
            down = pltpu.roll(spins, DEPTH - 1, 0)
            down = jnp.where(row == DEPTH - 1, down >> 1, down)
            a, b = up ^ spins, down ^ spins
            c, d = pltpu.roll(spins, 1, 1) ^ spins, pltpu.roll(spins, width - 1, 1) ^ spins
            either, other = a | b, c | d
            some = either | other
            several = (a & b) | (c & d) | (either & other)
            flips = several | (some & words[1 + 2 * k]) | (words[2 + 2 * k] & ~some)
            spins = jnp.where(parity == colour, spins ^ flips, spins)
    return spins


def weigh(spins, moments, plane):
    up = (spins & (jnp.int32(1) << (plane + 1))) != 0
    size = moments.astype(jnp.float32)
    return jnp.where(up, size, -size).astype(jnp.bfloat16)


def middle_kernel(
    odd_ref,
    bar_ref,
    spins_hbm,
    draws_hbm,
    moments_hbm,
    words_ref,
    last_ref,
    first_ref,
    given_ref,
    kept_ref,
    spins_buf,
    draws_buf,
    edge_spins,
    edge_draws,
    moments_buf,
    final_ref,
    sems,
    edge_sems,
):
    rows, columns = spins_hbm.shape
    half = rows // DEPTH // 2
    planes = list(range(half - MIDDLE - 1, half + MIDDLE + 1))
    top = planes[0] * DEPTH
    groups = groups_of(planes, PER_STEP)
    size = PER_STEP * DEPTH
    edges = [
        fetch(s, spins_hbm, draws_hbm, edge_spins, edge_draws, edge_sems, row, 8 * s, 8)
        for s, row in enumerate((rows - 8, 0))
    ]
    copies = [
        fetch(
            g,
            spins_hbm,
            draws_hbm,
            spins_buf,
            draws_buf,
            sems,
            top + g * size,
            g * size,
            len(group) * DEPTH,
        )
        for g, group in enumerate(groups)
    ]
    weights = pltpu.make_async_copy(
        moments_hbm.at[pl.ds((half - MIDDLE) * DEPTH, 2 * MIDDLE * DEPTH)],
        moments_buf,
        edge_sems.at[2, 0],
    )
    for copy in sum(edges + copies, []) + [weights]:
        copy.start()
    for s, ref in enumerate((last_ref, first_ref)):
        for copy in edges[s]:
            copy.wait()
        parts = [edge_spins[8 * s : 8 * s + 8, :]]
        for k in range(SWEEPS):
            draw = edge_draws[k, 8 * s : 8 * s + 8, :]
            one = (draw < bar_ref[0]).astype(jnp.int32)
            parts.append(one + 2 * (draw < bar_ref[1]).astype(jnp.int32))
        ref[...] = strips(parts + [jnp.zeros_like(parts[0])])
    for g, group in enumerate(groups):
        for copy in copies[g]:
            copy.wait()
        pack(bar_ref, words_ref, spins_buf, draws_buf, group, g * size, g == 0)
    inner = slice(LANES, columns - LANES)
    final_ref[:, inner] = sweeps_of([words_ref[w, :, inner] for w in range(WORDS)])
    weights.wait()
    for ref, lower in ((given_ref, 1 - odd_ref[0]), (kept_ref, odd_ref[0])):
        for i in range(MIDDLE):
            plane = half - MIDDLE + MIDDLE * lower + i
            at = pl.ds(pl.multiple_of((MIDDLE * lower + i) * DEPTH, DEPTH), DEPTH)
            for t in range(ref.shape[0]):
                lanes = pl.ds((t + 1) * TILE, TILE)
                ref[t, i * DEPTH : (i + 1) * DEPTH, :] = weigh(
                    final_ref[:, lanes], moments_buf[at, lanes], plane
                )


def outer_kernel(bar_ref, spins_hbm, draws_hbm, middle_ref, words_ref, spins_buf, draws_buf, sems):
    planes = spins_hbm.shape[0] // DEPTH
    side = planes // 2 - MIDDLE - 1
    outer = list(range(side)) + list(range(planes - side, planes))
    copies = []
    for g, plane in enumerate(outer):
        copies.append(
            fetch(
                g,
                spins_hbm,
                draws_hbm,
                spins_buf,
                draws_buf,
                sems,
                plane * DEPTH,
                g * DEPTH,
                DEPTH,
            )
        )
        for copy in copies[-1]:
            copy.start()
    words_ref[...] = middle_ref[...]
    for g in range(0, len(outer), PER_STEP):
        group = outer[g : g + PER_STEP]
        for copy in sum(copies[g : g + PER_STEP], []):
            copy.wait()
        pack(bar_ref, words_ref, spins_buf, draws_buf, group, g * DEPTH, False)


def inner_kernel(
    odd_ref,
    words_ref,
    above_ref,
    below_ref,
    moments_hbm,
    spins_ref,
    sides_ref,
    right_ref,
    left_ref,
    given_ref,
    kept_ref,
    joined_ref,
    moments_buf,
    sems,
):
    rows, columns = moments_hbm.shape
    planes = rows // DEPTH
    side = planes // 2 - MIDDLE
    weights = [
        pltpu.make_async_copy(
            moments_hbm.at[pl.ds(row, side * DEPTH)], moments_buf.at[s], sems.at[s]
        )
        for s, row in enumerate((0, rows - side * DEPTH))
    ]
    for copy in weights:
        copy.start()
    above, below = unstrips(above_ref, 8), unstrips(below_ref, 8)
    joined_ref[...] = words_ref[...]
    for w in range(WORDS):
        joined_ref[w, DEPTH - 8 :, :] = words_ref[w, DEPTH - 8 :, :] | above[w]
        joined_ref[w, :8, :] = words_ref[w, :8, :] | (below[w] << (planes + 1))
    lane = lax.broadcasted_iota(jnp.int32, (DEPTH, LANES), 1)
    for ref, at, held in (
        (right_ref, columns - LANES, lane >= LANES - 4),
        (left_ref, 0, lane < 4),
    ):
        bits = []
        for w in range(WORDS):
            edge = jnp.where(held, joined_ref[w, :, at : at + LANES], 0)
            bits.append((spread(edge) >> (lane // 4)) & 1)
        ref[...] = strips(codes(bits))
    reach = TILE + LANES
    sides_ref[:, :, :reach] = joined_ref[:, :, :reach]
    sides_ref[:, :, reach:] = joined_ref[:, :, columns - reach :]
    inner = slice(LANES, columns - LANES)
    spins_ref[:, :LANES] = jnp.zeros((DEPTH, LANES), jnp.int32)
    spins_ref[:, columns - LANES :] = jnp.zeros((DEPTH, LANES), jnp.int32)
    spins_ref[:, inner] = sweeps_of([joined_ref[w, :, inner] for w in range(WORDS)])
    for copy in weights:
        copy.wait()
    for ref, lower in ((given_ref, 1 - odd_ref[0]), (kept_ref, odd_ref[0])):
        for i in range(side):
            plane = (planes - side) * lower + i
            for t in range(ref.shape[0]):
                lanes = pl.ds((t + 1) * TILE, TILE)
                ref[t, i * DEPTH : (i + 1) * DEPTH, :] = weigh(
                    spins_ref[:, lanes],
                    moments_buf[lower, i * DEPTH : (i + 1) * DEPTH, lanes],
                    plane,
                )


def side_kernel(
    odd_ref,
    sides_ref,
    before_ref,
    after_ref,
    moments_hbm,
    spins_ref,
    given_ref,
    kept_ref,
    moments_buf,
    final_ref,
    sems,
):
    rows, columns = moments_hbm.shape
    half = rows // DEPTH // 2
    weights = [
        pltpu.make_async_copy(
            moments_hbm.at[:, pl.ds(at, TILE)], moments_buf.at[s], sems.at[s]
        )
        for s, at in enumerate((0, columns - TILE))
    ]
    for copy in weights:
        copy.start()
    lane = lax.broadcasted_iota(jnp.int32, (DEPTH, LANES), 1)
    before, after = unstrips(before_ref, DEPTH), unstrips(after_ref, DEPTH)
    words = [
        jnp.concatenate(
            [spread(before[w] << (lane // 4)), sides_ref[w], spread(after[w] << (lane // 4))],
            axis=1,
        )
        for w in range(WORDS)
    ]
    updated = sweeps_of(words)
    width = updated.shape[1]
    final_ref[0] = updated[:, LANES : LANES + TILE]
    final_ref[1] = updated[:, width - LANES - TILE : width - LANES]
    spins_ref[...] = final_ref[...]
    for copy in weights:
        copy.wait()
    for ref, lower in ((given_ref, 1 - odd_ref[0]), (kept_ref, odd_ref[0])):
        for i in range(half):
            plane = i + lower * (half + MIDDLE if i < half - MIDDLE else MIDDLE)
            at = pl.ds(pl.multiple_of(plane * DEPTH, DEPTH), DEPTH)
            for s in range(2):
                ref[s, i * DEPTH : (i + 1) * DEPTH, :] = weigh(
                    final_ref[s], moments_buf[s, at, :], plane
                )


def spell_kernel(spins_ref, sides_ref, out_ref):
    columns = out_ref.shape[1]
    first = pl.program_id(0) * PER_STEP + 1
    for plane in range(PER_STEP):
        bit = jnp.int32(1) << (first + plane)
        rows = pl.ds(plane * DEPTH, DEPTH)
        for left in range(0, columns, TILE):
            if left == 0:
                word = sides_ref[0]
            elif left == columns - TILE:
                word = sides_ref[1]
            else:
                word = spins_ref[:, left : left + TILE]
            out_ref[rows, left : left + TILE] = jnp.where((word & bit) != 0, 1.0, -1.0)


def gram(left, right):
    return lax.dot_general(
        left, right, (((0,), (0,)), ((), ())), preferred_element_type=jnp.float32
    )


def stack(refs, first, last):
    return jnp.concatenate(
        [ref[first:last].reshape((last - first) * ref.shape[1], TILE) for ref in refs], axis=0
    )


def fold(sums_ref):
    width = R + LANES
    value = sums_ref[:LANES, :width] + sums_ref[LANES:, LANES : LANES + width]
    height = LANES // 2
    while height >= 8:
        value = value[:height] + pltpu.roll(value[height:], width - height, 1)
        height //= 2
    return value


def own_kernel(*refs):
    parts, (out_ref, sums_ref, full_ref, sems) = refs[:-4], refs[-4:]
    copies = []
    for h in range(2):
        low, high, ends = parts[3 * h : 3 * h + 3]
        split = low.shape[1]
        full = full_ref.at[h]
        tiles = full_ref.shape[1]
        for source, target in (
            (low, full.at[pl.ds(1, tiles - 2), pl.ds(0, split)]),
            (high, full.at[pl.ds(1, tiles - 2), pl.ds(split, high.shape[1])]),
            (ends.at[0], full.at[0]),
            (ends.at[1], full.at[tiles - 1]),
        ):
            copies.append(pltpu.make_async_copy(source, target, sems.at[len(copies)]))
            copies[-1].start()
    for copy in copies:
        copy.wait()
    for n in range(tiles):
        sums_ref[:, n * TILE : (n + 1) * TILE] = sum(
            gram(stack([full_ref.at[h]], 0, tiles - n), stack([full_ref.at[h]], n, tiles))
            for h in range(2)
        )
    sums_ref[:, tiles * TILE :] = jnp.zeros((TILE, TILE), jnp.float32)
    out_ref[...] = fold(sums_ref)


def by_side(odd_ref, own, mid, far, run):
    @pl.when(odd_ref[0] == 0)
    def _():
        run(((own, mid), (mid, far)))

    @pl.when(odd_ref[0] == 1)
    def _():
        run(((far, mid), (mid, own)))


def early_kernel(odd_ref, *refs):
    (base_ref, out_ref, sums_ref) = refs[-3:]
    tiles = refs[0].shape[0]
    sums_ref[:, : 3 * TILE] = jnp.zeros((TILE, 3 * TILE), jnp.float32)

    def run(pairs):
        for n in range(1, tiles + 1):
            sums_ref[:, (n + 2) * TILE : (n + 3) * TILE] = sum(
                gram(stack(left, tiles - n, tiles), stack(right, 0, n)) for left, right in pairs
            )

    by_side(odd_ref, refs[0:2], refs[2:4], refs[4:6], run)
    out_ref[...] = fold(sums_ref) + base_ref[...]


def late_kernel(odd_ref, *refs):
    (base_ref, out_ref, sums_ref) = refs[-3:]
    tiles = refs[0].shape[0] + 2
    sums_ref[:, :TILE] = jnp.zeros((TILE, TILE), jnp.float32)

    def tile(block, t):
        low, high, ends = block
        if t in (0, tiles - 1):
            return ends[min(t, 1)]
        return stack([low, high], t - 1, t)

    def run(pairs):
        for n in range(1, tiles + 1):
            places = [(tiles - 1, n - 1)] + ([(tiles - n, 0)] if n > 1 else [])
            sums_ref[:, n * TILE : (n + 1) * TILE] = sum(
                gram(
                    jnp.concatenate([tile(left, t) for t, _ in places], axis=0),
                    jnp.concatenate([tile(right, q) for _, q in places], axis=0),
                )
                for left, right in pairs
            )

    by_side(odd_ref, refs[0:3], refs[3:6], refs[6:9], run)
    value = fold(sums_ref) + base_ref[...]
    for height in (4, 2, 1):
        value = value + pltpu.roll(pltpu.roll(value, value.shape[1] - height, 1), 8 - height, 0)
    share = out_ref.shape[2]
    for d in range(out_ref.shape[0]):
        out_ref[d] = value[:1, d * share : (d + 1) * share]


def on_device(spins_up, uniforms, moments, accept_bar):
    rows, columns = spins_up.shape
    planes, tiles = rows // DEPTH, columns // TILE
    half_rows, half = rows // 2, planes // 2
    row_devices, col_devices = lax.axis_size("row"), lax.axis_size("col")
    devices = row_devices * col_devices
    assert columns == R and col_devices % 2 == 0 and planes % 2 == 0 and planes + 2 <= 26
    vmem = pl.BlockSpec(memory_space=pltpu.VMEM)
    smem = pl.BlockSpec(memory_space=pltpu.SMEM)
    anywhere = pl.BlockSpec(memory_space=pl.ANY)
    strip = jax.ShapeDtypeStruct((8 * (2 + SWEEPS), columns), jnp.bfloat16)
    edge = jax.ShapeDtypeStruct((DEPTH * (1 + SWEEPS), LANES), jnp.bfloat16)
    words_shape = jax.ShapeDtypeStruct((WORDS, DEPTH, columns), jnp.int32)
    dma = pltpu.SemaphoreType.DMA
    odd = (lax.axis_index("col") % 2).reshape(1)

    def message(count, height):
        return jax.ShapeDtypeStruct((count, height, TILE), jnp.bfloat16)

    def ring(size, step):
        return [(i, (i + step) % size) for i in range(size)]

    def exchange(given, kept):
        mid = lax.ppermute(given, "col", [(i, i ^ 1) for i in range(col_devices)])
        far = lax.ppermute(
            kept, "col", [(i, (i - 2 + 4 * (i % 2)) % col_devices) for i in range(col_devices)]
        )
        return mid, far

    def call(kernel, name, specs, shapes, scratch, flops, moved, *operands):
        return pl.pallas_call(
            kernel,
            in_specs=specs,
            out_specs=jax.tree.map(lambda _: vmem, shapes),
            out_shape=shapes,
            scratch_shapes=scratch,
            compiler_params=params(),
            cost_estimate=pl.CostEstimate(flops=flops, bytes_accessed=moved, transcendentals=0),
            name=name,
        )(*operands)

    packed = (2 * MIDDLE + 2) * DEPTH
    middle = message(tiles - 2, MIDDLE * DEPTH)
    words, last, leading, given, kept = call(
        middle_kernel,
        "middle",
        [smem, smem, anywhere, anywhere, anywhere],
        [words_shape, strip, strip, middle, middle],
        [
            pltpu.VMEM((packed, columns), jnp.int32),
            pltpu.VMEM((SWEEPS, packed, columns), jnp.float32),
            pltpu.VMEM((16, columns), jnp.int32),
            pltpu.VMEM((SWEEPS, 16, columns), jnp.float32),
            pltpu.VMEM((2 * MIDDLE * DEPTH, columns), jnp.bfloat16),
            pltpu.VMEM((DEPTH, columns), jnp.int32),
            dma((pl.cdiv(2 * MIDDLE + 2, PER_STEP), 1 + SWEEPS)),
            dma((3, 1 + SWEEPS)),
        ],
        40 * packed * columns,
        4 * (1 + SWEEPS) * packed * columns,
        odd,
        accept_bar,
        spins_up,
        uniforms,
        moments,
    )
    own = [given, kept]
    got = [*exchange(given, kept)]
    above = lax.ppermute(last, "row", ring(row_devices, 1))
    below = lax.ppermute(leading, "row", ring(row_devices, -1))

    remaining = rows - packed
    words = call(
        outer_kernel,
        "outer",
        [smem, anywhere, anywhere, vmem],
        words_shape,
        [
            pltpu.VMEM((remaining, columns), jnp.int32),
            pltpu.VMEM((SWEEPS, remaining, columns), jnp.float32),
            dma((remaining // DEPTH, 1 + SWEEPS)),
        ],
        40 * remaining * columns,
        4 * (1 + SWEEPS) * remaining * columns,
        accept_bar,
        spins_up,
        uniforms,
        words,
    )
    side = half - MIDDLE
    low = message(tiles - 2, side * DEPTH)
    reach = 2 * (TILE + LANES)
    spins, sides, right, left, given, kept = call(
        inner_kernel,
        "inner",
        [smem, vmem, vmem, vmem, anywhere],
        [
            jax.ShapeDtypeStruct((DEPTH, columns), jnp.int32),
            jax.ShapeDtypeStruct((WORDS, DEPTH, reach), jnp.int32),
            edge,
            edge,
            low,
            low,
        ],
        [
            pltpu.VMEM(words_shape.shape, jnp.int32),
            pltpu.VMEM((2, side * DEPTH, columns), jnp.bfloat16),
            dma((2,)),
        ],
        40 * rows * columns,
        4 * rows * columns,
        odd,
        words,
        above,
        below,
        moments,
    )
    own = [given, own[0], kept, own[1]]
    mid, far = exchange(given, kept)
    got = [mid, got[0], far, got[1]]
    before = lax.ppermute(right, "col", ring(col_devices, 1))
    after = lax.ppermute(left, "col", ring(col_devices, -1))
    ends = message(2, half_rows)
    side_spins, given, kept = call(
        side_kernel,
        "side",
        [smem, vmem, vmem, vmem, anywhere],
        [jax.ShapeDtypeStruct((2, DEPTH, TILE), jnp.int32), ends, ends],
        [
            pltpu.VMEM((2, rows, TILE), jnp.bfloat16),
            pltpu.VMEM((2, DEPTH, TILE), jnp.int32),
            dma((2,)),
        ],
        10 * rows * columns,
        rows * columns,
        odd,
        sides,
        before,
        after,
        moments,
    )
    own = [own[0], own[1], given, own[2], own[3], kept]
    mid, far = exchange(given, kept)

    spins_out = pl.pallas_call(
        spell_kernel,
        grid=(rows // (PER_STEP * DEPTH),),
        in_specs=[
            pl.BlockSpec((DEPTH, columns), lambda i: (0, 0)),
            pl.BlockSpec((2, DEPTH, TILE), lambda i: (0, 0, 0)),
        ],
        out_specs=pl.BlockSpec((PER_STEP * DEPTH, columns), lambda i: (i, 0)),
        out_shape=jax.ShapeDtypeStruct((rows, columns), jnp.float32),
        compiler_params=params(),
        cost_estimate=pl.CostEstimate(
            flops=rows * columns, bytes_accessed=4 * rows * columns, transcendentals=0
        ),
        name="spell",
    )(spins, side_spins)
    sums = pltpu.VMEM((TILE, R + TILE), jnp.float32)
    folded = jax.ShapeDtypeStruct((8, R + LANES), jnp.float32)
    work = rows * columns * columns
    base = call(
        own_kernel,
        "own",
        [vmem] * 6,
        folded,
        [sums, pltpu.VMEM((2, tiles, half_rows, TILE), jnp.bfloat16), dma((8,))],
        work,
        2 * rows * columns,
        *own,
    )
    base = call(
        early_kernel,
        "early",
        [smem] + [vmem] * 7,
        folded,
        [sums],
        work // 2,
        2 * rows * columns,
        odd,
        own[3],
        own[4],
        *got,
        base,
    )
    partial_sums = call(
        late_kernel,
        "late",
        [smem] + [vmem] * 10,
        jax.ShapeDtypeStruct((devices, 1, R // devices), jnp.float32),
        [sums],
        work // 2,
        2 * rows * columns,
        odd,
        own[3],
        own[4],
        own[5],
        got[0],
        got[1],
        mid,
        got[2],
        got[3],
        far,
        base,
    )
    normaliser = 1.0 / math.sqrt(rows * row_devices * columns * col_devices)
    shares = lax.all_to_all(partial_sums, ("row", "col"), 0, 0, tiled=True)
    return spins_out, jnp.sum(shares, axis=(0, 1)) * normaliser


def solution(mesh):
    placed = (P("row", "col"), P(None, "row", "col"), P("row", "col"), P())
    return jax.shard_map(
        on_device,
        mesh=mesh,
        in_specs=placed,
        out_specs=(P("row", "col"), P(("row", "col"))),
        check_vma=False,
    )
```

time: 351 us -> 67.9 us (0.19)
  other arithmetic: 76.6 us -> 0.57 us
  local copies, waits for them, and re-layouts: 63.9 us -> 2.39 us
  matrix products: 54.5 us -> 0 us
  waiting for transfers between devices: 61.9 us -> 16.4 us
  blocking collectives: 39.7 us -> 0 us
  loops' own time: 31.6 us -> 0 us
  Pallas kernels: 0 us -> 29.6 us
    dot_general x17 -> x0, matrix products: 54.5 us -> none  [product(): jnp.einsum('itp,itq->pq', left_tiles, shifted, preferred_element_type=jnp...]
    ppermute x13 -> x10, waiting for transfers between devices: 61.9 us -> 13.6 us  [the longest x1 11.2 us: on_device(): before = lax.ppermute(right, 'col', ring(col_devices, 1))]
    unnamed x1 -> x0, blocking collectives: 39.7 us -> none
    another operation x1 -> x0, loops' own time: 31.6 us -> none  [correlate(): products = lax.map(product, jnp.arange(offsets + 1, dtype=jnp.int32))]
    select_n x2 -> x0, other arithmetic: 30 us -> none  [update_colour(): return jnp.where(flipped, -centre, centre)]
    pallas_call x0 -> x8, Pallas kernels: none -> 29.6 us  [the longest x7 25.2 us: call(): pl.pallas_call(kernel, in_specs=specs, out_specs=jax.tree.map(lambda _: v...]
    concatenate x3 -> x0, local copies, waits for them, and re-layouts: 26 us -> none  [with_halo(): value = jnp.concatenate([before, value, after], axis=dim)]
    convert_element_type x4 -> x0, other arithmetic: 20.2 us -> none  [the longest x2 13.3 us: on_device(): lattice.astype(jnp.bfloat16)]
  transfers between devices with their start and end apart: 13 -> 11, of which waited for: 7 -> 3; matrix products, arithmetic and copies ran while one was open for 6% -> 0% of each run, Pallas kernels for 0% -> 30%
where the time goes in v2:
time: 67.9 us; the launch traced here: 67.8 us
  Pallas kernels  29.6 us (44%)
  starting transfers between devices  18 us (27%)
  waiting for transfers between devices  16.4 us (24%)
  local copies, waits for them, and re-layouts  2.39 us (4%)
  between operations  0.76 us (1%)
    pallas_call x7, Pallas kernels, call(): pl.pallas_call(kernel, in_specs=specs, out_specs=jax.tree.map(lambda _: v...  25.2 us
    ppermute x1, waiting for transfers between devices, on_device(): before = lax.ppermute(right, 'col', ring(col_devices, 1))  11.2 us
    pallas_call x1, Pallas kernels, on_device(): pl.pallas_call(spell_kernel, grid=(rows // (PER_STEP * DEPTH),), in_specs...  4.44 us
    ppermute x1, starting transfers between devices, on_device(): below = lax.ppermute(leading, 'row', ring(row_devices, -1))  4.09 us
    ppermute x3, starting transfers between devices, exchange(): mid = lax.ppermute(given, 'col', [(i, i ^ 1) for i in range(col_devices)])  3.59 us
    ppermute x3, starting transfers between devices, exchange(): lax.ppermute(kept, 'col', [(i, (i - 2 + 4 * (i % 2)) % col_devices) for i...  3.55 us
    all_to_all x1, starting transfers between devices, on_device(): shares = lax.all_to_all(partial_sums, ('row', 'col'), 0, 0, tiled=True)  2.95 us
    all_to_all x1, waiting for transfers between devices, on_device(): shares = lax.all_to_all(partial_sums, ('row', 'col'), 0, 0, tiled=True)  2.76 us
  transfers between devices with their start and end apart: 11, of which 3 were waited for; matrix products, arithmetic and copies ran while one was open for 0% of the time, Pallas kernels for 30%

profile of v2, /device:TPU:0, one launch (start us, length us, event | category | flops | bytes accessed | tf_op | source)
XLA Modules:
  0.0 67.8 jit_solution(14380441267185184989)
XLA Ops:
  0.7 1.7 %copy-done = bf16[640,2048]{1,0:T(8,128)(2,1)S(1)} copy-done((bf16[640,2048]{1,0:T(8,128)(2,1)S(1)}, bf16[640,2048]{1,0:T(8,128)(2,1)}, u32[]{:S(2)}) %copy-start) | copy-done | bytes 2621464
  2.4 0.7 copy-done.2
  3.0 6.4 %middle.1 = (s32[5,32,2048]{2,1,0:T(8,128)S(1)}, bf16[32,2048]{1,0:T(8,128)(2,1)S(1)}, bf16[32,2048]{1,0:T(8,128)(2,1)S(1)}, bf16[6,128,256]{2,1,0:T(8,128)(2,1)S(1)}, bf16[6,128,256]{2,1,0:T(8,128)(2,1)S(1)}) custom-call(s32[1]{0:T(128)} %bitcast.odd_ref, f32[2]{0:T(128)S(1)} %copy-done.2, s32[640,2048]{1,0:T(8,128)} %spins_hbm.3, ...), custom_call_target="tpu_custom_call" | custom-call | flops 26214400 | bytes 7864320 | tf_op jit(solution)/shard_map/middle/pallas_call | solution.py:489
  9.4 0.5 collective-permute-start
  10.0 4.1 %collective-permute-start.1 = (bf16[32,2048]{1,0:T(8,128)(2,1)S(1)}, bf16[32,2048]{1,0:T(8,128)(2,1)S(1)}, u32[]{:S(2)}, u32[]{:S(2)}) collective-permute-start(bf16[32,2048]{1,0:T(8,128)(2,1)S(1)} %get-tuple-element.18), channel_id=1, source_target_pairs={{0,28},{4,0},{8,4},{12,8},{16,12},{20,16},{24,20},{28,24},{1,29},{... | collective-permute-start | bytes 393224 | tf_op jit(solution)/shard_map/ppermute | solution.py:528
  14.1 1.9 %collective-permute-start.5 = (bf16[6,128,256]{2,1,0:T(8,128)(2,1)S(1)}, bf16[6,128,256]{2,1,0:T(8,128)(2,1)S(1)}, u32[]{:S(2)}, u32[]{:S(2)}) collective-permute-start(bf16[6,128,256]{2,1,0:T(8,128)(2,1)S(1)} %get-tuple-element.28.refs_1_), channel_id=1, source_target_pairs={{0,1},{1,0},{2,3},{3,2},{4,5},{5,4},{6,7},{7,6},{8,9},{9,8},{10,11... | collective-permute-start | bytes 1179656 | tf_op jit(solution)/shard_map/ppermute | solution.py:482
  16.0 4.5 %outer.1.words_ref = s32[5,32,2048]{2,1,0:T(8,128)S(1)} custom-call(f32[2]{0:T(128)S(1)} %copy-done.2, s32[640,2048]{1,0:T(8,128)} %spins_hbm.3, f32[2,640,2048]{2,1,0:T(8,128)} %draws_hbm.3, s32[5,32,2048]{2,1,0:T(8,128)S(1)} %get-tuple-element.16.middle_ref), custom_call_target="tpu_custom_call" | custom-call | flops 26214400 | bytes 7864320 | tf_op jit(solution)/shard_map/outer/pallas_call | solution.py:489
  20.6 2.0 %inner.1 = (s32[32,2048]{1,0:T(8,128)S(1)}, s32[5,32,768]{2,1,0:T(8,128)S(1)}, bf16[96,128]{1,0:T(8,128)(2,1)S(1)}, bf16[96,128]{1,0:T(8,128)(2,1)S(1)}, bf16[6,...) custom-call(s32[1]{0:T(128)} %bitcast.odd_ref, s32[5,32,2048]{2,1,0:T(8,128)S(1)} %outer.1.words_ref, ...), custom_call_target="tpu_custom_call" | custom-call | flops 52428800 | bytes 5242880 | tf_op jit(solution)/shard_map/inner/pallas_call | solution.py:489
  22.6 0.2 collective-permute-start.4
  22.8 2.0 %collective-permute-start.7 = (bf16[6,192,256]{2,1,0:T(8,128)(2,1)S(1)}, bf16[6,192,256]{2,1,0:T(8,128)(2,1)S(1)}, u32[]{:S(2)}, u32[]{:S(2)}) collective-permute-start(bf16[6,192,256]{2,1,0:T(8,128)(2,1)S(1)} %get-tuple-element.24.refs_3_.refs_0_), channel_id=1, source_target_pairs={{0,2},{1,3},{2,0},{3,1},{4,6},{5,7},{6,4},{7,5},{8,10},{9,11},{10,... | collective-permute-start | bytes 1769480 | tf_op jit(solution)/shard_map/ppermute | solution.py:483
  24.8 1.9 %collective-permute-start.2 = (bf16[96,128]{1,0:T(8,128)(2,1)S(1)}, bf16[96,128]{1,0:T(8,128)(2,1)S(1)}, u32[]{:S(2)}, u32[]{:S(2)}) collective-permute-start(bf16[96,128]{1,0:T(8,128)(2,1)S(1)} %get-tuple-element.21), channel_id=1, source_target_pairs={{0,1},{1,2},{2,3},{3,0},{4,5},{5,6},{6,7},{7,4},{8,9},{9,10},{10,1... | collective-permute-start | bytes 73736 | tf_op jit(solution)/shard_map/ppermute | solution.py:579
  26.7 11.2 %collective-permute-done.2.before_ref = bf16[96,128]{1,0:T(8,128)(2,1)S(1)} collective-permute-done((bf16[96,128]{1,0:T(8,128)(2,1)S(1)}, bf16[96,128]{1,0:T(8,128)(2,1)S(1)}, u32[]{:S(2)}, u32[]{:S(2)}) %collective-permute-start.2) | collective-permute-done | bytes 24608 | tf_op jit(solution)/shard_map/ppermute | solution.py:579
  37.9 1.4 %collective-permute-start.3 = (bf16[96,128]{1,0:T(8,128)(2,1)S(1)}, bf16[96,128]{1,0:T(8,128)(2,1)S(1)}, u32[]{:S(2)}, u32[]{:S(2)}) collective-permute-start(bf16[96,128]{1,0:T(8,128)(2,1)S(1)} %get-tuple-element.22), channel_id=1, source_target_pairs={{0,3},{1,0},{2,1},{3,2},{4,7},{5,4},{6,5},{7,6},{8,11},{9,8},{10,9... | collective-permute-start | bytes 73736 | tf_op jit(solution)/shard_map/ppermute | solution.py:580
  39.3 2.4 %collective-permute-done.3.after_ref = bf16[96,128]{1,0:T(8,128)(2,1)S(1)} collective-permute-done((bf16[96,128]{1,0:T(8,128)(2,1)S(1)}, bf16[96,128]{1,0:T(8,128)(2,1)S(1)}, u32[]{:S(2)}, u32[]{:S(2)}) %collective-permute-start.3) | collective-permute-done | bytes 24608 | tf_op jit(solution)/shard_map/ppermute | solution.py:580
  41.7 1.4 %side.1 = (s32[2,32,256]{2,1,0:T(8,128)S(1)}, bf16[2,320,256]{2,1,0:T(8,128)(2,1)S(1)}, bf16[2,320,256]{2,1,0:T(8,128)(2,1)S(1)}) custom-call(s32[1]{0:T(128)} %bitcast.odd_ref, s32[5,32,768]{2,1,0:T(8,128)S(1)} %get-tuple-element.20.sides_ref, bf16[96,128]{1,0:T(8,128)(2,1)S(1)} %collective-permute-done.2.before_ref, ...), custom_call_target="tpu_custom_call" | custom-call | flops 13107200 | bytes 1310720 | tf_op jit(solution)/shard_map/side/pallas_call | solution.py:489
  43.2 1.5 %collective-permute-start.6 = (bf16[2,320,256]{2,1,0:T(8,128)(2,1)S(1)}, bf16[2,320,256]{2,1,0:T(8,128)(2,1)S(1)}, u32[]{:S(2)}, u32[]{:S(2)}) collective-permute-start(bf16[2,320,256]{2,1,0:T(8,128)(2,1)S(1)} %get-tuple-element.29.refs_2_), channel_id=1, source_target_pairs={{0,1},{1,0},{2,3},{3,2},{4,5},{5,4},{6,7},{7,6},{8,9},{9,8},{10,11... | collective-permute-start | bytes 983048 | tf_op jit(solution)/shard_map/ppermute | solution.py:482
  44.7 1.5 %collective-permute-start.9 = (bf16[2,320,256]{2,1,0:T(8,128)(2,1)S(1)}, bf16[2,320,256]{2,1,0:T(8,128)(2,1)S(1)}, u32[]{:S(2)}, u32[]{:S(2)}) collective-permute-start(bf16[2,320,256]{2,1,0:T(8,128)(2,1)S(1)} %get-tuple-element.26.refs_5_.refs_2_), channel_id=1, source_target_pairs={{0,2},{1,3},{2,0},{3,1},{4,6},{5,7},{6,4},{7,5},{8,10},{9,11},{10,... | collective-permute-start | bytes 983048 | tf_op jit(solution)/shard_map/ppermute | solution.py:483
  46.2 4.9 %own.1.refs_6_ = f32[8,2176]{1,0:T(8,128)S(1)} custom-call(bf16[6,192,256]{2,1,0:T(8,128)(2,1)S(1)} %get-tuple-element.27.refs_0_, bf16[6,128,256]{2,1,0:T(8,128)(2,1)S(1)} %get-tuple-element.28.refs_1_, bf16[2,320,256]{2,1,0:T(8,128)(2,1)S(1)} %get-tuple-element.29.refs_2_, bf16[6,192,256]{2,1,0:T(8,128)(2,1)S(1)} %get-tuple-element.24.refs_3_.refs_0_, ...), custom_call_target="tpu_custom_call" | custom-call | flops 2684354560 | bytes 2621440 | tf_op jit(solution)/shard_map/own/pallas_call | solution.py:489
  51.1 2.9 %early.1.refs_9_ = f32[8,2176]{1,0:T(8,128)S(1)} custom-call(s32[1]{0:T(128)} %bitcast.odd_ref, bf16[6,192,256]{2,1,0:T(8,128)(2,1)S(1)} %get-tuple-element.24.refs_3_.refs_0_, bf16[6,128,256]{2,1,0:T(8,128)(2,1)S(1)} %get-tuple-element.25.refs_4_.refs_1_, bf16[6,192,256]{2,1,0:T(8,128)(2,1)S(1)} %collective-permute-done.4.refs_2_.refs_3_, ...), custom_call_target="tpu_custom_call" | custom-call | flops 1342177280 | bytes 2621440 | tf_op jit(solution)/shard_map/early/pallas_call | solution.py:489
  54.0 3.0 %late.1 = f32[32,1,64]{2,1,0:T(1,128)} custom-call(s32[1]{0:T(128)} %bitcast.odd_ref, bf16[6,192,256]{2,1,0:T(8,128)(2,1)S(1)} %get-tuple-element.24.refs_3_.refs_0_, bf16[6,128,256]{2,1,0:T(8,128)(2,1)S(1)} %get-tuple-element.25.refs_4_.refs_1_, bf16[2,320,256]{2,1,0:T(8,128)(2,1)S(1)} %get-tuple-element.26.refs_5_.refs_2_, ...), custom_call_target="tpu_custom_call" | custom-call | flops 1342177280 | bytes 2621440 | tf_op jit(solution)/shard_map/late/pallas_call | solution.py:489
  57.0 2.9 %all-to-all-start = ((f32[32,1,64]{2,1,0:T(1,128)}), f32[32,1,64]{2,1,0:T(1,128)S(1)}, u32[]{:S(2)}, u32[]{:S(2)}) async-start(f32[32,1,64]{2,1,0:T(1,128)} %late.1), calls=%async_computation | async-start | bytes 32768 | tf_op jit(solution)/shard_map/all_to_all | solution.py:666
  60.0 4.4 %spell.1 = f32[640,2048]{1,0:T(8,128)} custom-call(s32[32,2048]{1,0:T(8,128)S(1)} %get-tuple-element.19.spins_ref, s32[2,32,256]{2,1,0:T(8,128)S(1)} %get-tuple-element.23.sides_ref), custom_call_target="tpu_custom_call" | custom-call | flops 1310720 | bytes 5242880 | tf_op jit(solution)/shard_map/spell/pallas_call | solution.py:603
  64.4 2.8 %all-to-all-done = f32[32,1,64]{2,1,0:T(1,128)S(1)} async-done(((f32[32,1,64]{2,1,0:T(1,128)}), f32[32,1,64]{2,1,0:T(1,128)S(1)}, u32[]{:S(2)}, u32[]{:S(2)}) %all-to-all-start) | async-done | bytes 8224 | tf_op jit(solution)/shard_map/all_to_all | solution.py:666
  67.2 0.5 broadcast_multiply_fusion
  (14 shorter events, 0.2 us)
Async XLA Ops:
  0.6 1.7 %copy-start = (bf16[640,2048]{1,0:T(8,128)(2,1)S(1)}, bf16[640,2048]{1,0:T(8,128)(2,1)}, u32[]{:S(2)}) copy-start(bf16[640,2048]{1,0:T(8,128)(2,1)} %moments_hbm.5) | copy-start | bytes 7864324
  2.4 0.7 copy-start.2
  9.4 11.1 %collective-permute-start = (bf16[32,2048]{1,0:T(8,128)(2,1)S(1)}, bf16[32,2048]{1,0:T(8,128)(2,1)S(1)}, u32[]{:S(2)}, u32[]{:S(2)}) collective-permute-start(bf16[32,2048]{1,0:T(8,128)(2,1)S(1)} %get-tuple-element.17), channel_id=1, source_target_pairs={{0,4},{4,8},{8,12},{12,16},{16,20},{20,24},{24,28},{28,0},{1,5},{5... | collective-permute-start | bytes 393224 | tf_op jit(solution)/shard_map/ppermute | solution.py:527
  10.0 10.6 %collective-permute-start.1 = (bf16[32,2048]{1,0:T(8,128)(2,1)S(1)}, bf16[32,2048]{1,0:T(8,128)(2,1)S(1)}, u32[]{:S(2)}, u32[]{:S(2)}) collective-permute-start(bf16[32,2048]{1,0:T(8,128)(2,1)S(1)} %get-tuple-element.18), channel_id=1, source_target_pairs={{0,28},{4,0},{8,4},{12,8},{16,12},{20,16},{24,20},{28,24},{1,29},{... | collective-permute-start | bytes 393224 | tf_op jit(solution)/shard_map/ppermute | solution.py:528
  14.1 30.6 %collective-permute-start.5 = (bf16[6,128,256]{2,1,0:T(8,128)(2,1)S(1)}, bf16[6,128,256]{2,1,0:T(8,128)(2,1)S(1)}, u32[]{:S(2)}, u32[]{:S(2)}) collective-permute-start(bf16[6,128,256]{2,1,0:T(8,128)(2,1)S(1)} %get-tuple-element.28.refs_1_), channel_id=1, source_target_pairs={{0,1},{1,0},{2,3},{3,2},{4,5},{5,4},{6,7},{7,6},{8,9},{9,8},{10,11... | collective-permute-start | bytes 1179656 | tf_op jit(solution)/shard_map/ppermute | solution.py:482
  16.0 4.6 %copy-start.1 = (bf16[640,2048]{1,0:T(8,128)(2,1)S(1)}, bf16[640,2048]{1,0:T(8,128)(2,1)}, u32[]{:S(2)}) copy-start(bf16[640,2048]{1,0:T(8,128)(2,1)} %moments_hbm.5) | copy-start | bytes 7864324
  22.6 28.5 %collective-permute-start.4 = (bf16[6,192,256]{2,1,0:T(8,128)(2,1)S(1)}, bf16[6,192,256]{2,1,0:T(8,128)(2,1)S(1)}, u32[]{:S(2)}, u32[]{:S(2)}) collective-permute-start(bf16[6,192,256]{2,1,0:T(8,128)(2,1)S(1)} %get-tuple-element.27.refs_0_), channel_id=1, source_target_pairs={{0,1},{1,0},{2,3},{3,2},{4,5},{5,4},{6,7},{7,6},{8,9},{9,8},{10,11... | collective-permute-start | bytes 1769480 | tf_op jit(solution)/shard_map/ppermute | solution.py:482
  22.8 28.3 %collective-permute-start.7 = (bf16[6,192,256]{2,1,0:T(8,128)(2,1)S(1)}, bf16[6,192,256]{2,1,0:T(8,128)(2,1)S(1)}, u32[]{:S(2)}, u32[]{:S(2)}) collective-permute-start(bf16[6,192,256]{2,1,0:T(8,128)(2,1)S(1)} %get-tuple-element.24.refs_3_.refs_0_), channel_id=1, source_target_pairs={{0,2},{1,3},{2,0},{3,1},{4,6},{5,7},{6,4},{7,5},{8,10},{9,11},{10,... | collective-permute-start | bytes 1769480 | tf_op jit(solution)/shard_map/ppermute | solution.py:483
  24.7 26.3 %collective-permute-start.8 = (bf16[6,128,256]{2,1,0:T(8,128)(2,1)S(1)}, bf16[6,128,256]{2,1,0:T(8,128)(2,1)S(1)}, u32[]{:S(2)}, u32[]{:S(2)}) collective-permute-start(bf16[6,128,256]{2,1,0:T(8,128)(2,1)S(1)} %get-tuple-element.25.refs_4_.refs_1_), channel_id=1, source_target_pairs={{0,2},{1,3},{2,0},{3,1},{4,6},{5,7},{6,4},{7,5},{8,10},{9,11},{10,... | collective-permute-start | bytes 1179656 | tf_op jit(solution)/shard_map/ppermute | solution.py:483
  24.8 13.1 %collective-permute-start.2 = (bf16[96,128]{1,0:T(8,128)(2,1)S(1)}, bf16[96,128]{1,0:T(8,128)(2,1)S(1)}, u32[]{:S(2)}, u32[]{:S(2)}) collective-permute-start(bf16[96,128]{1,0:T(8,128)(2,1)S(1)} %get-tuple-element.21), channel_id=1, source_target_pairs={{0,1},{1,2},{2,3},{3,0},{4,5},{5,6},{6,7},{7,4},{8,9},{9,10},{10,1... | collective-permute-start | bytes 73736 | tf_op jit(solution)/shard_map/ppermute | solution.py:579
  37.9 3.8 %collective-permute-start.3 = (bf16[96,128]{1,0:T(8,128)(2,1)S(1)}, bf16[96,128]{1,0:T(8,128)(2,1)S(1)}, u32[]{:S(2)}, u32[]{:S(2)}) collective-permute-start(bf16[96,128]{1,0:T(8,128)(2,1)S(1)} %get-tuple-element.22), channel_id=1, source_target_pairs={{0,3},{1,0},{2,1},{3,2},{4,7},{5,4},{6,5},{7,6},{8,11},{9,8},{10,9... | collective-permute-start | bytes 73736 | tf_op jit(solution)/shard_map/ppermute | solution.py:580
  43.2 10.8 %collective-permute-start.6 = (bf16[2,320,256]{2,1,0:T(8,128)(2,1)S(1)}, bf16[2,320,256]{2,1,0:T(8,128)(2,1)S(1)}, u32[]{:S(2)}, u32[]{:S(2)}) collective-permute-start(bf16[2,320,256]{2,1,0:T(8,128)(2,1)S(1)} %get-tuple-element.29.refs_2_), channel_id=1, source_target_pairs={{0,1},{1,0},{2,3},{3,2},{4,5},{5,4},{6,7},{7,6},{8,9},{9,8},{10,11... | collective-permute-start | bytes 983048 | tf_op jit(solution)/shard_map/ppermute | solution.py:482
  44.7 9.3 %collective-permute-start.9 = (bf16[2,320,256]{2,1,0:T(8,128)(2,1)S(1)}, bf16[2,320,256]{2,1,0:T(8,128)(2,1)S(1)}, u32[]{:S(2)}, u32[]{:S(2)}) collective-permute-start(bf16[2,320,256]{2,1,0:T(8,128)(2,1)S(1)} %get-tuple-element.26.refs_5_.refs_2_), channel_id=1, source_target_pairs={{0,2},{1,3},{2,0},{3,1},{4,6},{5,7},{6,4},{7,5},{8,10},{9,11},{10,... | collective-permute-start | bytes 983048 | tf_op jit(solution)/shard_map/ppermute | solution.py:483
  57.0 10.2 %all-to-all-start = ((f32[32,1,64]{2,1,0:T(1,128)}), f32[32,1,64]{2,1,0:T(1,128)S(1)}, u32[]{:S(2)}, u32[]{:S(2)}) async-start(f32[32,1,64]{2,1,0:T(1,128)} %late.1), calls=%async_computation | async-start | bytes 32768 | tf_op jit(solution)/shard_map/all_to_all | solution.py:666

commit v3 on v2

--- a/solution.py
+++ b/solution.py
@@ -1,4 +1,3 @@
-import functools
 import math
 
 import jax
@@ -14,7 +13,7 @@
 LANES = 128
 TILE = 256
 PER_STEP = 2
-MIDDLE = 4
+MIDDLE = 7
 WORDS = 1 + 2 * SWEEPS
 
 
@@ -133,6 +132,7 @@
     edge_draws,
     moments_buf,
     final_ref,
+    bar_smem,
     sems,
     edge_sems,
 ):
@@ -165,8 +165,11 @@
         moments_buf,
         edge_sems.at[2, 0],
     )
-    for copy in sum(edges + copies, []) + [weights]:
+    bars = pltpu.make_async_copy(bar_ref, bar_smem, edge_sems.at[2, 1])
+    for copy in [bars] + sum(edges + copies, []) + [weights]:
         copy.start()
+    bars.wait()
+    bar_ref = bar_smem
     for s, ref in enumerate((last_ref, first_ref)):
         for copy in edges[s]:
             copy.wait()
@@ -194,7 +197,20 @@
                 )
 
 
-def outer_kernel(bar_ref, spins_hbm, draws_hbm, middle_ref, words_ref, spins_buf, draws_buf, sems):
+def outer_kernel(
+    bar_ref,
+    spins_hbm,
+    draws_hbm,
+    middle_ref,
+    words_ref,
+    spins_buf,
+    draws_buf,
+    bar_smem,
+    sems,
+    bar_sem,
+):
+    bars = pltpu.make_async_copy(bar_ref, bar_smem, bar_sem)
+    bars.start()
     planes = spins_hbm.shape[0] // DEPTH
     side = planes // 2 - MIDDLE - 1
     outer = list(range(side)) + list(range(planes - side, planes))
@@ -216,6 +232,8 @@
         for copy in copies[-1]:
             copy.start()
     words_ref[...] = middle_ref[...]
+    bars.wait()
+    bar_ref = bar_smem
     for g in range(0, len(outer), PER_STEP):
         group = outer[g : g + PER_STEP]
         for copy in sum(copies[g : g + PER_STEP], []):
@@ -465,12 +483,14 @@
     assert columns == R and col_devices % 2 == 0 and planes % 2 == 0 and planes + 2 <= 26
     vmem = pl.BlockSpec(memory_space=pltpu.VMEM)
     smem = pl.BlockSpec(memory_space=pltpu.SMEM)
-    anywhere = pl.BlockSpec(memory_space=pl.ANY)
+    anywhere = pl.BlockSpec(memory_space=pltpu.HBM)
     strip = jax.ShapeDtypeStruct((8 * (2 + SWEEPS), columns), jnp.bfloat16)
     edge = jax.ShapeDtypeStruct((DEPTH * (1 + SWEEPS), LANES), jnp.bfloat16)
     words_shape = jax.ShapeDtypeStruct((WORDS, DEPTH, columns), jnp.int32)
     dma = pltpu.SemaphoreType.DMA
     odd = (lax.axis_index("col") % 2).reshape(1)
+    moments = pltpu.with_memory_space_constraint(moments, pltpu.HBM)
+    accept_bar = pltpu.with_memory_space_constraint(accept_bar, pltpu.HBM)
 
     def message(count, height):
         return jax.ShapeDtypeStruct((count, height, TILE), jnp.bfloat16)
@@ -479,13 +499,11 @@
         return [(i, (i + step) % size) for i in range(size)]
 
     def exchange(given, kept):
-        mid = lax.ppermute(given, "col", [(i, i ^ 1) for i in range(col_devices)])
-        far = lax.ppermute(
-            kept, "col", [(i, (i - 2 + 4 * (i % 2)) % col_devices) for i in range(col_devices)]
-        )
-        return mid, far
-
-    def call(kernel, name, specs, shapes, scratch, flops, moved, *operands):
+        beside = [(i, i ^ 1) for i in range(col_devices)]
+        beyond = [(i, (i - 2 + 4 * (i % 2)) % col_devices) for i in range(col_devices)]
+        return lax.ppermute(given, "col", beside), lax.ppermute(kept, "col", beyond)
+
+    def call(kernel, specs, shapes, scratch, flops, moved, *operands):
         return pl.pallas_call(
             kernel,
             in_specs=specs,
@@ -494,15 +512,13 @@
             scratch_shapes=scratch,
             compiler_params=params(),
             cost_estimate=pl.CostEstimate(flops=flops, bytes_accessed=moved, transcendentals=0),
-            name=name,
         )(*operands)
 
     packed = (2 * MIDDLE + 2) * DEPTH
     middle = message(tiles - 2, MIDDLE * DEPTH)
     words, last, leading, given, kept = call(
         middle_kernel,
-        "middle",
-        [smem, smem, anywhere, anywhere, anywhere],
+        [smem, anywhere, anywhere, anywhere, anywhere],
         [words_shape, strip, strip, middle, middle],
         [
             pltpu.VMEM((packed, columns), jnp.int32),
@@ -511,6 +527,7 @@
             pltpu.VMEM((SWEEPS, 16, columns), jnp.float32),
             pltpu.VMEM((2 * MIDDLE * DEPTH, columns), jnp.bfloat16),
             pltpu.VMEM((DEPTH, columns), jnp.int32),
+            pltpu.SMEM((2,), jnp.float32),
             dma((pl.cdiv(2 * MIDDLE + 2, PER_STEP), 1 + SWEEPS)),
             dma((3, 1 + SWEEPS)),
         ],
@@ -530,13 +547,14 @@
     remaining = rows - packed
     words = call(
         outer_kernel,
-        "outer",
-        [smem, anywhere, anywhere, vmem],
+        [anywhere, anywhere, anywhere, vmem],
         words_shape,
         [
             pltpu.VMEM((remaining, columns), jnp.int32),
             pltpu.VMEM((SWEEPS, remaining, columns), jnp.float32),
+            pltpu.SMEM((2,), jnp.float32),
             dma((remaining // DEPTH, 1 + SWEEPS)),
+            dma(()),
         ],
         40 * remaining * columns,
         4 * (1 + SWEEPS) * remaining * columns,
@@ -550,7 +568,6 @@
     reach = 2 * (TILE + LANES)
     spins, sides, right, left, given, kept = call(
         inner_kernel,
-        "inner",
         [smem, vmem, vmem, vmem, anywhere],
         [
             jax.ShapeDtypeStruct((DEPTH, columns), jnp.int32),
@@ -581,7 +598,6 @@
     ends = message(2, half_rows)
     side_spins, given, kept = call(
         side_kernel,
-        "side",
         [smem, vmem, vmem, vmem, anywhere],
         [jax.ShapeDtypeStruct((2, DEPTH, TILE), jnp.int32), ends, ends],
         [
@@ -620,7 +636,6 @@
     work = rows * columns * columns
     base = call(
         own_kernel,
-        "own",
         [vmem] * 6,
         folded,
         [sums, pltpu.VMEM((2, tiles, half_rows, TILE), jnp.bfloat16), dma((8,))],
@@ -630,7 +645,6 @@
     )
     base = call(
         early_kernel,
-        "early",
         [smem] + [vmem] * 7,
         folded,
         [sums],
@@ -644,7 +658,6 @@
     )
     partial_sums = call(
         late_kernel,
-        "late",
         [smem] + [vmem] * 10,
         jax.ShapeDtypeStruct((devices, 1, R // devices), jnp.float32),
         [sums],

time: 67.9 us -> 67 us (0.987)
  local copies, waits for them, and re-layouts: 2.39 us -> 0 us
  starting transfers between devices: 18 us -> 19.1 us
    unnamed x6 -> x0, local copies, waits for them, and re-layouts: 2.39 us -> none
    ppermute x6, starting transfers between devices: 7.14 us -> 8.58 us  [the longest x3 5.03 us: exchange(): lax.ppermute(given, 'col', beside)]
    all_to_all x1, starting transfers between devices: 2.95 us -> 4.06 us  [on_device(): shares = lax.all_to_all(partial_sums, ('row', 'col'), 0, 0, tiled=True)]
  transfers between devices with their start and end apart: 11 -> 11, of which waited for: 3 -> 4; matrix products, arithmetic and copies ran while one was open for 0% -> 0% of each run, Pallas kernels for 30% -> 28%
where the time goes in v3:
time: 67 us; the launch traced here: 66.8 us
  Pallas kernels  29.9 us (45%)
  starting transfers between devices  19.1 us (29%)
  waiting for transfers between devices  16.5 us (25%)
  between operations  0.73 us (1%)
    pallas_call x7, Pallas kernels, call(): pl.pallas_call(kernel, in_specs=specs, out_specs=jax.tree.map(lambda _: v...  25.5 us
    ppermute x1, waiting for transfers between devices, on_device(): before = lax.ppermute(right, 'col', ring(col_devices, 1))  10.8 us
    ppermute x3, starting transfers between devices, exchange(): lax.ppermute(given, 'col', beside)  5.03 us
    pallas_call x1, Pallas kernels, on_device(): pl.pallas_call(spell_kernel, grid=(rows // (PER_STEP * DEPTH),), in_specs...  4.44 us
    all_to_all x1, starting transfers between devices, on_device(): shares = lax.all_to_all(partial_sums, ('row', 'col'), 0, 0, tiled=True)  4.06 us
    ppermute x3, starting transfers between devices, exchange(): lax.ppermute(kept, 'col', beyond)  3.55 us
    ppermute x1, starting transfers between devices, on_device(): below = lax.ppermute(leading, 'row', ring(row_devices, -1))  3.54 us
    all_to_all x1, waiting for transfers between devices, on_device(): shares = lax.all_to_all(partial_sums, ('row', 'col'), 0, 0, tiled=True)  2.76 us
  transfers between devices with their start and end apart: 11, of which 4 were waited for; matrix products, arithmetic and copies ran while one was open for 0% of the time, Pallas kernels for 28%

profile of v3, /device:TPU:0, one launch (start us, length us, event | category | flops | bytes accessed | tf_op | source)
XLA Modules:
  0.0 66.8 jit_solution(14677301128341665279)
XLA Ops:
  0.6 8.4 %shard_map.59 = (s32[5,32,2048]{2,1,0:T(8,128)S(1)}, bf16[32,2048]{1,0:T(8,128)(2,1)S(1)}, bf16[32,2048]{1,0:T(8,128)(2,1)S(1)}, bf16[6,224,256]{2,1,0:T(8,128)(2,1)S(1)}, bf16[6,224,256]{2,1,0:T(8,128)(2,1)S(1)}) custom-call(s32[1]{0:T(128)} %bitcast.odd_ref, f32[2]{0:T(128)} %bar_ref.3, s32[640,2048]{1,0:T(8,128)} %spins_hbm.3, f32[2,640,2048]{2,1,0:T(8,128)} %draws_hbm.3, ...), custom_call_target="tpu_custom_call" | custom-call | flops 41943040 | bytes 12582912 | tf_op jit(solution)/shard_map/pallas_call | solution.py:507
  9.1 3.0 %collective-permute-start.5 = (bf16[6,224,256]{2,1,0:T(8,128)(2,1)S(1)}, bf16[6,224,256]{2,1,0:T(8,128)(2,1)S(1)}, u32[]{:S(2)}, u32[]{:S(2)}) collective-permute-start(bf16[6,224,256]{2,1,0:T(8,128)(2,1)S(1)} %get-tuple-element.28.refs_1_), channel_id=1, source_target_pairs={{0,1},{1,0},{2,3},{3,2},{4,5},{5,4},{6,7},{7,6},{8,9},{9,8},{10,11... | collective-permute-start | bytes 2064392 | tf_op jit(solution)/shard_map/ppermute | solution.py:504
  12.1 1.5 %collective-permute-start.8 = (bf16[6,224,256]{2,1,0:T(8,128)(2,1)S(1)}, bf16[6,224,256]{2,1,0:T(8,128)(2,1)S(1)}, u32[]{:S(2)}, u32[]{:S(2)}) collective-permute-start(bf16[6,224,256]{2,1,0:T(8,128)(2,1)S(1)} %get-tuple-element.25.refs_4_.refs_1_), channel_id=1, source_target_pairs={{0,2},{1,3},{2,0},{3,1},{4,6},{5,7},{6,4},{7,5},{8,10},{9,11},{10,... | collective-permute-start | bytes 2064392 | tf_op jit(solution)/shard_map/ppermute | solution.py:504
  13.6 3.5 %collective-permute-start.1 = (bf16[32,2048]{1,0:T(8,128)(2,1)S(1)}, bf16[32,2048]{1,0:T(8,128)(2,1)S(1)}, u32[]{:S(2)}, u32[]{:S(2)}) collective-permute-start(bf16[32,2048]{1,0:T(8,128)(2,1)S(1)} %get-tuple-element.18), channel_id=1, source_target_pairs={{0,28},{4,0},{8,4},{12,8},{16,12},{20,16},{24,20},{28,24},{1,29},{... | collective-permute-start | bytes 393224 | tf_op jit(solution)/shard_map/ppermute | solution.py:545
  17.2 2.2 %shard_map.60.words_ref = s32[5,32,2048]{2,1,0:T(8,128)S(1)} custom-call(f32[2]{0:T(128)} %bar_ref.3, s32[640,2048]{1,0:T(8,128)} %spins_hbm.3, f32[2,640,2048]{2,1,0:T(8,128)} %draws_hbm.3, s32[5,32,2048]{2,1,0:T(8,128)S(1)} %get-tuple-element.16.middle_ref), custom_call_target="tpu_custom_call" | custom-call | flops 10485760 | bytes 3145728 | tf_op jit(solution)/shard_map/pallas_call | solution.py:507
  19.4 0.5 collective-permute-done.above_ref
  19.9 2.4 %shard_map.61 = (s32[32,2048]{1,0:T(8,128)S(1)}, s32[5,32,768]{2,1,0:T(8,128)S(1)}, bf16[96,128]{1,0:T(8,128)(2,1)S(1)}, bf16[96,128]{1,0:T(8,128)(2,1)S(1)}, bf...) custom-call(s32[1]{0:T(128)} %bitcast.odd_ref, s32[5,32,2048]{2,1,0:T(8,128)S(1)} %shard_map.60.words_ref, ...), custom_call_target="tpu_custom_call" | custom-call | flops 52428800 | bytes 5242880 | tf_op jit(solution)/shard_map/pallas_call | solution.py:507
  22.3 0.6 collective-permute-start.4
  22.9 1.5 %collective-permute-start.2 = (bf16[96,128]{1,0:T(8,128)(2,1)S(1)}, bf16[96,128]{1,0:T(8,128)(2,1)S(1)}, u32[]{:S(2)}, u32[]{:S(2)}) collective-permute-start(bf16[96,128]{1,0:T(8,128)(2,1)S(1)} %get-tuple-element.21), channel_id=1, source_target_pairs={{0,1},{1,2},{2,3},{3,0},{4,5},{5,6},{6,7},{7,4},{8,9},{9,10},{10,1... | collective-permute-start | bytes 73736 | tf_op jit(solution)/shard_map/ppermute | solution.py:596
  24.4 0.5 collective-permute-start.7
  24.9 10.8 %collective-permute-done.2.before_ref = bf16[96,128]{1,0:T(8,128)(2,1)S(1)} collective-permute-done((bf16[96,128]{1,0:T(8,128)(2,1)S(1)}, bf16[96,128]{1,0:T(8,128)(2,1)S(1)}, u32[]{:S(2)}, u32[]{:S(2)}) %collective-permute-start.2) | collective-permute-done | bytes 24608 | tf_op jit(solution)/shard_map/ppermute | solution.py:596
  35.7 1.4 %collective-permute-start.3 = (bf16[96,128]{1,0:T(8,128)(2,1)S(1)}, bf16[96,128]{1,0:T(8,128)(2,1)S(1)}, u32[]{:S(2)}, u32[]{:S(2)}) collective-permute-start(bf16[96,128]{1,0:T(8,128)(2,1)S(1)} %get-tuple-element.22), channel_id=1, source_target_pairs={{0,3},{1,0},{2,1},{3,2},{4,7},{5,4},{6,5},{7,6},{8,11},{9,8},{10,9... | collective-permute-start | bytes 73736 | tf_op jit(solution)/shard_map/ppermute | solution.py:597
  37.1 2.4 %collective-permute-done.3.after_ref = bf16[96,128]{1,0:T(8,128)(2,1)S(1)} collective-permute-done((bf16[96,128]{1,0:T(8,128)(2,1)S(1)}, bf16[96,128]{1,0:T(8,128)(2,1)S(1)}, u32[]{:S(2)}, u32[]{:S(2)}) %collective-permute-start.3) | collective-permute-done | bytes 24608 | tf_op jit(solution)/shard_map/ppermute | solution.py:597
  39.5 1.7 %shard_map.62 = (s32[2,32,256]{2,1,0:T(8,128)S(1)}, bf16[2,320,256]{2,1,0:T(8,128)(2,1)S(1)}, bf16[2,320,256]{2,1,0:T(8,128)(2,1)S(1)}) custom-call(s32[1]{0:T(128)} %bitcast.odd_ref, s32[5,32,768]{2,1,0:T(8,128)S(1)} %get-tuple-element.20.sides_ref, bf16[96,128]{1,0:T(8,128)(2,1)S(1)} %collective-permute-done.2.before_ref, ...), custom_call_target="tpu_custom_call" | custom-call | flops 13107200 | bytes 1310720 | tf_op jit(solution)/shard_map/pallas_call | solution.py:507
  41.2 1.4 %collective-permute-start.6 = (bf16[2,320,256]{2,1,0:T(8,128)(2,1)S(1)}, bf16[2,320,256]{2,1,0:T(8,128)(2,1)S(1)}, u32[]{:S(2)}, u32[]{:S(2)}) collective-permute-start(bf16[2,320,256]{2,1,0:T(8,128)(2,1)S(1)} %get-tuple-element.29.refs_2_), channel_id=1, source_target_pairs={{0,1},{1,0},{2,3},{3,2},{4,5},{5,4},{6,7},{7,6},{8,9},{9,8},{10,11... | collective-permute-start | bytes 983048 | tf_op jit(solution)/shard_map/ppermute | solution.py:504
  42.6 1.5 %collective-permute-start.9 = (bf16[2,320,256]{2,1,0:T(8,128)(2,1)S(1)}, bf16[2,320,256]{2,1,0:T(8,128)(2,1)S(1)}, u32[]{:S(2)}, u32[]{:S(2)}) collective-permute-start(bf16[2,320,256]{2,1,0:T(8,128)(2,1)S(1)} %get-tuple-element.26.refs_5_.refs_2_), channel_id=1, source_target_pairs={{0,2},{1,3},{2,0},{3,1},{4,6},{5,7},{6,4},{7,5},{8,10},{9,11},{10,... | collective-permute-start | bytes 983048 | tf_op jit(solution)/shard_map/ppermute | solution.py:504
  44.1 4.9 %shard_map.63.refs_6_ = f32[8,2176]{1,0:T(8,128)S(1)} custom-call(bf16[6,96,256]{2,1,0:T(8,128)(2,1)S(1)} %get-tuple-element.27.refs_0_, bf16[6,224,256]{2,1,0:T(8,128)(2,1)S(1)} %get-tuple-element.28.refs_1_, bf16[2,320,256]{2,1,0:T(8,128)(2,1)S(1)} %get-tuple-element.29.refs_2_, bf16[6,96,256]{2,1,0:T(8,128)(2,1)S(1)} %get-tuple-element.24.refs_3_.refs_0_, ...), custom_call_target="tpu_custom_call" | custom-call | flops 2684354560 | bytes 2621440 | tf_op jit(solution)/shard_map/pallas_call | solution.py:507
  49.1 2.8 %shard_map.64.refs_9_ = f32[8,2176]{1,0:T(8,128)S(1)} custom-call(s32[1]{0:T(128)} %bitcast.odd_ref, bf16[6,96,256]{2,1,0:T(8,128)(2,1)S(1)} %get-tuple-element.24.refs_3_.refs_0_, bf16[6,224,256]{2,1,0:T(8,128)(2,1)S(1)} %get-tuple-element.25.refs_4_.refs_1_, bf16[6,96,256]{2,1,0:T(8,128)(2,1)S(1)} %collective-permute-done.4.refs_2_.refs_3_, ...), custom_call_target="tpu_custom_call" | custom-call | flops 1342177280 | bytes 2621440 | tf_op jit(solution)/shard_map/pallas_call | solution.py:507
  51.9 3.0 %shard_map.65 = f32[32,1,64]{2,1,0:T(1,128)} custom-call(s32[1]{0:T(128)} %bitcast.odd_ref, bf16[6,96,256]{2,1,0:T(8,128)(2,1)S(1)} %get-tuple-element.24.refs_3_.refs_0_, bf16[6,224,256]{2,1,0:T(8,128)(2,1)S(1)} %get-tuple-element.25.refs_4_.refs_1_, bf16[2,320,256]{2,1,0:T(8,128)(2,1)S(1)} %get-tuple-element.26.refs_5_.refs_2_, ...), custom_call_target="tpu_custom_call" | custom-call | flops 1342177280 | bytes 2621440 | tf_op jit(solution)/shard_map/pallas_call | solution.py:507
  54.9 4.1 %all-to-all-start = ((f32[32,1,64]{2,1,0:T(1,128)}), f32[32,1,64]{2,1,0:T(1,128)S(1)}, u32[]{:S(2)}, u32[]{:S(2)}) async-start(f32[32,1,64]{2,1,0:T(1,128)} %shard_map.65), calls=%async_computation | async-start | bytes 32768 | tf_op jit(solution)/shard_map/all_to_all | solution.py:679
  59.0 4.4 %spell.1 = f32[640,2048]{1,0:T(8,128)} custom-call(s32[32,2048]{1,0:T(8,128)S(1)} %get-tuple-element.19.spins_ref, s32[2,32,256]{2,1,0:T(8,128)S(1)} %get-tuple-element.23.sides_ref), custom_call_target="tpu_custom_call" | custom-call | flops 1310720 | bytes 5242880 | tf_op jit(solution)/shard_map/spell/pallas_call | solution.py:619
  63.4 2.8 %all-to-all-done = f32[32,1,64]{2,1,0:T(1,128)S(1)} async-done(((f32[32,1,64]{2,1,0:T(1,128)}), f32[32,1,64]{2,1,0:T(1,128)S(1)}, u32[]{:S(2)}, u32[]{:S(2)}) %all-to-all-start) | async-done | bytes 8224 | tf_op jit(solution)/shard_map/all_to_all | solution.py:679
  66.2 0.1 reduce_sum.9
  66.2 0.5 broadcast_multiply_fusion
  (8 shorter events, 0.0 us)
Async XLA Ops:
  9.1 40.0 %collective-permute-start.5 = (bf16[6,224,256]{2,1,0:T(8,128)(2,1)S(1)}, bf16[6,224,256]{2,1,0:T(8,128)(2,1)S(1)}, u32[]{:S(2)}, u32[]{:S(2)}) collective-permute-start(bf16[6,224,256]{2,1,0:T(8,128)(2,1)S(1)} %get-tuple-element.28.refs_1_), channel_id=1, source_target_pairs={{0,1},{1,0},{2,3},{3,2},{4,5},{5,4},{6,7},{7,6},{8,9},{9,8},{10,11... | collective-permute-start | bytes 2064392 | tf_op jit(solution)/shard_map/ppermute | solution.py:504
  12.1 37.0 %collective-permute-start.8 = (bf16[6,224,256]{2,1,0:T(8,128)(2,1)S(1)}, bf16[6,224,256]{2,1,0:T(8,128)(2,1)S(1)}, u32[]{:S(2)}, u32[]{:S(2)}) collective-permute-start(bf16[6,224,256]{2,1,0:T(8,128)(2,1)S(1)} %get-tuple-element.25.refs_4_.refs_1_), channel_id=1, source_target_pairs={{0,2},{1,3},{2,0},{3,1},{4,6},{5,7},{6,4},{7,5},{8,10},{9,11},{10,... | collective-permute-start | bytes 2064392 | tf_op jit(solution)/shard_map/ppermute | solution.py:504
  13.6 6.3 %collective-permute-start = (bf16[32,2048]{1,0:T(8,128)(2,1)S(1)}, bf16[32,2048]{1,0:T(8,128)(2,1)S(1)}, u32[]{:S(2)}, u32[]{:S(2)}) collective-permute-start(bf16[32,2048]{1,0:T(8,128)(2,1)S(1)} %get-tuple-element.17), channel_id=1, source_target_pairs={{0,4},{4,8},{8,12},{12,16},{16,20},{20,24},{24,28},{28,0},{1,5},{5... | collective-permute-start | bytes 393224 | tf_op jit(solution)/shard_map/ppermute | solution.py:544
  13.6 6.3 %collective-permute-start.1 = (bf16[32,2048]{1,0:T(8,128)(2,1)S(1)}, bf16[32,2048]{1,0:T(8,128)(2,1)S(1)}, u32[]{:S(2)}, u32[]{:S(2)}) collective-permute-start(bf16[32,2048]{1,0:T(8,128)(2,1)S(1)} %get-tuple-element.18), channel_id=1, source_target_pairs={{0,28},{4,0},{8,4},{12,8},{16,12},{20,16},{24,20},{28,24},{1,29},{... | collective-permute-start | bytes 393224 | tf_op jit(solution)/shard_map/ppermute | solution.py:545
  22.3 20.3 %collective-permute-start.4 = (bf16[6,96,256]{2,1,0:T(8,128)(2,1)S(1)}, bf16[6,96,256]{2,1,0:T(8,128)(2,1)S(1)}, u32[]{:S(2)}, u32[]{:S(2)}) collective-permute-start(bf16[6,96,256]{2,1,0:T(8,128)(2,1)S(1)} %get-tuple-element.27.refs_0_), channel_id=1, source_target_pairs={{0,1},{1,0},{2,3},{3,2},{4,5},{5,4},{6,7},{7,6},{8,9},{9,8},{10,11... | collective-permute-start | bytes 884744 | tf_op jit(solution)/shard_map/ppermute | solution.py:504
  22.9 12.8 %collective-permute-start.2 = (bf16[96,128]{1,0:T(8,128)(2,1)S(1)}, bf16[96,128]{1,0:T(8,128)(2,1)S(1)}, u32[]{:S(2)}, u32[]{:S(2)}) collective-permute-start(bf16[96,128]{1,0:T(8,128)(2,1)S(1)} %get-tuple-element.21), channel_id=1, source_target_pairs={{0,1},{1,2},{2,3},{3,0},{4,5},{5,6},{6,7},{7,4},{8,9},{9,10},{10,1... | collective-permute-start | bytes 73736 | tf_op jit(solution)/shard_map/ppermute | solution.py:596
  24.4 24.6 %collective-permute-start.7 = (bf16[6,96,256]{2,1,0:T(8,128)(2,1)S(1)}, bf16[6,96,256]{2,1,0:T(8,128)(2,1)S(1)}, u32[]{:S(2)}, u32[]{:S(2)}) collective-permute-start(bf16[6,96,256]{2,1,0:T(8,128)(2,1)S(1)} %get-tuple-element.24.refs_3_.refs_0_), channel_id=1, source_target_pairs={{0,2},{1,3},{2,0},{3,1},{4,6},{5,7},{6,4},{7,5},{8,10},{9,11},{10,... | collective-permute-start | bytes 884744 | tf_op jit(solution)/shard_map/ppermute | solution.py:504
  35.7 3.8 %collective-permute-start.3 = (bf16[96,128]{1,0:T(8,128)(2,1)S(1)}, bf16[96,128]{1,0:T(8,128)(2,1)S(1)}, u32[]{:S(2)}, u32[]{:S(2)}) collective-permute-start(bf16[96,128]{1,0:T(8,128)(2,1)S(1)} %get-tuple-element.22), channel_id=1, source_target_pairs={{0,3},{1,0},{2,1},{3,2},{4,7},{5,4},{6,5},{7,6},{8,11},{9,8},{10,9... | collective-permute-start | bytes 73736 | tf_op jit(solution)/shard_map/ppermute | solution.py:597
  41.2 10.7 %collective-permute-start.6 = (bf16[2,320,256]{2,1,0:T(8,128)(2,1)S(1)}, bf16[2,320,256]{2,1,0:T(8,128)(2,1)S(1)}, u32[]{:S(2)}, u32[]{:S(2)}) collective-permute-start(bf16[2,320,256]{2,1,0:T(8,128)(2,1)S(1)} %get-tuple-element.29.refs_2_), channel_id=1, source_target_pairs={{0,1},{1,0},{2,3},{3,2},{4,5},{5,4},{6,7},{7,6},{8,9},{9,8},{10,11... | collective-permute-start | bytes 983048 | tf_op jit(solution)/shard_map/ppermute | solution.py:504
  42.6 9.3 %collective-permute-start.9 = (bf16[2,320,256]{2,1,0:T(8,128)(2,1)S(1)}, bf16[2,320,256]{2,1,0:T(8,128)(2,1)S(1)}, u32[]{:S(2)}, u32[]{:S(2)}) collective-permute-start(bf16[2,320,256]{2,1,0:T(8,128)(2,1)S(1)} %get-tuple-element.26.refs_5_.refs_2_), channel_id=1, source_target_pairs={{0,2},{1,3},{2,0},{3,1},{4,6},{5,7},{6,4},{7,5},{8,10},{9,11},{10,... | collective-permute-start | bytes 983048 | tf_op jit(solution)/shard_map/ppermute | solution.py:504
  54.9 11.3 %all-to-all-start = ((f32[32,1,64]{2,1,0:T(1,128)}), f32[32,1,64]{2,1,0:T(1,128)S(1)}, u32[]{:S(2)}, u32[]{:S(2)}) async-start(f32[32,1,64]{2,1,0:T(1,128)} %shard_map.65), calls=%async_computation | async-start | bytes 32768 | tf_op jit(solution)/shard_map/all_to_all | solution.py:679

commit v4 on v3

--- a/solution.py
+++ b/solution.py
@@ -1,3 +1,4 @@
+import functools
 import math
 
 import jax
@@ -13,7 +14,7 @@
 LANES = 128
 TILE = 256
 PER_STEP = 2
-MIDDLE = 7
+MIDDLE = 6
 WORDS = 1 + 2 * SWEEPS
 
 
@@ -111,8 +112,7 @@
 
 def weigh(spins, moments, plane):
     up = (spins & (jnp.int32(1) << (plane + 1))) != 0
-    size = moments.astype(jnp.float32)
-    return jnp.where(up, size, -size).astype(jnp.bfloat16)
+    return jnp.where(up, 1.0, -1.0).astype(jnp.bfloat16) * moments
 
 
 def middle_kernel(
@@ -391,28 +391,26 @@
     return value
 
 
+def tile(block, t):
+    low, high, ends = block
+    last = low.shape[0] + 1
+    if t in (0, last):
+        return ends[min(t, 1)]
+    return stack([low, high], t - 1, t)
+
+
+def tiles_of(block, places):
+    return jnp.concatenate([tile(block, t) for t in places], axis=0)
+
+
 def own_kernel(*refs):
-    parts, (out_ref, sums_ref, full_ref, sems) = refs[:-4], refs[-4:]
-    copies = []
-    for h in range(2):
-        low, high, ends = parts[3 * h : 3 * h + 3]
-        split = low.shape[1]
-        full = full_ref.at[h]
-        tiles = full_ref.shape[1]
-        for source, target in (
-            (low, full.at[pl.ds(1, tiles - 2), pl.ds(0, split)]),
-            (high, full.at[pl.ds(1, tiles - 2), pl.ds(split, high.shape[1])]),
-            (ends.at[0], full.at[0]),
-            (ends.at[1], full.at[tiles - 1]),
-        ):
-            copies.append(pltpu.make_async_copy(source, target, sems.at[len(copies)]))
-            copies[-1].start()
-    for copy in copies:
-        copy.wait()
+    parts, (out_ref, sums_ref) = refs[:-2], refs[-2:]
+    blocks = (parts[:3], parts[3:])
+    tiles = parts[0].shape[0] + 2
     for n in range(tiles):
         sums_ref[:, n * TILE : (n + 1) * TILE] = sum(
-            gram(stack([full_ref.at[h]], 0, tiles - n), stack([full_ref.at[h]], n, tiles))
-            for h in range(2)
+            gram(tiles_of(block, range(tiles - n)), tiles_of(block, range(n, tiles)))
+            for block in blocks
         )
     sums_ref[:, tiles * TILE :] = jnp.zeros((TILE, TILE), jnp.float32)
     out_ref[...] = fold(sums_ref)
@@ -443,25 +441,16 @@
     out_ref[...] = fold(sums_ref) + base_ref[...]
 
 
-def late_kernel(odd_ref, *refs):
+def late_kernel(scale, odd_ref, *refs):
     (base_ref, out_ref, sums_ref) = refs[-3:]
     tiles = refs[0].shape[0] + 2
     sums_ref[:, :TILE] = jnp.zeros((TILE, TILE), jnp.float32)
-
-    def tile(block, t):
-        low, high, ends = block
-        if t in (0, tiles - 1):
-            return ends[min(t, 1)]
-        return stack([low, high], t - 1, t)
 
     def run(pairs):
         for n in range(1, tiles + 1):
             places = [(tiles - 1, n - 1)] + ([(tiles - n, 0)] if n > 1 else [])
             sums_ref[:, n * TILE : (n + 1) * TILE] = sum(
-                gram(
-                    jnp.concatenate([tile(left, t) for t, _ in places], axis=0),
-                    jnp.concatenate([tile(right, q) for _, q in places], axis=0),
-                )
+                gram(tiles_of(left, [t for t, _ in places]), tiles_of(right, [q for _, q in places]))
                 for left, right in pairs
             )
 
@@ -469,9 +458,10 @@
     value = fold(sums_ref) + base_ref[...]
     for height in (4, 2, 1):
         value = value + pltpu.roll(pltpu.roll(value, value.shape[1] - height, 1), 8 - height, 0)
+    value = value[:1] * scale
     share = out_ref.shape[2]
     for d in range(out_ref.shape[0]):
-        out_ref[d] = value[:1, d * share : (d + 1) * share]
+        out_ref[d] = value[:, d * share : (d + 1) * share]
 
 
 def on_device(spins_up, uniforms, moments, accept_bar):
@@ -631,18 +621,11 @@
         ),
         name="spell",
     )(spins, side_spins)
+    normaliser = 1.0 / math.sqrt(rows * row_devices * columns * col_devices)
     sums = pltpu.VMEM((TILE, R + TILE), jnp.float32)
     folded = jax.ShapeDtypeStruct((8, R + LANES), jnp.float32)
     work = rows * columns * columns
-    base = call(
-        own_kernel,
-        [vmem] * 6,
-        folded,
-        [sums, pltpu.VMEM((2, tiles, half_rows, TILE), jnp.bfloat16), dma((8,))],
-        work,
-        2 * rows * columns,
-        *own,
-    )
+    base = call(own_kernel, [vmem] * 6, folded, [sums], work, 2 * rows * columns, *own)
     base = call(
         early_kernel,
         [smem] + [vmem] * 7,
@@ -657,7 +640,7 @@
         base,
     )
     partial_sums = call(
-        late_kernel,
+        functools.partial(late_kernel, normaliser),
         [smem] + [vmem] * 10,
         jax.ShapeDtypeStruct((devices, 1, R // devices), jnp.float32),
         [sums],
@@ -675,9 +658,8 @@
         far,
         base,
     )
-    normaliser = 1.0 / math.sqrt(rows * row_devices * columns * col_devices)
     shares = lax.all_to_all(partial_sums, ("row", "col"), 0, 0, tiled=True)
-    return spins_out, jnp.sum(shares, axis=(0, 1)) * normaliser
+    return spins_out, jnp.sum(shares, axis=(0, 1))
 
 
 def solution(mesh):

time: 67 us -> 74.3 us (1.11)
  waiting for transfers between devices: 16.5 us -> 25.9 us
  Pallas kernels: 29.9 us -> 28.6 us
  starting transfers between devices: 19.1 us -> 18.3 us
    ppermute x1, waiting for transfers between devices: 10.8 us -> 20.5 us  [on_device(): before = lax.ppermute(right, 'col', ring(col_devices, 1))]
    ppermute x3, starting transfers between devices: 5.03 us -> 3.49 us  [exchange(): lax.ppermute(given, 'col', beside)]
    pallas_call x7, Pallas kernels: 25.5 us -> 24.1 us  [call(): pl.pallas_call(kernel, in_specs=specs, out_specs=jax.tree.map(lambda _: v...]
    all_to_all x1, starting transfers between devices: 4.06 us -> 3.29 us  [on_device(): shares = lax.all_to_all(partial_sums, ('row', 'col'), 0, 0, tiled=True)]
  transfers between devices with their start and end apart: 11 -> 11, of which waited for: 4 -> 4; matrix products, arithmetic and copies ran while one was open for 0% -> 0% of each run, Pallas kernels for 28% -> 21%
where the time goes in v4:
time: 74.3 us; the launch traced here: 74.1 us
  Pallas kernels  28.6 us (38%)
  waiting for transfers between devices  25.9 us (35%)
  starting transfers between devices  18.3 us (25%)
    pallas_call x7, Pallas kernels, call(): pl.pallas_call(kernel, in_specs=specs, out_specs=jax.tree.map(lambda _: v...  24.1 us
    ppermute x1, waiting for transfers between devices, on_device(): before = lax.ppermute(right, 'col', ring(col_devices, 1))  20.5 us
    pallas_call x1, Pallas kernels, on_device(): pl.pallas_call(spell_kernel, grid=(rows // (PER_STEP * DEPTH),), in_specs...  4.44 us
    ppermute x1, starting transfers between devices, on_device(): below = lax.ppermute(leading, 'row', ring(row_devices, -1))  4.09 us
    ppermute x3, starting transfers between devices, exchange(): lax.ppermute(kept, 'col', beyond)  3.55 us
    ppermute x3, starting transfers between devices, exchange(): lax.ppermute(given, 'col', beside)  3.49 us
    all_to_all x1, starting transfers between devices, on_device(): shares = lax.all_to_all(partial_sums, ('row', 'col'), 0, 0, tiled=True)  3.29 us
    all_to_all x1, waiting for transfers between devices, on_device(): shares = lax.all_to_all(partial_sums, ('row', 'col'), 0, 0, tiled=True)  2.76 us
  transfers between devices with their start and end apart: 11, of which 4 were waited for; matrix products, arithmetic and copies ran while one was open for 0% of the time, Pallas kernels for 21%

profile of v4, /device:TPU:0, one launch (start us, length us, event | category | flops | bytes accessed | tf_op | source)
XLA Modules:
  0.0 74.1 jit_solution(10287010394369118560)
XLA Ops:
  0.6 7.5 %shard_map.59 = (s32[5,32,2048]{2,1,0:T(8,128)S(1)}, bf16[32,2048]{1,0:T(8,128)(2,1)S(1)}, bf16[32,2048]{1,0:T(8,128)(2,1)S(1)}, bf16[6,192,256]{2,1,0:T(8,128)(2,1)S(1)}, bf16[6,192,256]{2,1,0:T(8,128)(2,1)S(1)}) custom-call(s32[1]{0:T(128)} %bitcast.odd_ref, f32[2]{0:T(128)} %bar_ref.3, s32[640,2048]{1,0:T(8,128)} %spins_hbm.3, f32[2,640,2048]{2,1,0:T(8,128)} %draws_hbm.3, ...), custom_call_target="tpu_custom_call" | custom-call | flops 36700160 | bytes 11010048 | tf_op jit(solution)/shard_map/pallas_call | solution.py:497
  8.1 0.5 collective-permute-start
  8.7 4.1 %collective-permute-start.1 = (bf16[32,2048]{1,0:T(8,128)(2,1)S(1)}, bf16[32,2048]{1,0:T(8,128)(2,1)S(1)}, u32[]{:S(2)}, u32[]{:S(2)}) collective-permute-start(bf16[32,2048]{1,0:T(8,128)(2,1)S(1)} %get-tuple-element.18), channel_id=1, source_target_pairs={{0,28},{4,0},{8,4},{12,8},{16,12},{20,16},{24,20},{28,24},{1,29},{... | collective-permute-start | bytes 393224 | tf_op jit(solution)/shard_map/ppermute | solution.py:535
  12.8 2.7 %shard_map.60.words_ref = s32[5,32,2048]{2,1,0:T(8,128)S(1)} custom-call(f32[2]{0:T(128)} %bar_ref.3, s32[640,2048]{1,0:T(8,128)} %spins_hbm.3, f32[2,640,2048]{2,1,0:T(8,128)} %draws_hbm.3, s32[5,32,2048]{2,1,0:T(8,128)S(1)} %get-tuple-element.16.middle_ref), custom_call_target="tpu_custom_call" | custom-call | flops 15728640 | bytes 4718592 | tf_op jit(solution)/shard_map/pallas_call | solution.py:497
  15.5 2.5 %shard_map.61 = (s32[32,2048]{1,0:T(8,128)S(1)}, s32[5,32,768]{2,1,0:T(8,128)S(1)}, bf16[96,128]{1,0:T(8,128)(2,1)S(1)}, bf16[96,128]{1,0:T(8,128)(2,1)S(1)}, bf...) custom-call(s32[1]{0:T(128)} %bitcast.odd_ref, s32[5,32,2048]{2,1,0:T(8,128)S(1)} %shard_map.60.words_ref, ...), custom_call_target="tpu_custom_call" | custom-call | flops 52428800 | bytes 5242880 | tf_op jit(solution)/shard_map/pallas_call | solution.py:497
  18.0 2.0 %collective-permute-start.4 = (bf16[6,128,256]{2,1,0:T(8,128)(2,1)S(1)}, bf16[6,128,256]{2,1,0:T(8,128)(2,1)S(1)}, u32[]{:S(2)}, u32[]{:S(2)}) collective-permute-start(bf16[6,128,256]{2,1,0:T(8,128)(2,1)S(1)} %get-tuple-element.27.refs_0_), channel_id=1, source_target_pairs={{0,1},{1,0},{2,3},{3,2},{4,5},{5,4},{6,7},{7,6},{8,9},{9,8},{10,11... | collective-permute-start | bytes 1179656 | tf_op jit(solution)/shard_map/ppermute | solution.py:494
  20.0 0.1 collective-permute-start.5
  20.1 2.0 %collective-permute-start.8 = (bf16[6,192,256]{2,1,0:T(8,128)(2,1)S(1)}, bf16[6,192,256]{2,1,0:T(8,128)(2,1)S(1)}, u32[]{:S(2)}, u32[]{:S(2)}) collective-permute-start(bf16[6,192,256]{2,1,0:T(8,128)(2,1)S(1)} %get-tuple-element.25.refs_4_.refs_1_), channel_id=1, source_target_pairs={{0,2},{1,3},{2,0},{3,1},{4,6},{5,7},{6,4},{7,5},{8,10},{9,11},{10,... | collective-permute-start | bytes 1769480 | tf_op jit(solution)/shard_map/ppermute | solution.py:494
  22.1 0.1 collective-permute-start.7
  22.2 1.9 %collective-permute-start.2 = (bf16[96,128]{1,0:T(8,128)(2,1)S(1)}, bf16[96,128]{1,0:T(8,128)(2,1)S(1)}, u32[]{:S(2)}, u32[]{:S(2)}) collective-permute-start(bf16[96,128]{1,0:T(8,128)(2,1)S(1)} %get-tuple-element.21), channel_id=1, source_target_pairs={{0,1},{1,2},{2,3},{3,0},{4,5},{5,6},{6,7},{7,4},{8,9},{9,10},{10,1... | collective-permute-start | bytes 73736 | tf_op jit(solution)/shard_map/ppermute | solution.py:586
  24.1 20.5 %collective-permute-done.2.before_ref = bf16[96,128]{1,0:T(8,128)(2,1)S(1)} collective-permute-done((bf16[96,128]{1,0:T(8,128)(2,1)S(1)}, bf16[96,128]{1,0:T(8,128)(2,1)S(1)}, u32[]{:S(2)}, u32[]{:S(2)}) %collective-permute-start.2) | collective-permute-done | bytes 24608 | tf_op jit(solution)/shard_map/ppermute | solution.py:586
  44.6 1.4 %collective-permute-start.3 = (bf16[96,128]{1,0:T(8,128)(2,1)S(1)}, bf16[96,128]{1,0:T(8,128)(2,1)S(1)}, u32[]{:S(2)}, u32[]{:S(2)}) collective-permute-start(bf16[96,128]{1,0:T(8,128)(2,1)S(1)} %get-tuple-element.22), channel_id=1, source_target_pairs={{0,3},{1,0},{2,1},{3,2},{4,7},{5,4},{6,5},{7,6},{8,11},{9,8},{10,9... | collective-permute-start | bytes 73736 | tf_op jit(solution)/shard_map/ppermute | solution.py:587
  46.0 2.4 %collective-permute-done.3.after_ref = bf16[96,128]{1,0:T(8,128)(2,1)S(1)} collective-permute-done((bf16[96,128]{1,0:T(8,128)(2,1)S(1)}, bf16[96,128]{1,0:T(8,128)(2,1)S(1)}, u32[]{:S(2)}, u32[]{:S(2)}) %collective-permute-start.3) | collective-permute-done | bytes 24608 | tf_op jit(solution)/shard_map/ppermute | solution.py:587
  48.5 1.7 %shard_map.62 = (s32[2,32,256]{2,1,0:T(8,128)S(1)}, bf16[2,320,256]{2,1,0:T(8,128)(2,1)S(1)}, bf16[2,320,256]{2,1,0:T(8,128)(2,1)S(1)}) custom-call(s32[1]{0:T(128)} %bitcast.odd_ref, s32[5,32,768]{2,1,0:T(8,128)S(1)} %get-tuple-element.20.sides_ref, bf16[96,128]{1,0:T(8,128)(2,1)S(1)} %collective-permute-done.2.before_ref, ...), custom_call_target="tpu_custom_call" | custom-call | flops 13107200 | bytes 1310720 | tf_op jit(solution)/shard_map/pallas_call | solution.py:497
  50.1 1.4 %collective-permute-start.6 = (bf16[2,320,256]{2,1,0:T(8,128)(2,1)S(1)}, bf16[2,320,256]{2,1,0:T(8,128)(2,1)S(1)}, u32[]{:S(2)}, u32[]{:S(2)}) collective-permute-start(bf16[2,320,256]{2,1,0:T(8,128)(2,1)S(1)} %get-tuple-element.29.refs_2_), channel_id=1, source_target_pairs={{0,1},{1,0},{2,3},{3,2},{4,5},{5,4},{6,7},{7,6},{8,9},{9,8},{10,11... | collective-permute-start | bytes 983048 | tf_op jit(solution)/shard_map/ppermute | solution.py:494
  51.5 1.5 %collective-permute-start.9 = (bf16[2,320,256]{2,1,0:T(8,128)(2,1)S(1)}, bf16[2,320,256]{2,1,0:T(8,128)(2,1)S(1)}, u32[]{:S(2)}, u32[]{:S(2)}) collective-permute-start(bf16[2,320,256]{2,1,0:T(8,128)(2,1)S(1)} %get-tuple-element.26.refs_5_.refs_2_), channel_id=1, source_target_pairs={{0,2},{1,3},{2,0},{3,1},{4,6},{5,7},{6,4},{7,5},{8,10},{9,11},{10,... | collective-permute-start | bytes 983048 | tf_op jit(solution)/shard_map/ppermute | solution.py:494
  53.1 3.9 %shard_map.63.refs_6_ = f32[8,2176]{1,0:T(8,128)S(1)} custom-call(bf16[6,128,256]{2,1,0:T(8,128)(2,1)S(1)} %get-tuple-element.27.refs_0_, bf16[6,192,256]{2,1,0:T(8,128)(2,1)S(1)} %get-tuple-element.28.refs_1_, bf16[2,320,256]{2,1,0:T(8,128)(2,1)S(1)} %get-tuple-element.29.refs_2_, bf16[6,128,256]{2,1,0:T(8,128)(2,1)S(1)} %get-tuple-element.24.refs_3_.refs_0_, ...), custom_call_target="tpu_custom_call" | custom-call | flops 2684354560 | bytes 2621440 | tf_op jit(solution)/shard_map/pallas_call | solution.py:497
  56.9 2.8 %shard_map.64.refs_9_ = f32[8,2176]{1,0:T(8,128)S(1)} custom-call(s32[1]{0:T(128)} %bitcast.odd_ref, bf16[6,128,256]{2,1,0:T(8,128)(2,1)S(1)} %get-tuple-element.24.refs_3_.refs_0_, bf16[6,192,256]{2,1,0:T(8,128)(2,1)S(1)} %get-tuple-element.25.refs_4_.refs_1_, bf16[6,128,256]{2,1,0:T(8,128)(2,1)S(1)} %collective-permute-done.4.refs_2_.refs_3_, ...), custom_call_target="tpu_custom_call" | custom-call | flops 1342177280 | bytes 2621440 | tf_op jit(solution)/shard_map/pallas_call | solution.py:497
  59.8 0.2 collective-permute-done.9.refs_8_
  60.0 3.0 %shard_map.65 = f32[32,1,64]{2,1,0:T(1,128)} custom-call(s32[1]{0:T(128)} %bitcast.odd_ref, bf16[6,128,256]{2,1,0:T(8,128)(2,1)S(1)} %get-tuple-element.24.refs_3_.refs_0_, bf16[6,192,256]{2,1,0:T(8,128)(2,1)S(1)} %get-tuple-element.25.refs_4_.refs_1_, bf16[2,320,256]{2,1,0:T(8,128)(2,1)S(1)} %get-tuple-element.26.refs_5_.refs_2_, ...), custom_call_target="tpu_custom_call" | custom-call | flops 1342177280 | bytes 2621440 | tf_op jit(solution)/shard_map/pallas_call | solution.py:497
  63.0 3.3 %all-to-all-start = ((f32[32,1,64]{2,1,0:T(1,128)}), f32[32,1,64]{2,1,0:T(1,128)S(1)}, u32[]{:S(2)}, u32[]{:S(2)}) async-start(f32[32,1,64]{2,1,0:T(1,128)} %shard_map.65), calls=%async_computation | async-start | bytes 32768 | tf_op jit(solution)/shard_map/all_to_all | solution.py:661
  66.3 4.4 %spell.1 = f32[640,2048]{1,0:T(8,128)} custom-call(s32[32,2048]{1,0:T(8,128)S(1)} %get-tuple-element.19.spins_ref, s32[2,32,256]{2,1,0:T(8,128)S(1)} %get-tuple-element.23.sides_ref), custom_call_target="tpu_custom_call" | custom-call | flops 1310720 | bytes 5242880 | tf_op jit(solution)/shard_map/spell/pallas_call | solution.py:609
  70.7 2.8 %all-to-all-done = f32[32,1,64]{2,1,0:T(1,128)S(1)} async-done(((f32[32,1,64]{2,1,0:T(1,128)}), f32[32,1,64]{2,1,0:T(1,128)S(1)}, u32[]{:S(2)}, u32[]{:S(2)}) %all-to-all-start) | async-done | bytes 8224 | tf_op jit(solution)/shard_map/all_to_all | solution.py:661
  73.5 0.6 reduce_sum.9
  (7 shorter events, 0.0 us)
Async XLA Ops:
  8.1 7.4 %collective-permute-start = (bf16[32,2048]{1,0:T(8,128)(2,1)S(1)}, bf16[32,2048]{1,0:T(8,128)(2,1)S(1)}, u32[]{:S(2)}, u32[]{:S(2)}) collective-permute-start(bf16[32,2048]{1,0:T(8,128)(2,1)S(1)} %get-tuple-element.17), channel_id=1, source_target_pairs={{0,4},{4,8},{8,12},{12,16},{16,20},{20,24},{24,28},{28,0},{1,5},{5... | collective-permute-start | bytes 393224 | tf_op jit(solution)/shard_map/ppermute | solution.py:534
  8.7 6.8 %collective-permute-start.1 = (bf16[32,2048]{1,0:T(8,128)(2,1)S(1)}, bf16[32,2048]{1,0:T(8,128)(2,1)S(1)}, u32[]{:S(2)}, u32[]{:S(2)}) collective-permute-start(bf16[32,2048]{1,0:T(8,128)(2,1)S(1)} %get-tuple-element.18), channel_id=1, source_target_pairs={{0,28},{4,0},{8,4},{12,8},{16,12},{20,16},{24,20},{28,24},{1,29},{... | collective-permute-start | bytes 393224 | tf_op jit(solution)/shard_map/ppermute | solution.py:535
  18.0 33.5 %collective-permute-start.4 = (bf16[6,128,256]{2,1,0:T(8,128)(2,1)S(1)}, bf16[6,128,256]{2,1,0:T(8,128)(2,1)S(1)}, u32[]{:S(2)}, u32[]{:S(2)}) collective-permute-start(bf16[6,128,256]{2,1,0:T(8,128)(2,1)S(1)} %get-tuple-element.27.refs_0_), channel_id=1, source_target_pairs={{0,1},{1,0},{2,3},{3,2},{4,5},{5,4},{6,7},{7,6},{8,9},{9,8},{10,11... | collective-permute-start | bytes 1179656 | tf_op jit(solution)/shard_map/ppermute | solution.py:494
  20.0 36.9 %collective-permute-start.5 = (bf16[6,192,256]{2,1,0:T(8,128)(2,1)S(1)}, bf16[6,192,256]{2,1,0:T(8,128)(2,1)S(1)}, u32[]{:S(2)}, u32[]{:S(2)}) collective-permute-start(bf16[6,192,256]{2,1,0:T(8,128)(2,1)S(1)} %get-tuple-element.28.refs_1_), channel_id=1, source_target_pairs={{0,1},{1,0},{2,3},{3,2},{4,5},{5,4},{6,7},{7,6},{8,9},{9,8},{10,11... | collective-permute-start | bytes 1769480 | tf_op jit(solution)/shard_map/ppermute | solution.py:494
  20.1 36.8 %collective-permute-start.8 = (bf16[6,192,256]{2,1,0:T(8,128)(2,1)S(1)}, bf16[6,192,256]{2,1,0:T(8,128)(2,1)S(1)}, u32[]{:S(2)}, u32[]{:S(2)}) collective-permute-start(bf16[6,192,256]{2,1,0:T(8,128)(2,1)S(1)} %get-tuple-element.25.refs_4_.refs_1_), channel_id=1, source_target_pairs={{0,2},{1,3},{2,0},{3,1},{4,6},{5,7},{6,4},{7,5},{8,10},{9,11},{10,... | collective-permute-start | bytes 1769480 | tf_op jit(solution)/shard_map/ppermute | solution.py:494
  22.1 34.8 %collective-permute-start.7 = (bf16[6,128,256]{2,1,0:T(8,128)(2,1)S(1)}, bf16[6,128,256]{2,1,0:T(8,128)(2,1)S(1)}, u32[]{:S(2)}, u32[]{:S(2)}) collective-permute-start(bf16[6,128,256]{2,1,0:T(8,128)(2,1)S(1)} %get-tuple-element.24.refs_3_.refs_0_), channel_id=1, source_target_pairs={{0,2},{1,3},{2,0},{3,1},{4,6},{5,7},{6,4},{7,5},{8,10},{9,11},{10,... | collective-permute-start | bytes 1179656 | tf_op jit(solution)/shard_map/ppermute | solution.py:494
  22.2 22.5 %collective-permute-start.2 = (bf16[96,128]{1,0:T(8,128)(2,1)S(1)}, bf16[96,128]{1,0:T(8,128)(2,1)S(1)}, u32[]{:S(2)}, u32[]{:S(2)}) collective-permute-start(bf16[96,128]{1,0:T(8,128)(2,1)S(1)} %get-tuple-element.21), channel_id=1, source_target_pairs={{0,1},{1,2},{2,3},{3,0},{4,5},{5,6},{6,7},{7,4},{8,9},{9,10},{10,1... | collective-permute-start | bytes 73736 | tf_op jit(solution)/shard_map/ppermute | solution.py:586
  44.6 3.8 %collective-permute-start.3 = (bf16[96,128]{1,0:T(8,128)(2,1)S(1)}, bf16[96,128]{1,0:T(8,128)(2,1)S(1)}, u32[]{:S(2)}, u32[]{:S(2)}) collective-permute-start(bf16[96,128]{1,0:T(8,128)(2,1)S(1)} %get-tuple-element.22), channel_id=1, source_target_pairs={{0,3},{1,0},{2,1},{3,2},{4,7},{5,4},{6,5},{7,6},{8,11},{9,8},{10,9... | collective-permute-start | bytes 73736 | tf_op jit(solution)/shard_map/ppermute | solution.py:587
  50.1 9.7 %collective-permute-start.6 = (bf16[2,320,256]{2,1,0:T(8,128)(2,1)S(1)}, bf16[2,320,256]{2,1,0:T(8,128)(2,1)S(1)}, u32[]{:S(2)}, u32[]{:S(2)}) collective-permute-start(bf16[2,320,256]{2,1,0:T(8,128)(2,1)S(1)} %get-tuple-element.29.refs_2_), channel_id=1, source_target_pairs={{0,1},{1,0},{2,3},{3,2},{4,5},{5,4},{6,7},{7,6},{8,9},{9,8},{10,11... | collective-permute-start | bytes 983048 | tf_op jit(solution)/shard_map/ppermute | solution.py:494
  51.5 8.4 %collective-permute-start.9 = (bf16[2,320,256]{2,1,0:T(8,128)(2,1)S(1)}, bf16[2,320,256]{2,1,0:T(8,128)(2,1)S(1)}, u32[]{:S(2)}, u32[]{:S(2)}) collective-permute-start(bf16[2,320,256]{2,1,0:T(8,128)(2,1)S(1)} %get-tuple-element.26.refs_5_.refs_2_), channel_id=1, source_target_pairs={{0,2},{1,3},{2,0},{3,1},{4,6},{5,7},{6,4},{7,5},{8,10},{9,11},{10,... | collective-permute-start | bytes 983048 | tf_op jit(solution)/shard_map/ppermute | solution.py:494
  63.0 10.5 %all-to-all-start = ((f32[32,1,64]{2,1,0:T(1,128)}), f32[32,1,64]{2,1,0:T(1,128)S(1)}, u32[]{:S(2)}, u32[]{:S(2)}) async-start(f32[32,1,64]{2,1,0:T(1,128)} %shard_map.65), calls=%async_computation | async-start | bytes 32768 | tf_op jit(solution)/shard_map/all_to_all | solution.py:661

commit v5 on v4

--- a/solution.py
+++ b/solution.py
@@ -14,7 +14,7 @@
 LANES = 128
 TILE = 256
 PER_STEP = 2
-MIDDLE = 6
+MIDDLE = 4
 WORDS = 1 + 2 * SWEEPS
 
 
@@ -115,15 +115,28 @@
     return jnp.where(up, 1.0, -1.0).astype(jnp.bfloat16) * moments
 
 
+def select(odd, when_odd, when_even):
+    return jnp.where(odd == 1, when_odd, when_even)
+
+
+def fill(refs, odd, planes_of, moments_of, spins_of):
+    for ref, lower in zip(refs, (1 - odd, odd)):
+        for i, plane in enumerate(planes_of(lower)):
+            for t in range(ref.shape[0]):
+                ref[t, i * DEPTH : (i + 1) * DEPTH, :] = weigh(
+                    spins_of(t), moments_of(lower, i, t), plane
+                )
+
+
 def middle_kernel(
     odd_ref,
-    bar_ref,
+    bar_hbm,
     spins_hbm,
     draws_hbm,
     moments_hbm,
     words_ref,
-    last_ref,
-    first_ref,
+    beside_ref,
+    across_ref,
     given_ref,
     kept_ref,
     spins_buf,
@@ -132,7 +145,7 @@
     edge_draws,
     moments_buf,
     final_ref,
-    bar_smem,
+    bar_ref,
     sems,
     edge_sems,
 ):
@@ -142,10 +155,21 @@
     top = planes[0] * DEPTH
     groups = groups_of(planes, PER_STEP)
     size = PER_STEP * DEPTH
-    edges = [
-        fetch(s, spins_hbm, draws_hbm, edge_spins, edge_draws, edge_sems, row, 8 * s, 8)
-        for s, row in enumerate((rows - 8, 0))
-    ]
+    bars = pltpu.make_async_copy(bar_hbm, bar_ref, edge_sems.at[4, 1])
+    edges = []
+    for e, (at, row) in enumerate(
+        (at, row) for at in (0, columns - LANES) for row in (0, rows - top)
+    ):
+        source = (pl.ds(row, top), pl.ds(at, LANES))
+        edges.append(
+            pltpu.make_async_copy(spins_hbm.at[source], edge_spins.at[e], edge_sems.at[e, 0])
+        )
+        for k in range(SWEEPS):
+            edges.append(
+                pltpu.make_async_copy(
+                    draws_hbm.at[(k, *source)], edge_draws.at[k, e], edge_sems.at[e, 1 + k]
+                )
+            )
     copies = [
         fetch(
             g,
@@ -163,57 +187,86 @@
     weights = pltpu.make_async_copy(
         moments_hbm.at[pl.ds((half - MIDDLE) * DEPTH, 2 * MIDDLE * DEPTH)],
         moments_buf,
-        edge_sems.at[2, 0],
-    )
-    bars = pltpu.make_async_copy(bar_ref, bar_smem, edge_sems.at[2, 1])
-    for copy in [bars] + sum(edges + copies, []) + [weights]:
+        edge_sems.at[4, 0],
+    )
+    for copy in [bars] + edges + sum(copies, []) + [weights]:
         copy.start()
     bars.wait()
-    bar_ref = bar_smem
-    for s, ref in enumerate((last_ref, first_ref)):
-        for copy in edges[s]:
-            copy.wait()
-        parts = [edge_spins[8 * s : 8 * s + 8, :]]
-        for k in range(SWEEPS):
-            draw = edge_draws[k, 8 * s : 8 * s + 8, :]
-            one = (draw < bar_ref[0]).astype(jnp.int32)
-            parts.append(one + 2 * (draw < bar_ref[1]).astype(jnp.int32))
-        ref[...] = strips(parts + [jnp.zeros_like(parts[0])])
+    for copy in edges:
+        copy.wait()
+    side_words = []
+    for e in range(4):
+        if e % 2 == 0:
+            side_words.append([jnp.zeros((DEPTH, LANES), jnp.int32)] * WORDS)
+        words = side_words[-1]
+        for i in range(top // DEPTH):
+            plane = i + (e % 2) * (rows - top) // DEPTH
+            at = pl.ds(i * DEPTH, DEPTH)
+            words[0] = words[0] | (edge_spins[e, at, :] << (plane + 1))
+            for k in range(SWEEPS):
+                draw = edge_draws[k, e, at, :]
+                for c in range(2):
+                    word = words[1 + 2 * k + c]
+                    words[1 + 2 * k + c] = jnp.where(
+                        draw < bar_ref[c], word | (1 << (plane + 1)), word
+                    )
     for g, group in enumerate(groups):
         for copy in copies[g]:
             copy.wait()
         pack(bar_ref, words_ref, spins_buf, draws_buf, group, g * size, g == 0)
+    lane = lax.broadcasted_iota(jnp.int32, (DEPTH, LANES), 1)
+    codes_of = []
+    for at, held, outer in (
+        (0, lane < 4, side_words[0]),
+        (columns - LANES, lane >= LANES - 4, side_words[1]),
+    ):
+        bits = []
+        for w in range(WORDS):
+            edge = jnp.where(held, words_ref[w, :, at : at + LANES] | outer[w], 0)
+            bits.append((spread(edge) >> (lane // 4)) & 1)
+        codes_of.append(jnp.concatenate(codes(bits), axis=0).astype(jnp.float32))
+    odd = odd_ref[0]
+    beside_ref[...] = select(odd, codes_of[0], codes_of[1]).astype(jnp.bfloat16)
+    across_ref[...] = select(odd, codes_of[1], codes_of[0]).astype(jnp.bfloat16)
     inner = slice(LANES, columns - LANES)
     final_ref[:, inner] = sweeps_of([words_ref[w, :, inner] for w in range(WORDS)])
     weights.wait()
-    for ref, lower in ((given_ref, 1 - odd_ref[0]), (kept_ref, odd_ref[0])):
-        for i in range(MIDDLE):
-            plane = half - MIDDLE + MIDDLE * lower + i
-            at = pl.ds(pl.multiple_of((MIDDLE * lower + i) * DEPTH, DEPTH), DEPTH)
-            for t in range(ref.shape[0]):
-                lanes = pl.ds((t + 1) * TILE, TILE)
-                ref[t, i * DEPTH : (i + 1) * DEPTH, :] = weigh(
-                    final_ref[:, lanes], moments_buf[at, lanes], plane
-                )
+    fill(
+        (given_ref, kept_ref),
+        odd,
+        lambda lower: [half - MIDDLE + MIDDLE * lower + i for i in range(MIDDLE)],
+        lambda lower, i, t: moments_buf[
+            pl.ds(pl.multiple_of((MIDDLE * lower + i) * DEPTH, DEPTH), DEPTH),
+            pl.ds((t + 1) * TILE, TILE),
+        ],
+        lambda t: final_ref[:, pl.ds((t + 1) * TILE, TILE)],
+    )
 
 
 def outer_kernel(
-    bar_ref,
+    odd_ref,
+    bar_hbm,
     spins_hbm,
     draws_hbm,
+    moments_hbm,
     middle_ref,
     words_ref,
+    given_ref,
+    kept_ref,
     spins_buf,
     draws_buf,
-    bar_smem,
+    moments_buf,
+    final_ref,
+    bar_ref,
     sems,
-    bar_sem,
+    more_sems,
 ):
-    bars = pltpu.make_async_copy(bar_ref, bar_smem, bar_sem)
-    bars.start()
-    planes = spins_hbm.shape[0] // DEPTH
+    rows, columns = spins_hbm.shape
+    planes = rows // DEPTH
     side = planes // 2 - MIDDLE - 1
     outer = list(range(side)) + list(range(planes - side, planes))
+    bars = pltpu.make_async_copy(bar_hbm, bar_ref, more_sems.at[2])
+    bars.start()
     copies = []
     for g, plane in enumerate(outer):
         copies.append(
@@ -231,142 +284,131 @@
         )
         for copy in copies[-1]:
             copy.start()
+    weights = [
+        pltpu.make_async_copy(
+            moments_hbm.at[pl.ds(row, side * DEPTH)], moments_buf.at[s], more_sems.at[s]
+        )
+        for s, row in enumerate((DEPTH, rows - (side + 1) * DEPTH))
+    ]
+    for copy in weights:
+        copy.start()
     words_ref[...] = middle_ref[...]
     bars.wait()
-    bar_ref = bar_smem
     for g in range(0, len(outer), PER_STEP):
         group = outer[g : g + PER_STEP]
         for copy in sum(copies[g : g + PER_STEP], []):
             copy.wait()
         pack(bar_ref, words_ref, spins_buf, draws_buf, group, g * DEPTH, False)
-
-
-def inner_kernel(
+    inner = slice(LANES, columns - LANES)
+    final_ref[:, inner] = sweeps_of([words_ref[w, :, inner] for w in range(WORDS)])
+    for copy in weights:
+        copy.wait()
+    fill(
+        (given_ref, kept_ref),
+        odd_ref[0],
+        lambda lower: [1 + i + (planes - side - 2) * lower for i in range(side)],
+        lambda lower, i, t: moments_buf[
+            lower, i * DEPTH : (i + 1) * DEPTH, pl.ds((t + 1) * TILE, TILE)
+        ],
+        lambda t: final_ref[:, pl.ds((t + 1) * TILE, TILE)],
+    )
+
+
+def widen_kernel(odd_ref, words_ref, beside_ref, across_ref, wide_ref, last_ref, first_ref, *, planes):
+    columns = words_ref.shape[2]
+    odd = odd_ref[0]
+    lane = lax.broadcasted_iota(jnp.int32, (DEPTH, LANES), 1)
+    beside, across = unstrips(beside_ref, DEPTH), unstrips(across_ref, DEPTH)
+    for w in range(WORDS):
+        wide_ref[w, :, LANES : LANES + columns] = words_ref[w]
+        before = select(odd, beside[w], across[w])
+        after = select(odd, across[w], beside[w])
+        wide_ref[w, :, :LANES] = spread(before << (lane // 4))
+        wide_ref[w, :, LANES + columns :] = spread(after << (lane // 4))
+    for ref, top, place in ((last_ref, DEPTH - 8, planes), (first_ref, 0, 1)):
+        bits = [(wide_ref[w, top : top + 8, :] >> place) & 1 for w in range(WORDS)]
+        ref[...] = strips(codes(bits) + [jnp.zeros_like(bits[0])])
+
+
+def side_kernel(
     odd_ref,
-    words_ref,
+    wide_ref,
     above_ref,
     below_ref,
     moments_hbm,
     spins_ref,
-    sides_ref,
-    right_ref,
-    left_ref,
     given_ref,
     kept_ref,
     joined_ref,
-    moments_buf,
+    tile_moments,
+    row_moments,
+    final_ref,
     sems,
 ):
     rows, columns = moments_hbm.shape
     planes = rows // DEPTH
-    side = planes // 2 - MIDDLE
+    half = planes // 2
+    side = half - MIDDLE
     weights = [
         pltpu.make_async_copy(
-            moments_hbm.at[pl.ds(row, side * DEPTH)], moments_buf.at[s], sems.at[s]
-        )
-        for s, row in enumerate((0, rows - side * DEPTH))
+            moments_hbm.at[:, pl.ds(at, TILE)], tile_moments.at[s], sems.at[s]
+        )
+        for s, at in enumerate((0, columns - TILE))
+    ] + [
+        pltpu.make_async_copy(
+            moments_hbm.at[pl.ds(at, DEPTH)], row_moments.at[s], sems.at[2 + s]
+        )
+        for s, at in enumerate((0, rows - DEPTH))
     ]
     for copy in weights:
         copy.start()
     above, below = unstrips(above_ref, 8), unstrips(below_ref, 8)
-    joined_ref[...] = words_ref[...]
+    joined_ref[...] = wide_ref[...]
     for w in range(WORDS):
-        joined_ref[w, DEPTH - 8 :, :] = words_ref[w, DEPTH - 8 :, :] | above[w]
-        joined_ref[w, :8, :] = words_ref[w, :8, :] | (below[w] << (planes + 1))
-    lane = lax.broadcasted_iota(jnp.int32, (DEPTH, LANES), 1)
-    for ref, at, held in (
-        (right_ref, columns - LANES, lane >= LANES - 4),
-        (left_ref, 0, lane < 4),
-    ):
-        bits = []
-        for w in range(WORDS):
-            edge = jnp.where(held, joined_ref[w, :, at : at + LANES], 0)
-            bits.append((spread(edge) >> (lane // 4)) & 1)
-        ref[...] = strips(codes(bits))
-    reach = TILE + LANES
-    sides_ref[:, :, :reach] = joined_ref[:, :, :reach]
-    sides_ref[:, :, reach:] = joined_ref[:, :, columns - reach :]
-    inner = slice(LANES, columns - LANES)
-    spins_ref[:, :LANES] = jnp.zeros((DEPTH, LANES), jnp.int32)
-    spins_ref[:, columns - LANES :] = jnp.zeros((DEPTH, LANES), jnp.int32)
-    spins_ref[:, inner] = sweeps_of([joined_ref[w, :, inner] for w in range(WORDS)])
+        joined_ref[w, DEPTH - 8 :, :] = wide_ref[w, DEPTH - 8 :, :] | above[w]
+        joined_ref[w, :8, :] = wide_ref[w, :8, :] | (below[w] << (planes + 1))
+    final_ref[...] = sweeps_of([joined_ref[w] for w in range(WORDS)])
+    spins_ref[...] = final_ref[:, LANES : LANES + columns]
     for copy in weights:
         copy.wait()
-    for ref, lower in ((given_ref, 1 - odd_ref[0]), (kept_ref, odd_ref[0])):
-        for i in range(side):
-            plane = (planes - side) * lower + i
-            for t in range(ref.shape[0]):
-                lanes = pl.ds((t + 1) * TILE, TILE)
-                ref[t, i * DEPTH : (i + 1) * DEPTH, :] = weigh(
-                    spins_ref[:, lanes],
-                    moments_buf[lower, i * DEPTH : (i + 1) * DEPTH, lanes],
-                    plane,
+    odd = odd_ref[0]
+    ends = (0, columns - TILE)
+    for ref, lower in ((given_ref, 1 - odd), (kept_ref, odd)):
+        for i in range(half):
+            if i < side - 1:
+                plane = 1 + i + (planes - side - 1) * lower
+            elif i < half - 1:
+                plane = 1 + i + MIDDLE * lower
+            else:
+                plane = (planes - 1) * lower
+            at = pl.ds(pl.multiple_of(plane * DEPTH, DEPTH), DEPTH)
+            for s, left in enumerate(ends):
+                row = (s * half + i) * DEPTH
+                ref[row : row + DEPTH, :] = weigh(
+                    final_ref[:, LANES + left : LANES + left + TILE], tile_moments[s, at, :], plane
                 )
-
-
-def side_kernel(
-    odd_ref,
-    sides_ref,
-    before_ref,
-    after_ref,
-    moments_hbm,
-    spins_ref,
-    given_ref,
-    kept_ref,
-    moments_buf,
-    final_ref,
-    sems,
-):
-    rows, columns = moments_hbm.shape
-    half = rows // DEPTH // 2
-    weights = [
-        pltpu.make_async_copy(
-            moments_hbm.at[:, pl.ds(at, TILE)], moments_buf.at[s], sems.at[s]
-        )
-        for s, at in enumerate((0, columns - TILE))
-    ]
-    for copy in weights:
-        copy.start()
-    lane = lax.broadcasted_iota(jnp.int32, (DEPTH, LANES), 1)
-    before, after = unstrips(before_ref, DEPTH), unstrips(after_ref, DEPTH)
-    words = [
-        jnp.concatenate(
-            [spread(before[w] << (lane // 4)), sides_ref[w], spread(after[w] << (lane // 4))],
-            axis=1,
-        )
-        for w in range(WORDS)
-    ]
-    updated = sweeps_of(words)
-    width = updated.shape[1]
-    final_ref[0] = updated[:, LANES : LANES + TILE]
-    final_ref[1] = updated[:, width - LANES - TILE : width - LANES]
-    spins_ref[...] = final_ref[...]
-    for copy in weights:
-        copy.wait()
-    for ref, lower in ((given_ref, 1 - odd_ref[0]), (kept_ref, odd_ref[0])):
-        for i in range(half):
-            plane = i + lower * (half + MIDDLE if i < half - MIDDLE else MIDDLE)
-            at = pl.ds(pl.multiple_of(plane * DEPTH, DEPTH), DEPTH)
-            for s in range(2):
-                ref[s, i * DEPTH : (i + 1) * DEPTH, :] = weigh(
-                    final_ref[s], moments_buf[s, at, :], plane
-                )
-
-
-def spell_kernel(spins_ref, sides_ref, out_ref):
-    columns = out_ref.shape[1]
-    first = pl.program_id(0) * PER_STEP + 1
-    for plane in range(PER_STEP):
-        bit = jnp.int32(1) << (first + plane)
+        for t in range(1, columns // TILE - 1):
+            row = (2 * half + t - 1) * DEPTH
+            ref[row : row + DEPTH, :] = weigh(
+                final_ref[:, LANES + t * TILE : LANES + (t + 1) * TILE],
+                row_moments[lower, :, t * TILE : (t + 1) * TILE],
+                (planes - 1) * lower,
+            )
+
+
+def spell_kernel(spins_ref, out_hbm, out_buf, sems):
+    columns = spins_ref.shape[1]
+    copies = []
+    for plane in range(out_hbm.shape[0] // DEPTH):
         rows = pl.ds(plane * DEPTH, DEPTH)
         for left in range(0, columns, TILE):
-            if left == 0:
-                word = sides_ref[0]
-            elif left == columns - TILE:
-                word = sides_ref[1]
-            else:
-                word = spins_ref[:, left : left + TILE]
-            out_ref[rows, left : left + TILE] = jnp.where((word & bit) != 0, 1.0, -1.0)
+            lanes = pl.ds(left, TILE)
+            up = (spins_ref[:, lanes] & (1 << (plane + 1))) != 0
+            out_buf[rows, lanes] = jnp.where(up, 1.0, -1.0)
+        copies.append(pltpu.make_async_copy(out_buf.at[rows], out_hbm.at[rows], sems.at[plane]))
+        copies[-1].start()
+    for copy in copies:
+        copy.wait()
 
 
 def gram(left, right):
@@ -391,12 +433,18 @@
     return value
 
 
+def edge_rows(ends, tiles, first, last):
+    start = ends.shape[0] - (tiles - 2) * DEPTH
+    return ends[start + (first - 1) * DEPTH : start + (last - 1) * DEPTH, :]
+
+
 def tile(block, t):
     low, high, ends = block
-    last = low.shape[0] + 1
-    if t in (0, last):
-        return ends[min(t, 1)]
-    return stack([low, high], t - 1, t)
+    tiles = low.shape[0] + 2
+    height = low.shape[1] + high.shape[1] + DEPTH
+    if t in (0, tiles - 1):
+        return ends[min(t, 1) * height : (min(t, 1) + 1) * height, :]
+    return jnp.concatenate([low[t - 1], high[t - 1], edge_rows(ends, tiles, t, t + 1)], axis=0)
 
 
 def tiles_of(block, places):
@@ -449,8 +497,20 @@
     def run(pairs):
         for n in range(1, tiles + 1):
             places = [(tiles - 1, n - 1)] + ([(tiles - n, 0)] if n > 1 else [])
+            inner = n > 2
             sums_ref[:, n * TILE : (n + 1) * TILE] = sum(
-                gram(tiles_of(left, [t for t, _ in places]), tiles_of(right, [q for _, q in places]))
+                gram(
+                    jnp.concatenate(
+                        [tile(left, t) for t, _ in places]
+                        + ([edge_rows(left[2], tiles, tiles + 1 - n, tiles - 1)] if inner else []),
+                        axis=0,
+                    ),
+                    jnp.concatenate(
+                        [tile(right, q) for _, q in places]
+                        + ([edge_rows(right[2], tiles, 1, n - 1)] if inner else []),
+                        axis=0,
+                    ),
+                )
                 for left, right in pairs
             )
 
@@ -474,7 +534,6 @@
     vmem = pl.BlockSpec(memory_space=pltpu.VMEM)
     smem = pl.BlockSpec(memory_space=pltpu.SMEM)
     anywhere = pl.BlockSpec(memory_space=pltpu.HBM)
-    strip = jax.ShapeDtypeStruct((8 * (2 + SWEEPS), columns), jnp.bfloat16)
     edge = jax.ShapeDtypeStruct((DEPTH * (1 + SWEEPS), LANES), jnp.bfloat16)
     words_shape = jax.ShapeDtypeStruct((WORDS, DEPTH, columns), jnp.int32)
     dma = pltpu.SemaphoreType.DMA
@@ -505,21 +564,25 @@
         )(*operands)
 
     packed = (2 * MIDDLE + 2) * DEPTH
+    remaining = rows - packed
+    side = half - MIDDLE - 1
     middle = message(tiles - 2, MIDDLE * DEPTH)
-    words, last, leading, given, kept = call(
+    across_pairs = [(i, (i - 1 + 2 * (i % 2)) % col_devices) for i in range(col_devices)]
+    beside_pairs = [(i, i ^ 1) for i in range(col_devices)]
+    words, beside, across, given, kept = call(
         middle_kernel,
         [smem, anywhere, anywhere, anywhere, anywhere],
-        [words_shape, strip, strip, middle, middle],
+        [words_shape, edge, edge, middle, middle],
         [
             pltpu.VMEM((packed, columns), jnp.int32),
             pltpu.VMEM((SWEEPS, packed, columns), jnp.float32),
-            pltpu.VMEM((16, columns), jnp.int32),
-            pltpu.VMEM((SWEEPS, 16, columns), jnp.float32),
+            pltpu.VMEM((4, remaining // 2, LANES), jnp.int32),
+            pltpu.VMEM((SWEEPS, 4, remaining // 2, LANES), jnp.float32),
             pltpu.VMEM((2 * MIDDLE * DEPTH, columns), jnp.bfloat16),
             pltpu.VMEM((DEPTH, columns), jnp.int32),
             pltpu.SMEM((2,), jnp.float32),
             dma((pl.cdiv(2 * MIDDLE + 2, PER_STEP), 1 + SWEEPS)),
-            dma((3, 1 + SWEEPS)),
+            dma((5, 1 + SWEEPS)),
         ],
         40 * packed * columns,
         4 * (1 + SWEEPS) * packed * columns,
@@ -531,96 +594,85 @@
     )
     own = [given, kept]
     got = [*exchange(given, kept)]
-    above = lax.ppermute(last, "row", ring(row_devices, 1))
-    below = lax.ppermute(leading, "row", ring(row_devices, -1))
-
-    remaining = rows - packed
-    words = call(
+    beside = lax.ppermute(beside, "col", beside_pairs)
+    across = lax.ppermute(across, "col", across_pairs)
+    low = message(tiles - 2, side * DEPTH)
+    words, given, kept = call(
         outer_kernel,
-        [anywhere, anywhere, anywhere, vmem],
-        words_shape,
+        [smem, anywhere, anywhere, anywhere, anywhere, vmem],
+        [words_shape, low, low],
         [
             pltpu.VMEM((remaining, columns), jnp.int32),
             pltpu.VMEM((SWEEPS, remaining, columns), jnp.float32),
+            pltpu.VMEM((2, side * DEPTH, columns), jnp.bfloat16),
+            pltpu.VMEM((DEPTH, columns), jnp.int32),
             pltpu.SMEM((2,), jnp.float32),
             dma((remaining // DEPTH, 1 + SWEEPS)),
-            dma(()),
+            dma((3,)),
         ],
         40 * remaining * columns,
         4 * (1 + SWEEPS) * remaining * columns,
+        odd,
         accept_bar,
         spins_up,
         uniforms,
+        moments,
         words,
     )
-    side = half - MIDDLE
-    low = message(tiles - 2, side * DEPTH)
-    reach = 2 * (TILE + LANES)
-    spins, sides, right, left, given, kept = call(
-        inner_kernel,
+    own = [given, own[0], kept, own[1]]
+    mid, far = exchange(given, kept)
+    got = [mid, got[0], far, got[1]]
+    wide_shape = jax.ShapeDtypeStruct((WORDS, DEPTH, columns + 2 * LANES), jnp.int32)
+    strip = jax.ShapeDtypeStruct((8 * (2 + SWEEPS), columns + 2 * LANES), jnp.bfloat16)
+    words, last, leading = call(
+        functools.partial(widen_kernel, planes=planes),
+        [smem, vmem, vmem, vmem],
+        [wide_shape, strip, strip],
+        [],
+        20 * DEPTH * columns,
+        40 * DEPTH * columns,
+        odd,
+        words,
+        beside,
+        across,
+    )
+    above = lax.ppermute(last, "row", ring(row_devices, 1))
+    below = lax.ppermute(leading, "row", ring(row_devices, -1))
+    ends = jax.ShapeDtypeStruct((2 * half_rows + (tiles - 2) * DEPTH, TILE), jnp.bfloat16)
+    spins, given, kept = call(
+        side_kernel,
         [smem, vmem, vmem, vmem, anywhere],
+        [jax.ShapeDtypeStruct((DEPTH, columns), jnp.int32), ends, ends],
         [
-            jax.ShapeDtypeStruct((DEPTH, columns), jnp.int32),
-            jax.ShapeDtypeStruct((WORDS, DEPTH, reach), jnp.int32),
-            edge,
-            edge,
-            low,
-            low,
+            pltpu.VMEM(wide_shape.shape, jnp.int32),
+            pltpu.VMEM((2, rows, TILE), jnp.bfloat16),
+            pltpu.VMEM((2, DEPTH, columns), jnp.bfloat16),
+            pltpu.VMEM(wide_shape.shape[1:], jnp.int32),
+            dma((4,)),
         ],
-        [
-            pltpu.VMEM(words_shape.shape, jnp.int32),
-            pltpu.VMEM((2, side * DEPTH, columns), jnp.bfloat16),
-            dma((2,)),
-        ],
-        40 * rows * columns,
-        4 * rows * columns,
+        10 * rows * columns,
+        rows * columns,
         odd,
         words,
         above,
         below,
         moments,
     )
-    own = [given, own[0], kept, own[1]]
-    mid, far = exchange(given, kept)
-    got = [mid, got[0], far, got[1]]
-    before = lax.ppermute(right, "col", ring(col_devices, 1))
-    after = lax.ppermute(left, "col", ring(col_devices, -1))
-    ends = message(2, half_rows)
-    side_spins, given, kept = call(
-        side_kernel,
-        [smem, vmem, vmem, vmem, anywhere],
-        [jax.ShapeDtypeStruct((2, DEPTH, TILE), jnp.int32), ends, ends],
-        [
-            pltpu.VMEM((2, rows, TILE), jnp.bfloat16),
-            pltpu.VMEM((2, DEPTH, TILE), jnp.int32),
-            dma((2,)),
-        ],
-        10 * rows * columns,
-        rows * columns,
-        odd,
-        sides,
-        before,
-        after,
-        moments,
-    )
     own = [own[0], own[1], given, own[2], own[3], kept]
     mid, far = exchange(given, kept)
 
     spins_out = pl.pallas_call(
         spell_kernel,
-        grid=(rows // (PER_STEP * DEPTH),),
-        in_specs=[
-            pl.BlockSpec((DEPTH, columns), lambda i: (0, 0)),
-            pl.BlockSpec((2, DEPTH, TILE), lambda i: (0, 0, 0)),
-        ],
-        out_specs=pl.BlockSpec((PER_STEP * DEPTH, columns), lambda i: (i, 0)),
+        in_specs=[vmem],
+        out_specs=anywhere,
         out_shape=jax.ShapeDtypeStruct((rows, columns), jnp.float32),
+        scratch_shapes=[pltpu.VMEM((rows, columns), jnp.float32), dma((planes,))],
         compiler_params=params(),
         cost_estimate=pl.CostEstimate(
             flops=rows * columns, bytes_accessed=4 * rows * columns, transcendentals=0
         ),
         name="spell",
-    )(spins, side_spins)
+    )(spins)
     normaliser = 1.0 / math.sqrt(rows * row_devices * columns * col_devices)
     sums = pltpu.VMEM((TILE, R + TILE), jnp.float32)
     folded = jax.ShapeDtypeStruct((8, R + LANES), jnp.float32)

time: 74.3 us -> 69.6 us (0.937)
  Pallas kernels: 28.6 us -> 26.2 us
  starting transfers between devices: 18.3 us -> 17.1 us
  waiting for transfers between devices: 25.9 us -> 24.9 us
    ppermute x2, waiting for transfers between devices: 23 us -> 3.11 us  [the longest x1 1.65 us: on_device(): beside = lax.ppermute(beside, 'col', beside_pairs)]
    ppermute x3, waiting for transfers between devices: 0.18 us -> 14.8 us  [exchange(): lax.ppermute(kept, 'col', beyond)]
    pallas_call x1, Pallas kernels: 4.44 us -> 2.52 us  [on_device(): pl.pallas_call(spell_kernel, in_specs=[vmem], out_specs=anywhere, out_sha...]
    all_to_all x1, waiting for transfers between devices: 2.76 us -> 4.64 us  [on_device(): shares = lax.all_to_all(partial_sums, ('row', 'col'), 0, 0, tiled=True)]
    ppermute x3, starting transfers between devices: 3.49 us -> 5.36 us  [exchange(): lax.ppermute(given, 'col', beside)]
    ppermute x1, waiting for transfers between devices: 0.01 us -> 1.39 us  [on_device(): above = lax.ppermute(last, 'row', ring(row_devices, 1))]
    ppermute x1, starting transfers between devices: 4.09 us -> 2.91 us  [on_device(): below = lax.ppermute(leading, 'row', ring(row_devices, -1))]
    ppermute x3, starting transfers between devices: 3.55 us -> 2.42 us  [exchange(): lax.ppermute(kept, 'col', beyond)]
  transfers between devices with their start and end apart: 11 -> 11, of which waited for: 4 -> 7; matrix products, arithmetic and copies ran while one was open for 0% -> 0% of each run, Pallas kernels for 21% -> 23%
where the time goes in v5:
time: 69.6 us; the launch traced here: 69.4 us
  Pallas kernels  26.2 us (38%)
  waiting for transfers between devices  24.9 us (36%)
  starting transfers between devices  17.1 us (25%)
  between operations  0.71 us (1%)
    pallas_call x7, Pallas kernels, call(): pl.pallas_call(kernel, in_specs=specs, out_specs=jax.tree.map(lambda _: v...  23.7 us
    ppermute x3, waiting for transfers between devices, exchange(): lax.ppermute(kept, 'col', beyond)  14.8 us
    ppermute x3, starting transfers between devices, exchange(): lax.ppermute(given, 'col', beside)  5.36 us
    all_to_all x1, waiting for transfers between devices, on_device(): shares = lax.all_to_all(partial_sums, ('row', 'col'), 0, 0, tiled=True)  4.64 us
    all_to_all x1, starting transfers between devices, on_device(): shares = lax.all_to_all(partial_sums, ('row', 'col'), 0, 0, tiled=True)  3.34 us
    ppermute x1, starting transfers between devices, on_device(): below = lax.ppermute(leading, 'row', ring(row_devices, -1))  2.91 us
    ppermute x1, starting transfers between devices, on_device(): across = lax.ppermute(across, 'col', across_pairs)  2.9 us
    pallas_call x1, Pallas kernels, on_device(): pl.pallas_call(spell_kernel, in_specs=[vmem], out_specs=anywhere, out_sha...  2.52 us
  transfers between devices with their start and end apart: 11, of which 7 were waited for; matrix products, arithmetic and copies ran while one was open for 0% of the time, Pallas kernels for 23%

profile of v5, /device:TPU:0, one launch (start us, length us, event | category | flops | bytes accessed | tf_op | source)
XLA Modules:
  0.0 69.4 jit_solution(11747730982229235358)
XLA Ops:
  0.6 6.5 %shard_map.59 = (s32[5,32,2048]{2,1,0:T(8,128)S(1)}, bf16[96,128]{1,0:T(8,128)(2,1)S(1)}, bf16[96,128]{1,0:T(8,128)(2,1)S(1)}, bf16[6,128,256]{2,1,0:T(8,128)(2,1)S(1)}, bf16[6,128,256]{2,1,0:T(8,128)(2,1)S(1)}) custom-call(s32[1]{0:T(128)} %bitcast.odd_ref, f32[2]{0:T(128)} %bar_hbm.3, s32[640,2048]{1,0:T(8,128)} %spins_hbm.3, f32[2,640,2048]{2,1,0:T(8,128)} %draws_hbm.3, ...), custom_call_target="tpu_custom_call" | custom-call | flops 26214400 | bytes 7864320 | tf_op jit(solution)/shard_map/pallas_call | solution.py:556
  7.2 3.0 %collective-permute-start.5 = (bf16[6,128,256]{2,1,0:T(8,128)(2,1)S(1)}, bf16[6,128,256]{2,1,0:T(8,128)(2,1)S(1)}, u32[]{:S(2)}, u32[]{:S(2)}) collective-permute-start(bf16[6,128,256]{2,1,0:T(8,128)(2,1)S(1)} %get-tuple-element.28.refs_1_), channel_id=1, source_target_pairs={{0,1},{1,0},{2,3},{3,2},{4,5},{5,4},{6,7},{7,6},{8,9},{9,8},{10,11... | collective-permute-start | bytes 1179656 | tf_op jit(solution)/shard_map/ppermute | solution.py:553
  10.3 2.9 %collective-permute-start.1 = (bf16[96,128]{1,0:T(8,128)(2,1)S(1)}, bf16[96,128]{1,0:T(8,128)(2,1)S(1)}, u32[]{:S(2)}, u32[]{:S(2)}) collective-permute-start(bf16[96,128]{1,0:T(8,128)(2,1)S(1)} %get-tuple-element.19), channel_id=1, source_target_pairs={{0,3},{1,2},{2,1},{3,0},{4,7},{5,6},{6,5},{7,4},{8,11},{9,10},{10,... | collective-permute-start | bytes 73736 | tf_op jit(solution)/shard_map/ppermute | solution.py:598
  13.2 5.3 %shard_map.60 = (s32[5,32,2048]{2,1,0:T(8,128)S(1)}, bf16[6,160,256]{2,1,0:T(8,128)(2,1)S(1)}, bf16[6,160,256]{2,1,0:T(8,128)(2,1)S(1)}) custom-call(s32[1]{0:T(128)} %bitcast.odd_ref, f32[2]{0:T(128)} %bar_hbm.3, s32[640,2048]{1,0:T(8,128)} %spins_hbm.3, f32[2,640,2048]{2,1,0:T(8,128)} %draws_hbm.3, bf16[640,2048]{1,0:T(8,128)(2,1)} %moments_hbm.5, ...), custom_call_target="tpu_custom_call" | custom-call | flops 26214400 | bytes 7864320 | tf_op jit(solution)/shard_map/pallas_call | solution.py:556
  18.5 1.6 %collective-permute-done.beside_ref = bf16[96,128]{1,0:T(8,128)(2,1)S(1)} collective-permute-done((bf16[96,128]{1,0:T(8,128)(2,1)S(1)}, bf16[96,128]{1,0:T(8,128)(2,1)S(1)}, u32[]{:S(2)}, u32[]{:S(2)}) %collective-permute-start) | collective-permute-done | bytes 24608 | tf_op jit(solution)/shard_map/ppermute | solution.py:597
  20.1 1.5 %collective-permute-done.1.across_ref = bf16[96,128]{1,0:T(8,128)(2,1)S(1)} collective-permute-done((bf16[96,128]{1,0:T(8,128)(2,1)S(1)}, bf16[96,128]{1,0:T(8,128)(2,1)S(1)}, u32[]{:S(2)}, u32[]{:S(2)}) %collective-permute-start.1) | collective-permute-done | bytes 24608 | tf_op jit(solution)/shard_map/ppermute | solution.py:598
  21.6 0.5 shard_map.61
  22.1 1.6 %collective-permute-start.4 = (bf16[6,160,256]{2,1,0:T(8,128)(2,1)S(1)}, bf16[6,160,256]{2,1,0:T(8,128)(2,1)S(1)}, u32[]{:S(2)}, u32[]{:S(2)}) collective-permute-start(bf16[6,160,256]{2,1,0:T(8,128)(2,1)S(1)} %get-tuple-element.27.refs_0_), channel_id=1, source_target_pairs={{0,1},{1,0},{2,3},{3,2},{4,5},{5,4},{6,7},{7,6},{8,9},{9,8},{10,11... | collective-permute-start | bytes 1474568 | tf_op jit(solution)/shard_map/ppermute | solution.py:553
  23.7 0.5 collective-permute-start.7
  24.2 2.9 %collective-permute-start.3 = (bf16[32,2304]{1,0:T(8,128)(2,1)S(1)}, bf16[32,2304]{1,0:T(8,128)(2,1)S(1)}, u32[]{:S(2)}, u32[]{:S(2)}) collective-permute-start(bf16[32,2304]{1,0:T(8,128)(2,1)S(1)} %get-tuple-element.22), channel_id=1, source_target_pairs={{0,28},{4,0},{8,4},{12,8},{16,12},{20,16},{24,20},{28,24},{1,29},{... | collective-permute-start | bytes 442376 | tf_op jit(solution)/shard_map/ppermute | solution.py:640
  27.1 1.4 %collective-permute-done.2.above_ref = bf16[32,2304]{1,0:T(8,128)(2,1)S(1)} collective-permute-done((bf16[32,2304]{1,0:T(8,128)(2,1)S(1)}, bf16[32,2304]{1,0:T(8,128)(2,1)S(1)}, u32[]{:S(2)}, u32[]{:S(2)}) %collective-permute-start.2) | collective-permute-done | bytes 147488 | tf_op jit(solution)/shard_map/ppermute | solution.py:639
  28.8 1.0 %collective-permute-done.3.below_ref = bf16[32,2304]{1,0:T(8,128)(2,1)S(1)} collective-permute-done((bf16[32,2304]{1,0:T(8,128)(2,1)S(1)}, bf16[32,2304]{1,0:T(8,128)(2,1)S(1)}, u32[]{:S(2)}, u32[]{:S(2)}) %collective-permute-start.3) | collective-permute-done | bytes 147488 | tf_op jit(solution)/shard_map/ppermute | solution.py:640
  29.8 1.7 %shard_map.62 = (s32[32,2048]{1,0:T(8,128)S(1)}, bf16[832,256]{1,0:T(8,128)(2,1)S(1)}, bf16[832,256]{1,0:T(8,128)(2,1)S(1)}) custom-call(s32[1]{0:T(128)} %bitcast.odd_ref, s32[5,32,2304]{2,1,0:T(8,128)S(1)} %get-tuple-element.20.wide_ref, bf16[32,2304]{1,0:T(8,128)(2,1)S(1)} %collective-permute-done.2.above_ref, ...), custom_call_target="tpu_custom_call" | custom-call | flops 13107200 | bytes 1310720 | tf_op jit(solution)/shard_map/pallas_call | solution.py:556
  31.4 0.8 %collective-permute-start.6 = (bf16[832,256]{1,0:T(8,128)(2,1)S(1)}, bf16[832,256]{1,0:T(8,128)(2,1)S(1)}, u32[]{:S(2)}, u32[]{:S(2)}) collective-permute-start(bf16[832,256]{1,0:T(8,128)(2,1)S(1)} %get-tuple-element.29.refs_2_), channel_id=1, source_target_pairs={{0,1},{1,0},{2,3},{3,2},{4,5},{5,4},{6,7},{7,6},{8,9},{9,8},{10,11... | collective-permute-start | bytes 1277960 | tf_op jit(solution)/shard_map/ppermute | solution.py:553
  32.2 1.6 %collective-permute-start.9 = (bf16[832,256]{1,0:T(8,128)(2,1)S(1)}, bf16[832,256]{1,0:T(8,128)(2,1)S(1)}, u32[]{:S(2)}, u32[]{:S(2)}) collective-permute-start(bf16[832,256]{1,0:T(8,128)(2,1)S(1)} %get-tuple-element.26.refs_5_.refs_2_), channel_id=1, source_target_pairs={{0,2},{1,3},{2,0},{3,1},{4,6},{5,7},{6,4},{7,5},{8,10},{9,11},{10,... | collective-permute-start | bytes 1277960 | tf_op jit(solution)/shard_map/ppermute | solution.py:553
  33.8 3.8 %shard_map.63.refs_6_ = f32[8,2176]{1,0:T(8,128)S(1)} custom-call(bf16[6,160,256]{2,1,0:T(8,128)(2,1)S(1)} %get-tuple-element.27.refs_0_, bf16[6,128,256]{2,1,0:T(8,128)(2,1)S(1)} %get-tuple-element.28.refs_1_, bf16[832,256]{1,0:T(8,128)(2,1)S(1)} %get-tuple-element.29.refs_2_, bf16[6,160,256]{2,1,0:T(8,128)(2,1)S(1)} %get-tuple-element.24.refs_3_.refs_0_, ...), custom_call_target="tpu_custom_call" | custom-call | flops 2684354560 | bytes 2621440 | tf_op jit(solution)/shard_map/pallas_call | solution.py:556
  37.7 8.2 %collective-permute-done.8.refs_5_.refs_7_ = bf16[6,128,256]{2,1,0:T(8,128)(2,1)S(1)} collective-permute-done((bf16[6,128,256]{2,1,0:T(8,128)(2,1)S(1)}, bf16[6,128,256]{2,1,0:T(8,128)(2,1)S(1)}, u32[]{:S(2)}, u32[]{:S(2)}) %collective-permute-start.8) | collective-permute-done | bytes 393248 | tf_op jit(solution)/shard_map/ppermute | solution.py:553
  45.8 2.5 %shard_map.64.refs_9_ = f32[8,2176]{1,0:T(8,128)S(1)} custom-call(s32[1]{0:T(128)} %bitcast.odd_ref, bf16[6,160,256]{2,1,0:T(8,128)(2,1)S(1)} %get-tuple-element.24.refs_3_.refs_0_, bf16[6,128,256]{2,1,0:T(8,128)(2,1)S(1)} %get-tuple-element.25.refs_4_.refs_1_, bf16[6,160,256]{2,1,0:T(8,128)(2,1)S(1)} %collective-permute-done.4.refs_2_.refs_3_, ...), custom_call_target="tpu_custom_call" | custom-call | flops 1342177280 | bytes 2621440 | tf_op jit(solution)/shard_map/pallas_call | solution.py:556
  48.4 6.6 %collective-permute-done.9.refs_8_ = bf16[832,256]{1,0:T(8,128)(2,1)S(1)} collective-permute-done((bf16[832,256]{1,0:T(8,128)(2,1)S(1)}, bf16[832,256]{1,0:T(8,128)(2,1)S(1)}, u32[]{:S(2)}, u32[]{:S(2)}) %collective-permute-start.9) | collective-permute-done | bytes 426016 | tf_op jit(solution)/shard_map/ppermute | solution.py:553
  55.0 3.4 %shard_map.65 = f32[32,1,64]{2,1,0:T(1,128)} custom-call(s32[1]{0:T(128)} %bitcast.odd_ref, bf16[6,160,256]{2,1,0:T(8,128)(2,1)S(1)} %get-tuple-element.24.refs_3_.refs_0_, bf16[6,128,256]{2,1,0:T(8,128)(2,1)S(1)} %get-tuple-element.25.refs_4_.refs_1_, bf16[832,256]{1,0:T(8,128)(2,1)S(1)} %get-tuple-element.26.refs_5_.refs_2_, ...), custom_call_target="tpu_custom_call" | custom-call | flops 1342177280 | bytes 2621440 | tf_op jit(solution)/shard_map/pallas_call | solution.py:556
  58.4 3.3 %all-to-all-start = ((f32[32,1,64]{2,1,0:T(1,128)}), f32[32,1,64]{2,1,0:T(1,128)S(1)}, u32[]{:S(2)}, u32[]{:S(2)}) async-start(f32[32,1,64]{2,1,0:T(1,128)} %shard_map.65), calls=%async_computation | async-start | bytes 32768 | tf_op jit(solution)/shard_map/all_to_all | solution.py:713
  61.7 2.5 %spell.1 = f32[640,2048]{1,0:T(8,128)} custom-call(s32[32,2048]{1,0:T(8,128)S(1)} %get-tuple-element.23.spins_ref), custom_call_target="tpu_custom_call" | custom-call | flops 1310720 | bytes 5242880 | tf_op jit(solution)/shard_map/spell/pallas_call | solution.py:664
  64.2 4.6 %all-to-all-done = f32[32,1,64]{2,1,0:T(1,128)S(1)} async-done(((f32[32,1,64]{2,1,0:T(1,128)}), f32[32,1,64]{2,1,0:T(1,128)S(1)}, u32[]{:S(2)}, u32[]{:S(2)}) %all-to-all-start) | async-done | bytes 8224 | tf_op jit(solution)/shard_map/all_to_all | solution.py:713
  68.9 0.6 reduce_sum.9
  (7 shorter events, 0.4 us)
Async XLA Ops:
  7.2 25.0 %collective-permute-start.5 = (bf16[6,128,256]{2,1,0:T(8,128)(2,1)S(1)}, bf16[6,128,256]{2,1,0:T(8,128)(2,1)S(1)}, u32[]{:S(2)}, u32[]{:S(2)}) collective-permute-start(bf16[6,128,256]{2,1,0:T(8,128)(2,1)S(1)} %get-tuple-element.28.refs_1_), channel_id=1, source_target_pairs={{0,1},{1,0},{2,3},{3,2},{4,5},{5,4},{6,7},{7,6},{8,9},{9,8},{10,11... | collective-permute-start | bytes 1179656 | tf_op jit(solution)/shard_map/ppermute | solution.py:553
  10.2 9.9 %collective-permute-start = (bf16[96,128]{1,0:T(8,128)(2,1)S(1)}, bf16[96,128]{1,0:T(8,128)(2,1)S(1)}, u32[]{:S(2)}, u32[]{:S(2)}) collective-permute-start(bf16[96,128]{1,0:T(8,128)(2,1)S(1)} %get-tuple-element.18), channel_id=1, source_target_pairs={{0,1},{1,0},{2,3},{3,2},{4,5},{5,4},{6,7},{7,6},{8,9},{9,8},{10,11... | collective-permute-start | bytes 73736 | tf_op jit(solution)/shard_map/ppermute | solution.py:597
  10.3 11.3 %collective-permute-start.1 = (bf16[96,128]{1,0:T(8,128)(2,1)S(1)}, bf16[96,128]{1,0:T(8,128)(2,1)S(1)}, u32[]{:S(2)}, u32[]{:S(2)}) collective-permute-start(bf16[96,128]{1,0:T(8,128)(2,1)S(1)} %get-tuple-element.19), channel_id=1, source_target_pairs={{0,3},{1,2},{2,1},{3,0},{4,7},{5,6},{6,5},{7,4},{8,11},{9,10},{10,... | collective-permute-start | bytes 73736 | tf_op jit(solution)/shard_map/ppermute | solution.py:598
  22.0 6.4 %collective-permute-start.2 = (bf16[32,2304]{1,0:T(8,128)(2,1)S(1)}, bf16[32,2304]{1,0:T(8,128)(2,1)S(1)}, u32[]{:S(2)}, u32[]{:S(2)}) collective-permute-start(bf16[32,2304]{1,0:T(8,128)(2,1)S(1)} %get-tuple-element.21), channel_id=1, source_target_pairs={{0,4},{4,8},{8,12},{12,16},{16,20},{20,24},{24,28},{28,0},{1,5},{5... | collective-permute-start | bytes 442376 | tf_op jit(solution)/shard_map/ppermute | solution.py:639
  22.1 23.7 %collective-permute-start.4 = (bf16[6,160,256]{2,1,0:T(8,128)(2,1)S(1)}, bf16[6,160,256]{2,1,0:T(8,128)(2,1)S(1)}, u32[]{:S(2)}, u32[]{:S(2)}) collective-permute-start(bf16[6,160,256]{2,1,0:T(8,128)(2,1)S(1)} %get-tuple-element.27.refs_0_), channel_id=1, source_target_pairs={{0,1},{1,0},{2,3},{3,2},{4,5},{5,4},{6,7},{7,6},{8,9},{9,8},{10,11... | collective-permute-start | bytes 1474568 | tf_op jit(solution)/shard_map/ppermute | solution.py:553
  23.7 22.2 %collective-permute-start.7 = (bf16[6,160,256]{2,1,0:T(8,128)(2,1)S(1)}, bf16[6,160,256]{2,1,0:T(8,128)(2,1)S(1)}, u32[]{:S(2)}, u32[]{:S(2)}) collective-permute-start(bf16[6,160,256]{2,1,0:T(8,128)(2,1)S(1)} %get-tuple-element.24.refs_3_.refs_0_), channel_id=1, source_target_pairs={{0,2},{1,3},{2,0},{3,1},{4,6},{5,7},{6,4},{7,5},{8,10},{9,11},{10,... | collective-permute-start | bytes 1474568 | tf_op jit(solution)/shard_map/ppermute | solution.py:553
  24.2 5.6 %collective-permute-start.3 = (bf16[32,2304]{1,0:T(8,128)(2,1)S(1)}, bf16[32,2304]{1,0:T(8,128)(2,1)S(1)}, u32[]{:S(2)}, u32[]{:S(2)}) collective-permute-start(bf16[32,2304]{1,0:T(8,128)(2,1)S(1)} %get-tuple-element.22), channel_id=1, source_target_pairs={{0,28},{4,0},{8,4},{12,8},{16,12},{20,16},{24,20},{28,24},{1,29},{... | collective-permute-start | bytes 442376 | tf_op jit(solution)/shard_map/ppermute | solution.py:640
  28.5 17.4 %collective-permute-start.8 = (bf16[6,128,256]{2,1,0:T(8,128)(2,1)S(1)}, bf16[6,128,256]{2,1,0:T(8,128)(2,1)S(1)}, u32[]{:S(2)}, u32[]{:S(2)}) collective-permute-start(bf16[6,128,256]{2,1,0:T(8,128)(2,1)S(1)} %get-tuple-element.25.refs_4_.refs_1_), channel_id=1, source_target_pairs={{0,2},{1,3},{2,0},{3,1},{4,6},{5,7},{6,4},{7,5},{8,10},{9,11},{10,... | collective-permute-start | bytes 1179656 | tf_op jit(solution)/shard_map/ppermute | solution.py:553
  31.4 16.9 %collective-permute-start.6 = (bf16[832,256]{1,0:T(8,128)(2,1)S(1)}, bf16[832,256]{1,0:T(8,128)(2,1)S(1)}, u32[]{:S(2)}, u32[]{:S(2)}) collective-permute-start(bf16[832,256]{1,0:T(8,128)(2,1)S(1)} %get-tuple-element.29.refs_2_), channel_id=1, source_target_pairs={{0,1},{1,0},{2,3},{3,2},{4,5},{5,4},{6,7},{7,6},{8,9},{9,8},{10,11... | collective-permute-start | bytes 1277960 | tf_op jit(solution)/shard_map/ppermute | solution.py:553
  32.2 22.7 %collective-permute-start.9 = (bf16[832,256]{1,0:T(8,128)(2,1)S(1)}, bf16[832,256]{1,0:T(8,128)(2,1)S(1)}, u32[]{:S(2)}, u32[]{:S(2)}) collective-permute-start(bf16[832,256]{1,0:T(8,128)(2,1)S(1)} %get-tuple-element.26.refs_5_.refs_2_), channel_id=1, source_target_pairs={{0,2},{1,3},{2,0},{3,1},{4,6},{5,7},{6,4},{7,5},{8,10},{9,11},{10,... | collective-permute-start | bytes 1277960 | tf_op jit(solution)/shard_map/ppermute | solution.py:553
  58.4 10.5 %all-to-all-start = ((f32[32,1,64]{2,1,0:T(1,128)}), f32[32,1,64]{2,1,0:T(1,128)S(1)}, u32[]{:S(2)}, u32[]{:S(2)}) async-start(f32[32,1,64]{2,1,0:T(1,128)} %shard_map.65), calls=%async_computation | async-start | bytes 32768 | tf_op jit(solution)/shard_map/all_to_all | solution.py:713

commit v6 on v4

--- a/solution.py
+++ b/solution.py
@@ -253,6 +253,8 @@
     left_ref,
     given_ref,
     kept_ref,
+    given_rest_ref,
+    kept_rest_ref,
     joined_ref,
     moments_buf,
     sems,
@@ -292,12 +294,16 @@
     spins_ref[:, inner] = sweeps_of([joined_ref[w, :, inner] for w in range(WORDS)])
     for copy in weights:
         copy.wait()
-    for ref, lower in ((given_ref, 1 - odd_ref[0]), (kept_ref, odd_ref[0])):
+    for ref, rest, lower in (
+        (given_ref, given_rest_ref, 1 - odd_ref[0]),
+        (kept_ref, kept_rest_ref, odd_ref[0]),
+    ):
         for i in range(side):
             plane = (planes - side) * lower + i
+            target = ref.at[:, pl.ds(i * DEPTH, DEPTH)] if i < side - 1 else rest
             for t in range(ref.shape[0]):
                 lanes = pl.ds((t + 1) * TILE, TILE)
-                ref[t, i * DEPTH : (i + 1) * DEPTH, :] = weigh(
+                target[t] = weigh(
                     spins_ref[:, lanes],
                     moments_buf[lower, i * DEPTH : (i + 1) * DEPTH, lanes],
                     plane,
@@ -353,20 +359,23 @@
                 )
 
 
-def spell_kernel(spins_ref, sides_ref, out_ref):
-    columns = out_ref.shape[1]
-    first = pl.program_id(0) * PER_STEP + 1
-    for plane in range(PER_STEP):
-        bit = jnp.int32(1) << (first + plane)
+def spell_kernel(spins_ref, sides_ref, out_hbm, out_buf, sems):
+    columns = spins_ref.shape[1]
+    copies = []
+    for plane in range(out_hbm.shape[0] // DEPTH):
         rows = pl.ds(plane * DEPTH, DEPTH)
         for left in range(0, columns, TILE):
-            if left == 0:
-                word = sides_ref[0]
-            elif left == columns - TILE:
-                word = sides_ref[1]
+            lanes = pl.ds(left, TILE)
+            if left in (0, columns - TILE):
+                word = sides_ref[min(left, 1)]
             else:
-                word = spins_ref[:, left : left + TILE]
-            out_ref[rows, left : left + TILE] = jnp.where((word & bit) != 0, 1.0, -1.0)
+                word = spins_ref[:, lanes]
+            up = (word & (1 << (plane + 1))) != 0
+            out_buf[rows, lanes] = jnp.where(up, 1.0, -1.0)
+        copies.append(pltpu.make_async_copy(out_buf.at[rows], out_hbm.at[rows], sems.at[plane]))
+        copies[-1].start()
+    for copy in copies:
+        copy.wait()
 
 
 def gram(left, right):
@@ -392,20 +401,36 @@
 
 
 def tile(block, t):
-    low, high, ends = block
-    last = low.shape[0] + 1
+    parts, ends, rows = block
+    last = parts[0].shape[0] + 1
     if t in (0, last):
-        return ends[min(t, 1)]
-    return stack([low, high], t - 1, t)
+        return jnp.concatenate([ends[min(t, 1), at] for at in rows], axis=0)
+    return stack(parts, t - 1, t)
 
 
 def tiles_of(block, places):
     return jnp.concatenate([tile(block, t) for t in places], axis=0)
 
 
+def whole(parts):
+    low, rest, high, ends = parts
+    return (low, rest, high), ends, (slice(0, ends.shape[1]),)
+
+
+def without_rest(parts):
+    low, rest, high, ends = parts
+    held = low.shape[1] + rest.shape[1]
+    return (low, high), ends, (slice(0, low.shape[1]), slice(held, ends.shape[1]))
+
+
+def rest_only(parts):
+    low, rest, _, ends = parts
+    return (rest,), ends, (slice(low.shape[1], low.shape[1] + rest.shape[1]),)
+
+
 def own_kernel(*refs):
     parts, (out_ref, sums_ref) = refs[:-2], refs[-2:]
-    blocks = (parts[:3], parts[3:])
+    blocks = (whole(parts[:4]), whole(parts[4:]))
     tiles = parts[0].shape[0] + 2
     for n in range(tiles):
         sums_ref[:, n * TILE : (n + 1) * TILE] = sum(
@@ -441,12 +466,13 @@
     out_ref[...] = fold(sums_ref) + base_ref[...]
 
 
-def late_kernel(scale, odd_ref, *refs):
+def late_kernel(odd_ref, *refs):
     (base_ref, out_ref, sums_ref) = refs[-3:]
     tiles = refs[0].shape[0] + 2
     sums_ref[:, :TILE] = jnp.zeros((TILE, TILE), jnp.float32)
 
     def run(pairs):
+        pairs = [tuple(without_rest(part) for part in pair) for pair in pairs]
         for n in range(1, tiles + 1):
             places = [(tiles - 1, n - 1)] + ([(tiles - n, 0)] if n > 1 else [])
             sums_ref[:, n * TILE : (n + 1) * TILE] = sum(
@@ -454,7 +480,26 @@
                 for left, right in pairs
             )
 
-    by_side(odd_ref, refs[0:3], refs[3:6], refs[6:9], run)
+    by_side(odd_ref, refs[0:4], refs[4:8], refs[8:12], run)
+    out_ref[...] = fold(sums_ref) + base_ref[...]
+
+
+def last_kernel(scale, odd_ref, *refs):
+    (base_ref, out_ref, sums_ref) = refs[-3:]
+    tiles = refs[0].shape[0] + 2
+    sums_ref[:, :TILE] = jnp.zeros((TILE, TILE), jnp.float32)
+
+    def run(pairs):
+        pairs = [tuple(rest_only(part) for part in pair) for pair in pairs]
+        for n in range(1, tiles + 1):
+            sums_ref[:, n * TILE : (n + 1) * TILE] = gram(
+                jnp.concatenate(
+                    [tiles_of(left, range(tiles - n, tiles)) for left, _ in pairs], axis=0
+                ),
+                jnp.concatenate([tiles_of(right, range(n)) for _, right in pairs], axis=0),
+            )
+
+    by_side(odd_ref, refs[0:4], refs[4:8], refs[8:12], run)
     value = fold(sums_ref) + base_ref[...]
     for height in (4, 2, 1):
         value = value + pltpu.roll(pltpu.roll(value, value.shape[1] - height, 1), 8 - height, 0)
@@ -554,9 +599,9 @@
         words,
     )
     side = half - MIDDLE
-    low = message(tiles - 2, side * DEPTH)
+    low, rest = message(tiles - 2, (side - 1) * DEPTH), message(tiles - 2, DEPTH)
     reach = 2 * (TILE + LANES)
-    spins, sides, right, left, given, kept = call(
+    spins, sides, right, left, given, kept, given_rest, kept_rest = call(
         inner_kernel,
         [smem, vmem, vmem, vmem, anywhere],
         [
@@ -566,6 +611,8 @@
             edge,
             low,
             low,
+            rest,
+            rest,
         ],
         [
             pltpu.VMEM(words_shape.shape, jnp.int32),
@@ -580,13 +627,13 @@
         below,
         moments,
     )
-    own = [given, own[0], kept, own[1]]
     mid, far = exchange(given, kept)
-    got = [mid, got[0], far, got[1]]
+    given, kept = [given, given_rest, own[0]], [kept, kept_rest, own[1]]
+    got = [[mid, got[0]], [far, got[1]]]
     before = lax.ppermute(right, "col", ring(col_devices, 1))
     after = lax.ppermute(left, "col", ring(col_devices, -1))
     ends = message(2, half_rows)
-    side_spins, given, kept = call(
+    side_spins, given_ends, kept_ends = call(
         side_kernel,
         [smem, vmem, vmem, vmem, anywhere],
         [jax.ShapeDtypeStruct((2, DEPTH, TILE), jnp.int32), ends, ends],
@@ -603,18 +650,16 @@
         after,
         moments,
     )
-    own = [own[0], own[1], given, own[2], own[3], kept]
-    mid, far = exchange(given, kept)
+    given, kept = given + [given_ends], kept + [kept_ends]
+    mid_ends, far_ends = exchange(given_ends, kept_ends)
+    mid_rest, far_rest = exchange(given_rest, kept_rest)
 
     spins_out = pl.pallas_call(
         spell_kernel,
-        grid=(rows // (PER_STEP * DEPTH),),
-        in_specs=[
-            pl.BlockSpec((DEPTH, columns), lambda i: (0, 0)),
-            pl.BlockSpec((2, DEPTH, TILE), lambda i: (0, 0, 0)),
-        ],
-        out_specs=pl.BlockSpec((PER_STEP * DEPTH, columns), lambda i: (i, 0)),
+        in_specs=[vmem, vmem],
+        out_specs=anywhere,
         out_shape=jax.ShapeDtypeStruct((rows, columns), jnp.float32),
+        scratch_shapes=[pltpu.VMEM((rows, columns), jnp.float32), dma((planes,))],
         compiler_params=params(),
         cost_estimate=pl.CostEstimate(
             flops=rows * columns, bytes_accessed=4 * rows * columns, transcendentals=0
@@ -625,7 +670,7 @@
     sums = pltpu.VMEM((TILE, R + TILE), jnp.float32)
     folded = jax.ShapeDtypeStruct((8, R + LANES), jnp.float32)
     work = rows * columns * columns
-    base = call(own_kernel, [vmem] * 6, folded, [sums], work, 2 * rows * columns, *own)
+    base = call(own_kernel, [vmem] * 8, folded, [sums], work, 2 * rows * columns, *given, *kept)
     base = call(
         early_kernel,
         [smem] + [vmem] * 7,
@@ -634,28 +679,48 @@
         work // 2,
         2 * rows * columns,
         odd,
-        own[3],
-        own[4],
-        *got,
+        kept[0],
+        kept[2],
+        *got[0],
+        *got[1],
         base,
     )
-    partial_sums = call(
-        functools.partial(late_kernel, normaliser),
-        [smem] + [vmem] * 10,
-        jax.ShapeDtypeStruct((devices, 1, R // devices), jnp.float32),
+    base = call(
+        late_kernel,
+        [smem] + [vmem] * 13,
+        folded,
         [sums],
         work // 2,
         2 * rows * columns,
         odd,
-        own[3],
-        own[4],
-        own[5],
-        got[0],
-        got[1],
-        mid,
-        got[2],
-        got[3],
-        far,
+        *kept,
+        got[0][0],
+        given_rest,
+        got[0][1],
+        mid_ends,
+        got[1][0],
+        kept_rest,
+        got[1][1],
+        far_ends,
+        base,
+    )
+    partial_sums = call(
+        functools.partial(last_kernel, normaliser),
+        [smem] + [vmem] * 13,
+        jax.ShapeDtypeStruct((devices, 1, R // devices), jnp.float32),
+        [sums],
+        work // 8,
+        rows * columns,
+        odd,
+        *kept,
+        got[0][0],
+        mid_rest,
+        got[0][1],
+        mid_ends,
+        got[1][0],
+        far_rest,
+        got[1][1],
+        far_ends,
         base,
     )
     shares = lax.all_to_all(partial_sums, ("row", "col"), 0, 0, tiled=True)

time: 74.3 us -> 67.6 us (0.910)
  waiting for transfers between devices: 25.9 us -> 17.4 us
  starting transfers between devices: 18.3 us -> 21.1 us
  Pallas kernels: 28.6 us -> 27.6 us
    ppermute x1, waiting for transfers between devices: 20.5 us -> 10.4 us  [on_device(): before = lax.ppermute(right, 'col', ring(col_devices, 1))]
    pallas_call x1, Pallas kernels: 4.44 us -> 2.52 us  [on_device(): pl.pallas_call(spell_kernel, in_specs=[vmem, vmem], out_specs=anywhere, o...]
    all_to_all x1, waiting for transfers between devices: 2.76 us -> 4.67 us  [on_device(): shares = lax.all_to_all(partial_sums, ('row', 'col'), 0, 0, tiled=True)]
    all_to_all x1, starting transfers between devices: 3.29 us -> 4.69 us  [on_device(): shares = lax.all_to_all(partial_sums, ('row', 'col'), 0, 0, tiled=True)]
    ppermute x3 -> x4, starting transfers between devices: 3.55 us -> 4.66 us  [exchange(): lax.ppermute(kept, 'col', beyond)]
    pallas_call x7 -> x8, Pallas kernels: 24.1 us -> 25.1 us  [call(): pl.pallas_call(kernel, in_specs=specs, out_specs=jax.tree.map(lambda _: v...]
    ppermute x3 -> x4, starting transfers between devices: 3.49 us -> 4.08 us  [exchange(): lax.ppermute(given, 'col', beside)]
  transfers between devices with their start and end apart: 11 -> 13, of which waited for: 4 -> 3; matrix products, arithmetic and copies ran while one was open for 0% -> 0% of each run, Pallas kernels for 21% -> 27%
where the time goes in v6:
time: 67.6 us; the launch traced here: 67.4 us
  Pallas kernels  27.6 us (41%)
  starting transfers between devices  21.1 us (31%)
  waiting for transfers between devices  17.4 us (26%)
  between operations  0.75 us (1%)
    pallas_call x8, Pallas kernels, call(): pl.pallas_call(kernel, in_specs=specs, out_specs=jax.tree.map(lambda _: v...  25.1 us
    ppermute x1, waiting for transfers between devices, on_device(): before = lax.ppermute(right, 'col', ring(col_devices, 1))  10.4 us
    all_to_all x1, starting transfers between devices, on_device(): shares = lax.all_to_all(partial_sums, ('row', 'col'), 0, 0, tiled=True)  4.69 us
    all_to_all x1, waiting for transfers between devices, on_device(): shares = lax.all_to_all(partial_sums, ('row', 'col'), 0, 0, tiled=True)  4.67 us
    ppermute x4, starting transfers between devices, exchange(): lax.ppermute(kept, 'col', beyond)  4.66 us
    ppermute x1, starting transfers between devices, on_device(): below = lax.ppermute(leading, 'row', ring(row_devices, -1))  4.09 us
    ppermute x4, starting transfers between devices, exchange(): lax.ppermute(given, 'col', beside)  4.08 us
    pallas_call x1, Pallas kernels, on_device(): pl.pallas_call(spell_kernel, in_specs=[vmem, vmem], out_specs=anywhere, o...  2.52 us
  transfers between devices with their start and end apart: 13, of which 3 were waited for; matrix products, arithmetic and copies ran while one was open for 0% of the time, Pallas kernels for 27%

profile of v6, /device:TPU:0, one launch (start us, length us, event | category | flops | bytes accessed | tf_op | source)
XLA Modules:
  0.0 67.4 jit_solution(726671872243064958)
XLA Ops:
  0.6 7.5 %shard_map.59 = (s32[5,32,2048]{2,1,0:T(8,128)S(1)}, bf16[32,2048]{1,0:T(8,128)(2,1)S(1)}, bf16[32,2048]{1,0:T(8,128)(2,1)S(1)}, bf16[6,192,256]{2,1,0:T(8,128)(2,1)S(1)}, bf16[6,192,256]{2,1,0:T(8,128)(2,1)S(1)}) custom-call(s32[1]{0:T(128)} %bitcast.odd_ref, f32[2]{0:T(128)} %bar_ref.3, s32[640,2048]{1,0:T(8,128)} %spins_hbm.3, f32[2,640,2048]{2,1,0:T(8,128)} %draws_hbm.3, ...), custom_call_target="tpu_custom_call" | custom-call | flops 36700160 | bytes 11010048 | tf_op jit(solution)/shard_map/pallas_call | solution.py:542
  8.1 0.5 collective-permute-start
  8.7 4.1 %collective-permute-start.1 = (bf16[32,2048]{1,0:T(8,128)(2,1)S(1)}, bf16[32,2048]{1,0:T(8,128)(2,1)S(1)}, u32[]{:S(2)}, u32[]{:S(2)}) collective-permute-start(bf16[32,2048]{1,0:T(8,128)(2,1)S(1)} %get-tuple-element.20), channel_id=1, source_target_pairs={{0,28},{4,0},{8,4},{12,8},{16,12},{20,16},{24,20},{28,24},{1,29},{... | collective-permute-start | bytes 393224 | tf_op jit(solution)/shard_map/ppermute | solution.py:580
  12.8 1.9 %collective-permute-start.6 = (bf16[6,192,256]{2,1,0:T(8,128)(2,1)S(1)}, bf16[6,192,256]{2,1,0:T(8,128)(2,1)S(1)}, u32[]{:S(2)}, u32[]{:S(2)}) collective-permute-start(bf16[6,192,256]{2,1,0:T(8,128)(2,1)S(1)} %get-tuple-element.32.refs_2_), channel_id=1, source_target_pairs={{0,1},{1,0},{2,3},{3,2},{4,5},{5,4},{6,7},{7,6},{8,9},{9,8},{10,11... | collective-permute-start | bytes 1769480 | tf_op jit(solution)/shard_map/ppermute | solution.py:539
  14.7 1.5 %collective-permute-start.10 = (bf16[6,192,256]{2,1,0:T(8,128)(2,1)S(1)}, bf16[6,192,256]{2,1,0:T(8,128)(2,1)S(1)}, u32[]{:S(2)}, u32[]{:S(2)}) collective-permute-start(bf16[6,192,256]{2,1,0:T(8,128)(2,1)S(1)} %get-tuple-element.28.refs_6_.refs_1_.refs_2_), channel_id=1, source_target_pairs={{0,2},{1,3},{2,0},{3,1},{4,6},{5,7},{6,4},{7,5},{8,10},{9,11},{10,... | collective-permute-start | bytes 1769480 | tf_op jit(solution)/shard_map/ppermute | solution.py:539
  16.2 2.7 %shard_map.60.words_ref = s32[5,32,2048]{2,1,0:T(8,128)S(1)} custom-call(f32[2]{0:T(128)} %bar_ref.3, s32[640,2048]{1,0:T(8,128)} %spins_hbm.3, f32[2,640,2048]{2,1,0:T(8,128)} %draws_hbm.3, s32[5,32,2048]{2,1,0:T(8,128)S(1)} %get-tuple-element.18.middle_ref), custom_call_target="tpu_custom_call" | custom-call | flops 15728640 | bytes 4718592 | tf_op jit(solution)/shard_map/pallas_call | solution.py:542
  19.0 2.5 %shard_map.61 = (s32[32,2048]{1,0:T(8,128)S(1)}, s32[5,32,768]{2,1,0:T(8,128)S(1)}, bf16[96,128]{1,0:T(8,128)(2,1)S(1)}, bf16[96,128]{1,0:T(8,128)(2,1)S(1)}, bf...) custom-call(s32[1]{0:T(128)} %bitcast.odd_ref, ...), custom_call_target="tpu_custom_call" | custom-call | flops 52428800 | bytes 5242880 | tf_op jit(solution)/shard_map/pallas_call | solution.py:542
  21.5 0.6 collective-permute-start.4
  22.1 1.5 %collective-permute-start.2 = (bf16[96,128]{1,0:T(8,128)(2,1)S(1)}, bf16[96,128]{1,0:T(8,128)(2,1)S(1)}, u32[]{:S(2)}, u32[]{:S(2)}) collective-permute-start(bf16[96,128]{1,0:T(8,128)(2,1)S(1)} %get-tuple-element.23), channel_id=1, source_target_pairs={{0,1},{1,2},{2,3},{3,0},{4,5},{5,6},{6,7},{7,4},{8,9},{9,10},{10,1... | collective-permute-start | bytes 73736 | tf_op jit(solution)/shard_map/ppermute | solution.py:633
  24.1 10.4 %collective-permute-done.2.before_ref = bf16[96,128]{1,0:T(8,128)(2,1)S(1)} collective-permute-done((bf16[96,128]{1,0:T(8,128)(2,1)S(1)}, bf16[96,128]{1,0:T(8,128)(2,1)S(1)}, u32[]{:S(2)}, u32[]{:S(2)}) %collective-permute-start.2) | collective-permute-done | bytes 24608 | tf_op jit(solution)/shard_map/ppermute | solution.py:633
  34.5 1.6 %collective-permute-start.3 = (bf16[96,128]{1,0:T(8,128)(2,1)S(1)}, bf16[96,128]{1,0:T(8,128)(2,1)S(1)}, u32[]{:S(2)}, u32[]{:S(2)}) collective-permute-start(bf16[96,128]{1,0:T(8,128)(2,1)S(1)} %get-tuple-element.24), channel_id=1, source_target_pairs={{0,3},{1,0},{2,1},{3,2},{4,7},{5,4},{6,5},{7,6},{8,11},{9,8},{10,9... | collective-permute-start | bytes 73736 | tf_op jit(solution)/shard_map/ppermute | solution.py:634
  36.0 2.3 %collective-permute-done.3.after_ref = bf16[96,128]{1,0:T(8,128)(2,1)S(1)} collective-permute-done((bf16[96,128]{1,0:T(8,128)(2,1)S(1)}, bf16[96,128]{1,0:T(8,128)(2,1)S(1)}, u32[]{:S(2)}, u32[]{:S(2)}) %collective-permute-start.3) | collective-permute-done | bytes 24608 | tf_op jit(solution)/shard_map/ppermute | solution.py:634
  38.3 1.7 %shard_map.62 = (s32[2,32,256]{2,1,0:T(8,128)S(1)}, bf16[2,320,256]{2,1,0:T(8,128)(2,1)S(1)}, bf16[2,320,256]{2,1,0:T(8,128)(2,1)S(1)}) custom-call(s32[1]{0:T(128)} %bitcast.odd_ref, s32[5,32,768]{2,1,0:T(8,128)S(1)} %get-tuple-element.22.sides_ref, bf16[96,128]{1,0:T(8,128)(2,1)S(1)} %collective-permute-done.2.before_ref, ...), custom_call_target="tpu_custom_call" | custom-call | flops 13107200 | bytes 1310720 | tf_op jit(solution)/shard_map/pallas_call | solution.py:542
  40.0 1.4 %collective-permute-start.7 = (bf16[2,320,256]{2,1,0:T(8,128)(2,1)S(1)}, bf16[2,320,256]{2,1,0:T(8,128)(2,1)S(1)}, u32[]{:S(2)}, u32[]{:S(2)}) collective-permute-start(bf16[2,320,256]{2,1,0:T(8,128)(2,1)S(1)} %get-tuple-element.33.refs_3_), channel_id=1, source_target_pairs={{0,1},{1,0},{2,3},{3,2},{4,5},{5,4},{6,7},{7,6},{8,9},{9,8},{10,11... | collective-permute-start | bytes 983048 | tf_op jit(solution)/shard_map/ppermute | solution.py:539
  41.4 1.7 %collective-permute-start.11 = (bf16[2,320,256]{2,1,0:T(8,128)(2,1)S(1)}, bf16[2,320,256]{2,1,0:T(8,128)(2,1)S(1)}, u32[]{:S(2)}, u32[]{:S(2)}) collective-permute-start(bf16[2,320,256]{2,1,0:T(8,128)(2,1)S(1)} %get-tuple-element.29.refs_7_.refs_3_), channel_id=1, source_target_pairs={{0,2},{1,3},{2,0},{3,1},{4,6},{5,7},{6,4},{7,5},{8,10},{9,11},{10,... | collective-permute-start | bytes 983048 | tf_op jit(solution)/shard_map/ppermute | solution.py:539
  43.1 3.9 %shard_map.63.refs_6_ = f32[8,2176]{1,0:T(8,128)S(1)} custom-call(bf16[6,96,256]{2,1,0:T(8,128)(2,1)S(1)} %get-tuple-element.30.refs_0_, bf16[6,32,256]{2,1,0:T(8,128)(2,1)S(1)} %get-tuple-element.31.refs_1_.refs_5_, bf16[6,192,256]{2,1,0:T(8,128)(2,1)S(1)} %get-tuple-element.32.refs_2_, bf16[2,320,256]{2,1,0:T(8,128)(2,1)S(1)} %get-tuple-element.33.refs_3_, ...), custom_call_target="tpu_custom_call" | custom-call | flops 2684354560 | bytes 2621440 | tf_op jit(solution)/shard_map/pallas_call | solution.py:542
  47.1 1.0 %collective-permute-start.9 = (bf16[6,32,256]{2,1,0:T(8,128)(2,1)S(1)}, bf16[6,32,256]{2,1,0:T(8,128)(2,1)S(1)}, u32[]{:S(2)}, u32[]{:S(2)}) collective-permute-start(bf16[6,32,256]{2,1,0:T(8,128)(2,1)S(1)} %get-tuple-element.27.refs_5_.refs_1_.refs_9_), channel_id=1, source_target_pairs={{0,2},{1,3},{2,0},{3,1},{4,6},{5,7},{6,4},{7,5},{8,10},{9,11},{10,... | collective-permute-start | bytes 294920 | tf_op jit(solution)/shard_map/ppermute | solution.py:539
  48.1 2.7 %shard_map.64.refs_12_ = f32[8,2176]{1,0:T(8,128)S(1)} custom-call(s32[1]{0:T(128)} %bitcast.odd_ref, bf16[6,96,256]{2,1,0:T(8,128)(2,1)S(1)} %get-tuple-element.26.refs_4_.refs_0_, bf16[6,192,256]{2,1,0:T(8,128)(2,1)S(1)} %get-tuple-element.28.refs_6_.refs_1_.refs_2_, bf16[6,96,256]{2,1,0:T(8,128)(2,1)S(1)} %collective-permute-done.4.refs_2_.refs_4_, ...), custom_call_target="tpu_custom_call" | custom-call | flops 1342177280 | bytes 2621440 | tf_op jit(solution)/shard_map/pallas_call | solution.py:542
  50.8 2.2 %shard_map.65.refs_12_ = f32[8,2176]{1,0:T(8,128)S(1)} custom-call(s32[1]{0:T(128)} %bitcast.odd_ref, bf16[6,96,256]{2,1,0:T(8,128)(2,1)S(1)} %get-tuple-element.26.refs_4_.refs_0_, bf16[6,32,256]{2,1,0:T(8,128)(2,1)S(1)} %get-tuple-element.27.refs_5_.refs_1_.refs_9_, bf16[6,192,256]{2,1,0:T(8,128)(2,1)S(1)} %get-tuple-element.28.refs_6_.refs_1_.refs_2_, ...), custom_call_target="tpu_custom_call" | custom-call | flops 1342177280 | bytes 2621440 | tf_op jit(solution)/shard_map/pallas_call | solution.py:542
  53.1 1.9 %shard_map.66 = f32[32,1,64]{2,1,0:T(1,128)} custom-call(s32[1]{0:T(128)} %bitcast.odd_ref, bf16[6,96,256]{2,1,0:T(8,128)(2,1)S(1)} %get-tuple-element.26.refs_4_.refs_0_, bf16[6,32,256]{2,1,0:T(8,128)(2,1)S(1)} %get-tuple-element.27.refs_5_.refs_1_.refs_9_, bf16[6,192,256]{2,1,0:T(8,128)(2,1)S(1)} %get-tuple-element.28.refs_6_.refs_1_.refs_2_, ...), custom_call_target="tpu_custom_call" | custom-call | flops 335544320 | bytes 1310720 | tf_op jit(solution)/shard_map/pallas_call | solution.py:542
  54.9 4.7 %all-to-all-start = ((f32[32,1,64]{2,1,0:T(1,128)}), f32[32,1,64]{2,1,0:T(1,128)S(1)}, u32[]{:S(2)}, u32[]{:S(2)}) async-start(f32[32,1,64]{2,1,0:T(1,128)} %shard_map.66), calls=%async_computation | async-start | bytes 32768 | tf_op jit(solution)/shard_map/all_to_all | solution.py:726
  59.6 2.5 %spell.1 = f32[640,2048]{1,0:T(8,128)} custom-call(s32[32,2048]{1,0:T(8,128)S(1)} %get-tuple-element.21.spins_ref, s32[2,32,256]{2,1,0:T(8,128)S(1)} %get-tuple-element.25.sides_ref), custom_call_target="tpu_custom_call" | custom-call | flops 1310720 | bytes 5242880 | tf_op jit(solution)/shard_map/spell/pallas_call | solution.py:657
  62.2 4.7 %all-to-all-done = f32[32,1,64]{2,1,0:T(1,128)S(1)} async-done(((f32[32,1,64]{2,1,0:T(1,128)}), f32[32,1,64]{2,1,0:T(1,128)S(1)}, u32[]{:S(2)}, u32[]{:S(2)}) %all-to-all-start) | async-done | bytes 8224 | tf_op jit(solution)/shard_map/all_to_all | solution.py:726
  66.8 0.6 reduce_sum.9
  (12 shorter events, 0.7 us)
Async XLA Ops:
  8.1 10.8 %collective-permute-start = (bf16[32,2048]{1,0:T(8,128)(2,1)S(1)}, bf16[32,2048]{1,0:T(8,128)(2,1)S(1)}, u32[]{:S(2)}, u32[]{:S(2)}) collective-permute-start(bf16[32,2048]{1,0:T(8,128)(2,1)S(1)} %get-tuple-element.19), channel_id=1, source_target_pairs={{0,4},{4,8},{8,12},{12,16},{16,20},{20,24},{24,28},{28,0},{1,5},{5... | collective-permute-start | bytes 393224 | tf_op jit(solution)/shard_map/ppermute | solution.py:579
  8.7 10.3 %collective-permute-start.1 = (bf16[32,2048]{1,0:T(8,128)(2,1)S(1)}, bf16[32,2048]{1,0:T(8,128)(2,1)S(1)}, u32[]{:S(2)}, u32[]{:S(2)}) collective-permute-start(bf16[32,2048]{1,0:T(8,128)(2,1)S(1)} %get-tuple-element.20), channel_id=1, source_target_pairs={{0,28},{4,0},{8,4},{12,8},{16,12},{20,16},{24,20},{28,24},{1,29},{... | collective-permute-start | bytes 393224 | tf_op jit(solution)/shard_map/ppermute | solution.py:580
  12.8 34.4 %collective-permute-start.6 = (bf16[6,192,256]{2,1,0:T(8,128)(2,1)S(1)}, bf16[6,192,256]{2,1,0:T(8,128)(2,1)S(1)}, u32[]{:S(2)}, u32[]{:S(2)}) collective-permute-start(bf16[6,192,256]{2,1,0:T(8,128)(2,1)S(1)} %get-tuple-element.32.refs_2_), channel_id=1, source_target_pairs={{0,1},{1,0},{2,3},{3,2},{4,5},{5,4},{6,7},{7,6},{8,9},{9,8},{10,11... | collective-permute-start | bytes 1769480 | tf_op jit(solution)/shard_map/ppermute | solution.py:539
  14.7 33.4 %collective-permute-start.10 = (bf16[6,192,256]{2,1,0:T(8,128)(2,1)S(1)}, bf16[6,192,256]{2,1,0:T(8,128)(2,1)S(1)}, u32[]{:S(2)}, u32[]{:S(2)}) collective-permute-start(bf16[6,192,256]{2,1,0:T(8,128)(2,1)S(1)} %get-tuple-element.28.refs_6_.refs_1_.refs_2_), channel_id=1, source_target_pairs={{0,2},{1,3},{2,0},{3,1},{4,6},{5,7},{6,4},{7,5},{8,10},{9,11},{10,... | collective-permute-start | bytes 1769480 | tf_op jit(solution)/shard_map/ppermute | solution.py:539
  21.5 19.9 %collective-permute-start.4 = (bf16[6,96,256]{2,1,0:T(8,128)(2,1)S(1)}, bf16[6,96,256]{2,1,0:T(8,128)(2,1)S(1)}, u32[]{:S(2)}, u32[]{:S(2)}) collective-permute-start(bf16[6,96,256]{2,1,0:T(8,128)(2,1)S(1)} %get-tuple-element.30.refs_0_), channel_id=1, source_target_pairs={{0,1},{1,0},{2,3},{3,2},{4,5},{5,4},{6,7},{7,6},{8,9},{9,8},{10,11... | collective-permute-start | bytes 884744 | tf_op jit(solution)/shard_map/ppermute | solution.py:539
  22.1 12.4 %collective-permute-start.2 = (bf16[96,128]{1,0:T(8,128)(2,1)S(1)}, bf16[96,128]{1,0:T(8,128)(2,1)S(1)}, u32[]{:S(2)}, u32[]{:S(2)}) collective-permute-start(bf16[96,128]{1,0:T(8,128)(2,1)S(1)} %get-tuple-element.23), channel_id=1, source_target_pairs={{0,1},{1,2},{2,3},{3,0},{4,5},{5,6},{6,7},{7,4},{8,9},{9,10},{10,1... | collective-permute-start | bytes 73736 | tf_op jit(solution)/shard_map/ppermute | solution.py:633
  23.6 23.4 %collective-permute-start.8 = (bf16[6,96,256]{2,1,0:T(8,128)(2,1)S(1)}, bf16[6,96,256]{2,1,0:T(8,128)(2,1)S(1)}, u32[]{:S(2)}, u32[]{:S(2)}) collective-permute-start(bf16[6,96,256]{2,1,0:T(8,128)(2,1)S(1)} %get-tuple-element.26.refs_4_.refs_0_), channel_id=1, source_target_pairs={{0,2},{1,3},{2,0},{3,1},{4,6},{5,7},{6,4},{7,5},{8,10},{9,11},{10,... | collective-permute-start | bytes 884744 | tf_op jit(solution)/shard_map/ppermute | solution.py:539
  34.5 3.8 %collective-permute-start.3 = (bf16[96,128]{1,0:T(8,128)(2,1)S(1)}, bf16[96,128]{1,0:T(8,128)(2,1)S(1)}, u32[]{:S(2)}, u32[]{:S(2)}) collective-permute-start(bf16[96,128]{1,0:T(8,128)(2,1)S(1)} %get-tuple-element.24), channel_id=1, source_target_pairs={{0,3},{1,0},{2,1},{3,2},{4,7},{5,4},{6,5},{7,6},{8,11},{9,8},{10,9... | collective-permute-start | bytes 73736 | tf_op jit(solution)/shard_map/ppermute | solution.py:634
  40.0 10.8 %collective-permute-start.7 = (bf16[2,320,256]{2,1,0:T(8,128)(2,1)S(1)}, bf16[2,320,256]{2,1,0:T(8,128)(2,1)S(1)}, u32[]{:S(2)}, u32[]{:S(2)}) collective-permute-start(bf16[2,320,256]{2,1,0:T(8,128)(2,1)S(1)} %get-tuple-element.33.refs_3_), channel_id=1, source_target_pairs={{0,1},{1,0},{2,3},{3,2},{4,5},{5,4},{6,7},{7,6},{8,9},{9,8},{10,11... | collective-permute-start | bytes 983048 | tf_op jit(solution)/shard_map/ppermute | solution.py:539
  41.4 9.4 %collective-permute-start.11 = (bf16[2,320,256]{2,1,0:T(8,128)(2,1)S(1)}, bf16[2,320,256]{2,1,0:T(8,128)(2,1)S(1)}, u32[]{:S(2)}, u32[]{:S(2)}) collective-permute-start(bf16[2,320,256]{2,1,0:T(8,128)(2,1)S(1)} %get-tuple-element.29.refs_7_.refs_3_), channel_id=1, source_target_pairs={{0,2},{1,3},{2,0},{3,1},{4,6},{5,7},{6,4},{7,5},{8,10},{9,11},{10,... | collective-permute-start | bytes 983048 | tf_op jit(solution)/shard_map/ppermute | solution.py:539
  47.0 6.1 %collective-permute-start.5 = (bf16[6,32,256]{2,1,0:T(8,128)(2,1)S(1)}, bf16[6,32,256]{2,1,0:T(8,128)(2,1)S(1)}, u32[]{:S(2)}, u32[]{:S(2)}) collective-permute-start(bf16[6,32,256]{2,1,0:T(8,128)(2,1)S(1)} %get-tuple-element.31.refs_1_.refs_5_), channel_id=1, source_target_pairs={{0,1},{1,0},{2,3},{3,2},{4,5},{5,4},{6,7},{7,6},{8,9},{9,8},{10,11... | collective-permute-start | bytes 294920 | tf_op jit(solution)/shard_map/ppermute | solution.py:539
  47.1 5.9 %collective-permute-start.9 = (bf16[6,32,256]{2,1,0:T(8,128)(2,1)S(1)}, bf16[6,32,256]{2,1,0:T(8,128)(2,1)S(1)}, u32[]{:S(2)}, u32[]{:S(2)}) collective-permute-start(bf16[6,32,256]{2,1,0:T(8,128)(2,1)S(1)} %get-tuple-element.27.refs_5_.refs_1_.refs_9_), channel_id=1, source_target_pairs={{0,2},{1,3},{2,0},{3,1},{4,6},{5,7},{6,4},{7,5},{8,10},{9,11},{10,... | collective-permute-start | bytes 294920 | tf_op jit(solution)/shard_map/ppermute | solution.py:539
  54.9 11.9 %all-to-all-start = ((f32[32,1,64]{2,1,0:T(1,128)}), f32[32,1,64]{2,1,0:T(1,128)S(1)}, u32[]{:S(2)}, u32[]{:S(2)}) async-start(f32[32,1,64]{2,1,0:T(1,128)} %shard_map.66), calls=%async_computation | async-start | bytes 32768 | tf_op jit(solution)/shard_map/all_to_all | solution.py:726

commit v7 on v5

--- a/solution.py
+++ b/solution.py
@@ -14,7 +14,7 @@
 LANES = 128
 TILE = 256
 PER_STEP = 2
-MIDDLE = 4
+MIDDLE = 5
 WORDS = 1 + 2 * SWEEPS
 
 
@@ -130,13 +130,13 @@
 
 def middle_kernel(
     odd_ref,
-    bar_hbm,
+    bar_ref,
     spins_hbm,
     draws_hbm,
     moments_hbm,
     words_ref,
-    beside_ref,
-    across_ref,
+    last_ref,
+    first_ref,
     given_ref,
     kept_ref,
     spins_buf,
@@ -145,7 +145,7 @@
     edge_draws,
     moments_buf,
     final_ref,
-    bar_ref,
+    bar_smem,
     sems,
     edge_sems,
 ):
@@ -153,23 +153,12 @@
     half = rows // DEPTH // 2
     planes = list(range(half - MIDDLE - 1, half + MIDDLE + 1))
     top = planes[0] * DEPTH
-    groups = groups_of(planes, PER_STEP)
-    size = PER_STEP * DEPTH
-    bars = pltpu.make_async_copy(bar_hbm, bar_ref, edge_sems.at[4, 1])
-    edges = []
-    for e, (at, row) in enumerate(
-        (at, row) for at in (0, columns - LANES) for row in (0, rows - top)
-    ):
-        source = (pl.ds(row, top), pl.ds(at, LANES))
-        edges.append(
-            pltpu.make_async_copy(spins_hbm.at[source], edge_spins.at[e], edge_sems.at[e, 0])
-        )
-        for k in range(SWEEPS):
-            edges.append(
-                pltpu.make_async_copy(
-                    draws_hbm.at[(k, *source)], edge_draws.at[k, e], edge_sems.at[e, 1 + k]
-                )
-            )
+    groups = groups_of(planes, 2 * PER_STEP)
+    size = 2 * PER_STEP * DEPTH
+    edges = [
+        fetch(s, spins_hbm, draws_hbm, edge_spins, edge_draws, edge_sems, row, 8 * s, 8)
+        for s, row in enumerate((rows - 8, 0))
+    ]
     copies = [
         fetch(
             g,
@@ -187,60 +176,38 @@
     weights = pltpu.make_async_copy(
         moments_hbm.at[pl.ds((half - MIDDLE) * DEPTH, 2 * MIDDLE * DEPTH)],
         moments_buf,
-        edge_sems.at[4, 0],
-    )
-    for copy in [bars] + edges + sum(copies, []) + [weights]:
+        edge_sems.at[2, 0],
+    )
+    bars = pltpu.make_async_copy(bar_ref, bar_smem, edge_sems.at[2, 1])
+    for copy in [bars] + sum(edges + copies, []) + [weights]:
         copy.start()
     bars.wait()
-    for copy in edges:
-        copy.wait()
-    side_words = []
-    for e in range(4):
-        if e % 2 == 0:
-            side_words.append([jnp.zeros((DEPTH, LANES), jnp.int32)] * WORDS)
-        words = side_words[-1]
-        for i in range(top // DEPTH):
-            plane = i + (e % 2) * (rows - top) // DEPTH
-            at = pl.ds(i * DEPTH, DEPTH)
-            words[0] = words[0] | (edge_spins[e, at, :] << (plane + 1))
-            for k in range(SWEEPS):
-                draw = edge_draws[k, e, at, :]
-                for c in range(2):
-                    word = words[1 + 2 * k + c]
-                    words[1 + 2 * k + c] = jnp.where(
-                        draw < bar_ref[c], word | (1 << (plane + 1)), word
-                    )
+    bar_ref = bar_smem
+    for s, ref in enumerate((last_ref, first_ref)):
+        for copy in edges[s]:
+            copy.wait()
+        parts = [edge_spins[8 * s : 8 * s + 8, :]]
+        for k in range(SWEEPS):
+            draw = edge_draws[k, 8 * s : 8 * s + 8, :]
+            one = (draw < bar_ref[0]).astype(jnp.int32)
+            parts.append(one + 2 * (draw < bar_ref[1]).astype(jnp.int32))
+        ref[...] = strips(parts + [jnp.zeros_like(parts[0])])
     for g, group in enumerate(groups):
         for copy in copies[g]:
             copy.wait()
         pack(bar_ref, words_ref, spins_buf, draws_buf, group, g * size, g == 0)
-    lane = lax.broadcasted_iota(jnp.int32, (DEPTH, LANES), 1)
-    codes_of = []
-    for at, held, outer in (
-        (0, lane < 4, side_words[0]),
-        (columns - LANES, lane >= LANES - 4, side_words[1]),
-    ):
-        bits = []
-        for w in range(WORDS):
-            edge = jnp.where(held, words_ref[w, :, at : at + LANES] | outer[w], 0)
-            bits.append((spread(edge) >> (lane // 4)) & 1)
-        codes_of.append(jnp.concatenate(codes(bits), axis=0).astype(jnp.float32))
-    odd = odd_ref[0]
-    beside_ref[...] = select(odd, codes_of[0], codes_of[1]).astype(jnp.bfloat16)
-    across_ref[...] = select(odd, codes_of[1], codes_of[0]).astype(jnp.bfloat16)
     inner = slice(LANES, columns - LANES)
     final_ref[:, inner] = sweeps_of([words_ref[w, :, inner] for w in range(WORDS)])
     weights.wait()
-    fill(
-        (given_ref, kept_ref),
-        odd,
-        lambda lower: [half - MIDDLE + MIDDLE * lower + i for i in range(MIDDLE)],
-        lambda lower, i, t: moments_buf[
-            pl.ds(pl.multiple_of((MIDDLE * lower + i) * DEPTH, DEPTH), DEPTH),
-            pl.ds((t + 1) * TILE, TILE),
-        ],
-        lambda t: final_ref[:, pl.ds((t + 1) * TILE, TILE)],
-    )
+    for ref, lower in ((given_ref, 1 - odd_ref[0]), (kept_ref, odd_ref[0])):
+        for i in range(MIDDLE):
+            plane = half - MIDDLE + MIDDLE * lower + i
+            at = pl.ds(pl.multiple_of((MIDDLE * lower + i) * DEPTH, DEPTH), DEPTH)
+            for t in range(ref.shape[0]):
+                lanes = pl.ds((t + 1) * TILE, TILE)
+                ref[t, i * DEPTH : (i + 1) * DEPTH, :] = weigh(
+                    final_ref[:, lanes], moments_buf[at, lanes], plane
+                )
 
 
 def outer_kernel(
@@ -314,32 +281,35 @@
     )
 
 
-def widen_kernel(odd_ref, words_ref, beside_ref, across_ref, wide_ref, last_ref, first_ref, *, planes):
+def join_kernel(odd_ref, words_ref, above_ref, below_ref, joined_ref, beside_ref, across_ref, *, planes):
     columns = words_ref.shape[2]
+    above, below = unstrips(above_ref, 8), unstrips(below_ref, 8)
+    joined_ref[...] = words_ref[...]
+    for w in range(WORDS):
+        joined_ref[w, DEPTH - 8 :, :] = words_ref[w, DEPTH - 8 :, :] | above[w]
+        joined_ref[w, :8, :] = words_ref[w, :8, :] | (below[w] << (planes + 1))
+    lane = lax.broadcasted_iota(jnp.int32, (DEPTH, LANES), 1)
+    sent = []
+    for at, held in ((columns - LANES, lane >= LANES - 4), (0, lane < 4)):
+        bits = []
+        for w in range(WORDS):
+            edge = jnp.where(held, joined_ref[w, :, at : at + LANES], 0)
+            bits.append((spread(edge) >> (lane // 4)) & 1)
+        sent.append(jnp.concatenate(codes(bits), axis=0).astype(jnp.float32))
     odd = odd_ref[0]
-    lane = lax.broadcasted_iota(jnp.int32, (DEPTH, LANES), 1)
-    beside, across = unstrips(beside_ref, DEPTH), unstrips(across_ref, DEPTH)
-    for w in range(WORDS):
-        wide_ref[w, :, LANES : LANES + columns] = words_ref[w]
-        before = select(odd, beside[w], across[w])
-        after = select(odd, across[w], beside[w])
-        wide_ref[w, :, :LANES] = spread(before << (lane // 4))
-        wide_ref[w, :, LANES + columns :] = spread(after << (lane // 4))
-    for ref, top, place in ((last_ref, DEPTH - 8, planes), (first_ref, 0, 1)):
-        bits = [(wide_ref[w, top : top + 8, :] >> place) & 1 for w in range(WORDS)]
-        ref[...] = strips(codes(bits) + [jnp.zeros_like(bits[0])])
+    beside_ref[...] = select(odd, sent[1], sent[0]).astype(jnp.bfloat16)
+    across_ref[...] = select(odd, sent[0], sent[1]).astype(jnp.bfloat16)
 
 
 def side_kernel(
     odd_ref,
-    wide_ref,
-    above_ref,
-    below_ref,
+    joined_ref,
+    beside_ref,
+    across_ref,
     moments_hbm,
     spins_ref,
     given_ref,
     kept_ref,
-    joined_ref,
     tile_moments,
     row_moments,
     final_ref,
@@ -362,12 +332,18 @@
     ]
     for copy in weights:
         copy.start()
-    above, below = unstrips(above_ref, 8), unstrips(below_ref, 8)
-    joined_ref[...] = wide_ref[...]
-    for w in range(WORDS):
-        joined_ref[w, DEPTH - 8 :, :] = wide_ref[w, DEPTH - 8 :, :] | above[w]
-        joined_ref[w, :8, :] = wide_ref[w, :8, :] | (below[w] << (planes + 1))
-    final_ref[...] = sweeps_of([joined_ref[w] for w in range(WORDS)])
+    lane = lax.broadcasted_iota(jnp.int32, (DEPTH, LANES), 1)
+    odd = odd_ref[0]
+    words = []
+    for w, halos in enumerate(zip(unstrips(beside_ref, DEPTH), unstrips(across_ref, DEPTH))):
+        before, after = select(odd, *halos), select(odd, *halos[::-1])
+        words.append(
+            jnp.concatenate(
+                [spread(before << (lane // 4)), joined_ref[w], spread(after << (lane // 4))],
+                axis=1,
+            )
+        )
+    final_ref[...] = sweeps_of(words)
     spins_ref[...] = final_ref[:, LANES : LANES + columns]
     for copy in weights:
         copy.wait()
@@ -534,6 +510,7 @@
     vmem = pl.BlockSpec(memory_space=pltpu.VMEM)
     smem = pl.BlockSpec(memory_space=pltpu.SMEM)
     anywhere = pl.BlockSpec(memory_space=pltpu.HBM)
+    strip = jax.ShapeDtypeStruct((8 * (2 + SWEEPS), columns), jnp.bfloat16)
     edge = jax.ShapeDtypeStruct((DEPTH * (1 + SWEEPS), LANES), jnp.bfloat16)
     words_shape = jax.ShapeDtypeStruct((WORDS, DEPTH, columns), jnp.int32)
     dma = pltpu.SemaphoreType.DMA
@@ -567,22 +544,20 @@
     remaining = rows - packed
     side = half - MIDDLE - 1
     middle = message(tiles - 2, MIDDLE * DEPTH)
-    across_pairs = [(i, (i - 1 + 2 * (i % 2)) % col_devices) for i in range(col_devices)]
-    beside_pairs = [(i, i ^ 1) for i in range(col_devices)]
-    words, beside, across, given, kept = call(
+    words, last, leading, given, kept = call(
         middle_kernel,
         [smem, anywhere, anywhere, anywhere, anywhere],
-        [words_shape, edge, edge, middle, middle],
+        [words_shape, strip, strip, middle, middle],
         [
             pltpu.VMEM((packed, columns), jnp.int32),
             pltpu.VMEM((SWEEPS, packed, columns), jnp.float32),
-            pltpu.VMEM((4, remaining // 2, LANES), jnp.int32),
-            pltpu.VMEM((SWEEPS, 4, remaining // 2, LANES), jnp.float32),
+            pltpu.VMEM((16, columns), jnp.int32),
+            pltpu.VMEM((SWEEPS, 16, columns), jnp.float32),
             pltpu.VMEM((2 * MIDDLE * DEPTH, columns), jnp.bfloat16),
             pltpu.VMEM((DEPTH, columns), jnp.int32),
             pltpu.SMEM((2,), jnp.float32),
-            dma((pl.cdiv(2 * MIDDLE + 2, PER_STEP), 1 + SWEEPS)),
-            dma((5, 1 + SWEEPS)),
+            dma((pl.cdiv(2 * MIDDLE + 2, 2 * PER_STEP), 1 + SWEEPS)),
+            dma((3, 1 + SWEEPS)),
         ],
         40 * packed * columns,
         4 * (1 + SWEEPS) * packed * columns,
@@ -594,8 +569,8 @@
     )
     own = [given, kept]
     got = [*exchange(given, kept)]
-    beside = lax.ppermute(beside, "col", beside_pairs)
-    across = lax.ppermute(across, "col", across_pairs)
+    above = lax.ppermute(last, "row", ring(row_devices, 1))
+    below = lax.ppermute(leading, "row", ring(row_devices, -1))
     low = message(tiles - 2, side * DEPTH)
     words, given, kept = call(
         outer_kernel,
@@ -622,40 +597,39 @@
     own = [given, own[0], kept, own[1]]
     mid, far = exchange(given, kept)
     got = [mid, got[0], far, got[1]]
-    wide_shape = jax.ShapeDtypeStruct((WORDS, DEPTH, columns + 2 * LANES), jnp.int32)
-    strip = jax.ShapeDtypeStruct((8 * (2 + SWEEPS), columns + 2 * LANES), jnp.bfloat16)
-    words, last, leading = call(
-        functools.partial(widen_kernel, planes=planes),
+    joined, beside, across = call(
+        functools.partial(join_kernel, planes=planes),
         [smem, vmem, vmem, vmem],
-        [wide_shape, strip, strip],
+        [words_shape, edge, edge],
         [],
         20 * DEPTH * columns,
         40 * DEPTH * columns,
         odd,
         words,
-        beside,
-        across,
-    )
-    above = lax.ppermute(last, "row", ring(row_devices, 1))
-    below = lax.ppermute(leading, "row", ring(row_devices, -1))
+        above,
+        below,
+    )
+    across = lax.ppermute(
+        across, "col", [(i, (i - 1 + 2 * (i % 2)) % col_devices) for i in range(col_devices)]
+    )
+    beside = lax.ppermute(beside, "col", [(i, i ^ 1) for i in range(col_devices)])
     ends = jax.ShapeDtypeStruct((2 * half_rows + (tiles - 2) * DEPTH, TILE), jnp.bfloat16)
     spins, given, kept = call(
         side_kernel,
         [smem, vmem, vmem, vmem, anywhere],
         [jax.ShapeDtypeStruct((DEPTH, columns), jnp.int32), ends, ends],
         [
-            pltpu.VMEM(wide_shape.shape, jnp.int32),
             pltpu.VMEM((2, rows, TILE), jnp.bfloat16),
             pltpu.VMEM((2, DEPTH, columns), jnp.bfloat16),
-            pltpu.VMEM(wide_shape.shape[1:], jnp.int32),
+            pltpu.VMEM((DEPTH, columns + 2 * LANES), jnp.int32),
             dma((4,)),
         ],
         10 * rows * columns,
         rows * columns,
         odd,
-        words,
-        above,
-        below,
+        joined,
+        beside,
+        across,
         moments,
     )
     own = [own[0], own[1], given, own[2], own[3], kept]

time: 69.6 us -> 69.4 us (level)
  waiting for transfers between devices: 24.9 us -> 19.8 us
  starting transfers between devices: 17.1 us -> 21.8 us
    ppermute x3, waiting for transfers between devices: 14.8 us -> 1.29 us  [exchange(): lax.ppermute(kept, 'col', beyond)]
    ppermute x2, waiting for transfers between devices: 3.11 us -> 12.6 us  [the longest x1 10.5 us: on_device(): lax.ppermute(beside, 'col', [(i, i ^ 1) for i in range(col_devices)])]
    ppermute x3, starting transfers between devices: 2.42 us -> 5.04 us  [exchange(): lax.ppermute(kept, 'col', beyond)]
    all_to_all x1, starting transfers between devices: 3.34 us -> 4.82 us  [on_device(): shares = lax.all_to_all(partial_sums, ('row', 'col'), 0, 0, tiled=True)]
    ppermute x2, starting transfers between devices: 2.98 us -> 4.01 us  [the longest x1 2.7 us: on_device(): lax.ppermute(across, 'col', [(i, (i - 1 + 2 * (i % 2)) % col_devices) for...]
    ppermute x1, waiting for transfers between devices: 0.99 us -> 0.01 us  [on_device(): below = lax.ppermute(leading, 'row', ring(row_devices, -1))]
  transfers between devices with their start and end apart: 11 -> 11, of which waited for: 7 -> 6; matrix products, arithmetic and copies ran while one was open for 0% -> 0% of each run, Pallas kernels for 23% -> 18%
where the time goes in v7:
time: 69.4 us; the launch traced here: 69.2 us
  Pallas kernels  26.3 us (38%)
  starting transfers between devices  21.8 us (31%)
  waiting for transfers between devices  19.8 us (29%)
  between operations  0.72 us (1%)
    pallas_call x7, Pallas kernels, call(): pl.pallas_call(kernel, in_specs=specs, out_specs=jax.tree.map(lambda _: v...  23.8 us
    ppermute x1, waiting for transfers between devices, on_device(): lax.ppermute(beside, 'col', [(i, i ^ 1) for i in range(col_devices)])  10.5 us
    ppermute x3, starting transfers between devices, exchange(): lax.ppermute(kept, 'col', beyond)  5.04 us
    ppermute x3, starting transfers between devices, exchange(): lax.ppermute(given, 'col', beside)  4.98 us
    all_to_all x1, starting transfers between devices, on_device(): shares = lax.all_to_all(partial_sums, ('row', 'col'), 0, 0, tiled=True)  4.82 us
    all_to_all x1, waiting for transfers between devices, on_device(): shares = lax.all_to_all(partial_sums, ('row', 'col'), 0, 0, tiled=True)  4.64 us
    ppermute x1, starting transfers between devices, on_device(): below = lax.ppermute(leading, 'row', ring(row_devices, -1))  2.98 us
    ppermute x1, starting transfers between devices, on_device(): lax.ppermute(across, 'col', [(i, (i - 1 + 2 * (i % 2)) % col_devices) for...  2.7 us
  transfers between devices with their start and end apart: 11, of which 6 were waited for; matrix products, arithmetic and copies ran while one was open for 0% of the time, Pallas kernels for 18%

profile of v7, /device:TPU:0, one launch (start us, length us, event | category | flops | bytes accessed | tf_op | source)
XLA Modules:
  0.0 69.2 jit_solution(1114841385474266441)
XLA Ops:
  0.6 6.1 %shard_map.59 = (s32[5,32,2048]{2,1,0:T(8,128)S(1)}, bf16[32,2048]{1,0:T(8,128)(2,1)S(1)}, bf16[32,2048]{1,0:T(8,128)(2,1)S(1)}, bf16[6,160,256]{2,1,0:T(8,128)(2,1)S(1)}, bf16[6,160,256]{2,1,0:T(8,128)(2,1)S(1)}) custom-call(s32[1]{0:T(128)} %bitcast.odd_ref, f32[2]{0:T(128)} %bar_hbm.1, s32[640,2048]{1,0:T(8,128)} %spins_hbm.3, f32[2,640,2048]{2,1,0:T(8,128)} %draws_hbm.3, ...), custom_call_target="tpu_custom_call" | custom-call | flops 31457280 | bytes 9437184 | tf_op jit(solution)/shard_map/pallas_call | solution.py:533
  6.7 4.7 %shard_map.60 = (s32[5,32,2048]{2,1,0:T(8,128)S(1)}, bf16[6,128,256]{2,1,0:T(8,128)(2,1)S(1)}, bf16[6,128,256]{2,1,0:T(8,128)(2,1)S(1)}) custom-call(s32[1]{0:T(128)} %bitcast.odd_ref, f32[2]{0:T(128)} %bar_hbm.1, s32[640,2048]{1,0:T(8,128)} %spins_hbm.3, f32[2,640,2048]{2,1,0:T(8,128)} %draws_hbm.3, bf16[640,2048]{1,0:T(8,128)(2,1)} %moments_hbm.5, ...), custom_call_target="tpu_custom_call" | custom-call | flops 20971520 | bytes 6291456 | tf_op jit(solution)/shard_map/pallas_call | solution.py:533
  11.4 3.0 %collective-permute-start.4 = (bf16[6,128,256]{2,1,0:T(8,128)(2,1)S(1)}, bf16[6,128,256]{2,1,0:T(8,128)(2,1)S(1)}, u32[]{:S(2)}, u32[]{:S(2)}) collective-permute-start(bf16[6,128,256]{2,1,0:T(8,128)(2,1)S(1)} %get-tuple-element.27.refs_0_), channel_id=1, source_target_pairs={{0,1},{1,0},{2,3},{3,2},{4,5},{5,4},{6,7},{7,6},{8,9},{9,8},{10,11... | collective-permute-start | bytes 1179656 | tf_op jit(solution)/shard_map/ppermute | solution.py:530
  14.4 0.1 collective-permute-start.5
  14.6 1.9 %collective-permute-start.8 = (bf16[6,160,256]{2,1,0:T(8,128)(2,1)S(1)}, bf16[6,160,256]{2,1,0:T(8,128)(2,1)S(1)}, u32[]{:S(2)}, u32[]{:S(2)}) collective-permute-start(bf16[6,160,256]{2,1,0:T(8,128)(2,1)S(1)} %get-tuple-element.25.refs_4_.refs_1_), channel_id=1, source_target_pairs={{0,2},{1,3},{2,0},{3,1},{4,6},{5,7},{6,4},{7,5},{8,10},{9,11},{10,... | collective-permute-start | bytes 1474568 | tf_op jit(solution)/shard_map/ppermute | solution.py:530
  16.5 3.0 %collective-permute-start.1 = (bf16[32,2048]{1,0:T(8,128)(2,1)S(1)}, bf16[32,2048]{1,0:T(8,128)(2,1)S(1)}, u32[]{:S(2)}, u32[]{:S(2)}) collective-permute-start(bf16[32,2048]{1,0:T(8,128)(2,1)S(1)} %get-tuple-element.19), channel_id=1, source_target_pairs={{0,28},{4,0},{8,4},{12,8},{16,12},{20,16},{24,20},{28,24},{1,29},{... | collective-permute-start | bytes 393224 | tf_op jit(solution)/shard_map/ppermute | solution.py:573
  19.5 1.2 %collective-permute-done.above_ref = bf16[32,2048]{1,0:T(8,128)(2,1)S(1)} collective-permute-done((bf16[32,2048]{1,0:T(8,128)(2,1)S(1)}, bf16[32,2048]{1,0:T(8,128)(2,1)S(1)}, u32[]{:S(2)}, u32[]{:S(2)}) %collective-permute-start) | collective-permute-done | bytes 131104 | tf_op jit(solution)/shard_map/ppermute | solution.py:572
  20.6 1.6 %collective-permute-start.7 = (bf16[6,128,256]{2,1,0:T(8,128)(2,1)S(1)}, bf16[6,128,256]{2,1,0:T(8,128)(2,1)S(1)}, u32[]{:S(2)}, u32[]{:S(2)}) collective-permute-start(bf16[6,128,256]{2,1,0:T(8,128)(2,1)S(1)} %get-tuple-element.24.refs_3_.refs_0_), channel_id=1, source_target_pairs={{0,2},{1,3},{2,0},{3,1},{4,6},{5,7},{6,4},{7,5},{8,10},{9,11},{10,... | collective-permute-start | bytes 1179656 | tf_op jit(solution)/shard_map/ppermute | solution.py:530
  22.2 0.5 shard_map.61
  22.8 1.3 %collective-permute-start.2 = (bf16[96,128]{1,0:T(8,128)(2,1)S(1)}, bf16[96,128]{1,0:T(8,128)(2,1)S(1)}, u32[]{:S(2)}, u32[]{:S(2)}) collective-permute-start(bf16[96,128]{1,0:T(8,128)(2,1)S(1)} %get-tuple-element.21), channel_id=1, source_target_pairs={{0,1},{1,0},{2,3},{3,2},{4,5},{5,4},{6,7},{7,6},{8,9},{9,8},{10,11... | collective-permute-start | bytes 73736 | tf_op jit(solution)/shard_map/ppermute | solution.py:615
  24.1 10.5 %collective-permute-done.2.beside_ref = bf16[96,128]{1,0:T(8,128)(2,1)S(1)} collective-permute-done((bf16[96,128]{1,0:T(8,128)(2,1)S(1)}, bf16[96,128]{1,0:T(8,128)(2,1)S(1)}, u32[]{:S(2)}, u32[]{:S(2)}) %collective-permute-start.2) | collective-permute-done | bytes 24608 | tf_op jit(solution)/shard_map/ppermute | solution.py:615
  34.6 2.7 %collective-permute-start.3 = (bf16[96,128]{1,0:T(8,128)(2,1)S(1)}, bf16[96,128]{1,0:T(8,128)(2,1)S(1)}, u32[]{:S(2)}, u32[]{:S(2)}) collective-permute-start(bf16[96,128]{1,0:T(8,128)(2,1)S(1)} %get-tuple-element.22), channel_id=1, source_target_pairs={{0,3},{1,2},{2,1},{3,0},{4,7},{5,6},{6,5},{7,4},{8,11},{9,10},{10,... | collective-permute-start | bytes 73736 | tf_op jit(solution)/shard_map/ppermute | solution.py:612
  37.3 2.0 %collective-permute-done.3.across_ref = bf16[96,128]{1,0:T(8,128)(2,1)S(1)} collective-permute-done((bf16[96,128]{1,0:T(8,128)(2,1)S(1)}, bf16[96,128]{1,0:T(8,128)(2,1)S(1)}, u32[]{:S(2)}, u32[]{:S(2)}) %collective-permute-start.3) | collective-permute-done | bytes 24608 | tf_op jit(solution)/shard_map/ppermute | solution.py:612
  39.3 2.7 %shard_map.62 = (s32[32,2048]{1,0:T(8,128)S(1)}, bf16[832,256]{1,0:T(8,128)(2,1)S(1)}, bf16[832,256]{1,0:T(8,128)(2,1)S(1)}) custom-call(s32[1]{0:T(128)} %bitcast.odd_ref, s32[5,32,2048]{2,1,0:T(8,128)S(1)} %get-tuple-element.20.joined_ref, bf16[96,128]{1,0:T(8,128)(2,1)S(1)} %collective-permute-done.2.beside_ref, ...), custom_call_target="tpu_custom_call" | custom-call | flops 13107200 | bytes 1310720 | tf_op jit(solution)/shard_map/pallas_call | solution.py:533
  42.0 1.8 %collective-permute-start.6 = (bf16[832,256]{1,0:T(8,128)(2,1)S(1)}, bf16[832,256]{1,0:T(8,128)(2,1)S(1)}, u32[]{:S(2)}, u32[]{:S(2)}) collective-permute-start(bf16[832,256]{1,0:T(8,128)(2,1)S(1)} %get-tuple-element.29.refs_2_), channel_id=1, source_target_pairs={{0,1},{1,0},{2,3},{3,2},{4,5},{5,4},{6,7},{7,6},{8,9},{9,8},{10,11... | collective-permute-start | bytes 1277960 | tf_op jit(solution)/shard_map/ppermute | solution.py:530
  43.8 1.5 %collective-permute-start.9 = (bf16[832,256]{1,0:T(8,128)(2,1)S(1)}, bf16[832,256]{1,0:T(8,128)(2,1)S(1)}, u32[]{:S(2)}, u32[]{:S(2)}) collective-permute-start(bf16[832,256]{1,0:T(8,128)(2,1)S(1)} %get-tuple-element.26.refs_5_.refs_2_), channel_id=1, source_target_pairs={{0,2},{1,3},{2,0},{3,1},{4,6},{5,7},{6,4},{7,5},{8,10},{9,11},{10,... | collective-permute-start | bytes 1277960 | tf_op jit(solution)/shard_map/ppermute | solution.py:530
  45.4 3.9 %shard_map.63.refs_6_ = f32[8,2176]{1,0:T(8,128)S(1)} custom-call(bf16[6,128,256]{2,1,0:T(8,128)(2,1)S(1)} %get-tuple-element.27.refs_0_, bf16[6,160,256]{2,1,0:T(8,128)(2,1)S(1)} %get-tuple-element.28.refs_1_, bf16[832,256]{1,0:T(8,128)(2,1)S(1)} %get-tuple-element.29.refs_2_, bf16[6,128,256]{2,1,0:T(8,128)(2,1)S(1)} %get-tuple-element.24.refs_3_.refs_0_, ...), custom_call_target="tpu_custom_call" | custom-call | flops 2684354560 | bytes 2621440 | tf_op jit(solution)/shard_map/pallas_call | solution.py:533
  49.3 2.5 %shard_map.64.refs_9_ = f32[8,2176]{1,0:T(8,128)S(1)} custom-call(s32[1]{0:T(128)} %bitcast.odd_ref, bf16[6,128,256]{2,1,0:T(8,128)(2,1)S(1)} %get-tuple-element.24.refs_3_.refs_0_, bf16[6,160,256]{2,1,0:T(8,128)(2,1)S(1)} %get-tuple-element.25.refs_4_.refs_1_, bf16[6,128,256]{2,1,0:T(8,128)(2,1)S(1)} %collective-permute-done.4.refs_2_.refs_3_, ...), custom_call_target="tpu_custom_call" | custom-call | flops 1342177280 | bytes 2621440 | tf_op jit(solution)/shard_map/pallas_call | solution.py:533
  51.9 1.3 %collective-permute-done.9.refs_8_ = bf16[832,256]{1,0:T(8,128)(2,1)S(1)} collective-permute-done((bf16[832,256]{1,0:T(8,128)(2,1)S(1)}, bf16[832,256]{1,0:T(8,128)(2,1)S(1)}, u32[]{:S(2)}, u32[]{:S(2)}) %collective-permute-start.9) | collective-permute-done | bytes 426016 | tf_op jit(solution)/shard_map/ppermute | solution.py:530
  53.2 3.4 %shard_map.65 = f32[32,1,64]{2,1,0:T(1,128)} custom-call(s32[1]{0:T(128)} %bitcast.odd_ref, bf16[6,128,256]{2,1,0:T(8,128)(2,1)S(1)} %get-tuple-element.24.refs_3_.refs_0_, bf16[6,160,256]{2,1,0:T(8,128)(2,1)S(1)} %get-tuple-element.25.refs_4_.refs_1_, bf16[832,256]{1,0:T(8,128)(2,1)S(1)} %get-tuple-element.26.refs_5_.refs_2_, ...), custom_call_target="tpu_custom_call" | custom-call | flops 1342177280 | bytes 2621440 | tf_op jit(solution)/shard_map/pallas_call | solution.py:533
  56.6 4.8 %all-to-all-start = ((f32[32,1,64]{2,1,0:T(1,128)}), f32[32,1,64]{2,1,0:T(1,128)S(1)}, u32[]{:S(2)}, u32[]{:S(2)}) async-start(f32[32,1,64]{2,1,0:T(1,128)} %shard_map.65), calls=%async_computation | async-start | bytes 32768 | tf_op jit(solution)/shard_map/all_to_all | solution.py:687
  61.4 2.5 %spell.1 = f32[640,2048]{1,0:T(8,128)} custom-call(s32[32,2048]{1,0:T(8,128)S(1)} %get-tuple-element.23.spins_ref), custom_call_target="tpu_custom_call" | custom-call | flops 1310720 | bytes 5242880 | tf_op jit(solution)/shard_map/spell/pallas_call | solution.py:638
  64.0 4.6 %all-to-all-done = f32[32,1,64]{2,1,0:T(1,128)S(1)} async-done(((f32[32,1,64]{2,1,0:T(1,128)}), f32[32,1,64]{2,1,0:T(1,128)S(1)}, u32[]{:S(2)}, u32[]{:S(2)}) %all-to-all-start) | async-done | bytes 8224 | tf_op jit(solution)/shard_map/all_to_all | solution.py:687
  68.6 0.6 reduce_sum.9
  (7 shorter events, 0.1 us)
Async XLA Ops:
  11.4 32.4 %collective-permute-start.4 = (bf16[6,128,256]{2,1,0:T(8,128)(2,1)S(1)}, bf16[6,128,256]{2,1,0:T(8,128)(2,1)S(1)}, u32[]{:S(2)}, u32[]{:S(2)}) collective-permute-start(bf16[6,128,256]{2,1,0:T(8,128)(2,1)S(1)} %get-tuple-element.27.refs_0_), channel_id=1, source_target_pairs={{0,1},{1,0},{2,3},{3,2},{4,5},{5,4},{6,7},{7,6},{8,9},{9,8},{10,11... | collective-permute-start | bytes 1179656 | tf_op jit(solution)/shard_map/ppermute | solution.py:530
  14.4 6.2 %collective-permute-start = (bf16[32,2048]{1,0:T(8,128)(2,1)S(1)}, bf16[32,2048]{1,0:T(8,128)(2,1)S(1)}, u32[]{:S(2)}, u32[]{:S(2)}) collective-permute-start(bf16[32,2048]{1,0:T(8,128)(2,1)S(1)} %get-tuple-element.18), channel_id=1, source_target_pairs={{0,4},{4,8},{8,12},{12,16},{16,20},{20,24},{24,28},{28,0},{1,5},{5... | collective-permute-start | bytes 393224 | tf_op jit(solution)/shard_map/ppermute | solution.py:572
  14.4 34.8 %collective-permute-start.5 = (bf16[6,160,256]{2,1,0:T(8,128)(2,1)S(1)}, bf16[6,160,256]{2,1,0:T(8,128)(2,1)S(1)}, u32[]{:S(2)}, u32[]{:S(2)}) collective-permute-start(bf16[6,160,256]{2,1,0:T(8,128)(2,1)S(1)} %get-tuple-element.28.refs_1_), channel_id=1, source_target_pairs={{0,1},{1,0},{2,3},{3,2},{4,5},{5,4},{6,7},{7,6},{8,9},{9,8},{10,11... | collective-permute-start | bytes 1474568 | tf_op jit(solution)/shard_map/ppermute | solution.py:530
  14.6 34.7 %collective-permute-start.8 = (bf16[6,160,256]{2,1,0:T(8,128)(2,1)S(1)}, bf16[6,160,256]{2,1,0:T(8,128)(2,1)S(1)}, u32[]{:S(2)}, u32[]{:S(2)}) collective-permute-start(bf16[6,160,256]{2,1,0:T(8,128)(2,1)S(1)} %get-tuple-element.25.refs_4_.refs_1_), channel_id=1, source_target_pairs={{0,2},{1,3},{2,0},{3,1},{4,6},{5,7},{6,4},{7,5},{8,10},{9,11},{10,... | collective-permute-start | bytes 1474568 | tf_op jit(solution)/shard_map/ppermute | solution.py:530
  16.5 5.7 %collective-permute-start.1 = (bf16[32,2048]{1,0:T(8,128)(2,1)S(1)}, bf16[32,2048]{1,0:T(8,128)(2,1)S(1)}, u32[]{:S(2)}, u32[]{:S(2)}) collective-permute-start(bf16[32,2048]{1,0:T(8,128)(2,1)S(1)} %get-tuple-element.19), channel_id=1, source_target_pairs={{0,28},{4,0},{8,4},{12,8},{16,12},{20,16},{24,20},{28,24},{1,29},{... | collective-permute-start | bytes 393224 | tf_op jit(solution)/shard_map/ppermute | solution.py:573
  20.6 28.6 %collective-permute-start.7 = (bf16[6,128,256]{2,1,0:T(8,128)(2,1)S(1)}, bf16[6,128,256]{2,1,0:T(8,128)(2,1)S(1)}, u32[]{:S(2)}, u32[]{:S(2)}) collective-permute-start(bf16[6,128,256]{2,1,0:T(8,128)(2,1)S(1)} %get-tuple-element.24.refs_3_.refs_0_), channel_id=1, source_target_pairs={{0,2},{1,3},{2,0},{3,1},{4,6},{5,7},{6,4},{7,5},{8,10},{9,11},{10,... | collective-permute-start | bytes 1179656 | tf_op jit(solution)/shard_map/ppermute | solution.py:530
  22.8 11.8 %collective-permute-start.2 = (bf16[96,128]{1,0:T(8,128)(2,1)S(1)}, bf16[96,128]{1,0:T(8,128)(2,1)S(1)}, u32[]{:S(2)}, u32[]{:S(2)}) collective-permute-start(bf16[96,128]{1,0:T(8,128)(2,1)S(1)} %get-tuple-element.21), channel_id=1, source_target_pairs={{0,1},{1,0},{2,3},{3,2},{4,5},{5,4},{6,7},{7,6},{8,9},{9,8},{10,11... | collective-permute-start | bytes 73736 | tf_op jit(solution)/shard_map/ppermute | solution.py:615
  34.6 4.7 %collective-permute-start.3 = (bf16[96,128]{1,0:T(8,128)(2,1)S(1)}, bf16[96,128]{1,0:T(8,128)(2,1)S(1)}, u32[]{:S(2)}, u32[]{:S(2)}) collective-permute-start(bf16[96,128]{1,0:T(8,128)(2,1)S(1)} %get-tuple-element.22), channel_id=1, source_target_pairs={{0,3},{1,2},{2,1},{3,0},{4,7},{5,6},{6,5},{7,4},{8,11},{9,10},{10,... | collective-permute-start | bytes 73736 | tf_op jit(solution)/shard_map/ppermute | solution.py:612
  42.0 9.9 %collective-permute-start.6 = (bf16[832,256]{1,0:T(8,128)(2,1)S(1)}, bf16[832,256]{1,0:T(8,128)(2,1)S(1)}, u32[]{:S(2)}, u32[]{:S(2)}) collective-permute-start(bf16[832,256]{1,0:T(8,128)(2,1)S(1)} %get-tuple-element.29.refs_2_), channel_id=1, source_target_pairs={{0,1},{1,0},{2,3},{3,2},{4,5},{5,4},{6,7},{7,6},{8,9},{9,8},{10,11... | collective-permute-start | bytes 1277960 | tf_op jit(solution)/shard_map/ppermute | solution.py:530
  43.8 9.4 %collective-permute-start.9 = (bf16[832,256]{1,0:T(8,128)(2,1)S(1)}, bf16[832,256]{1,0:T(8,128)(2,1)S(1)}, u32[]{:S(2)}, u32[]{:S(2)}) collective-permute-start(bf16[832,256]{1,0:T(8,128)(2,1)S(1)} %get-tuple-element.26.refs_5_.refs_2_), channel_id=1, source_target_pairs={{0,2},{1,3},{2,0},{3,1},{4,6},{5,7},{6,4},{7,5},{8,10},{9,11},{10,... | collective-permute-start | bytes 1277960 | tf_op jit(solution)/shard_map/ppermute | solution.py:530
  56.6 12.0 %all-to-all-start = ((f32[32,1,64]{2,1,0:T(1,128)}), f32[32,1,64]{2,1,0:T(1,128)S(1)}, u32[]{:S(2)}, u32[]{:S(2)}) async-start(f32[32,1,64]{2,1,0:T(1,128)} %shard_map.65), calls=%async_computation | async-start | bytes 32768 | tf_op jit(solution)/shard_map/all_to_all | solution.py:687

commit v8 on v7

--- a/solution.py
+++ b/solution.py
@@ -220,6 +220,8 @@
     words_ref,
     given_ref,
     kept_ref,
+    given_rest_ref,
+    kept_rest_ref,
     spins_buf,
     draws_buf,
     moments_buf,
@@ -270,15 +272,21 @@
     final_ref[:, inner] = sweeps_of([words_ref[w, :, inner] for w in range(WORDS)])
     for copy in weights:
         copy.wait()
-    fill(
-        (given_ref, kept_ref),
-        odd_ref[0],
-        lambda lower: [1 + i + (planes - side - 2) * lower for i in range(side)],
-        lambda lower, i, t: moments_buf[
-            lower, i * DEPTH : (i + 1) * DEPTH, pl.ds((t + 1) * TILE, TILE)
-        ],
-        lambda t: final_ref[:, pl.ds((t + 1) * TILE, TILE)],
-    )
+    for refs, first, count in (
+        ((given_ref, kept_ref), 0, side - 1),
+        ((given_rest_ref, kept_rest_ref), side - 1, 1),
+    ):
+        fill(
+            refs,
+            odd_ref[0],
+            lambda lower: [1 + first + i + (planes - side - 2) * lower for i in range(count)],
+            lambda lower, i, t: moments_buf[
+                lower,
+                (first + i) * DEPTH : (first + i + 1) * DEPTH,
+                pl.ds((t + 1) * TILE, TILE),
+            ],
+            lambda t: final_ref[:, pl.ds((t + 1) * TILE, TILE)],
+        )
 
 
 def join_kernel(odd_ref, words_ref, above_ref, below_ref, joined_ref, beside_ref, across_ref, *, planes):
@@ -415,21 +423,41 @@
 
 
 def tile(block, t):
-    low, high, ends = block
-    tiles = low.shape[0] + 2
-    height = low.shape[1] + high.shape[1] + DEPTH
+    parts, ends, spans, edges = block
+    tiles = parts[0].shape[0] + 2
+    height = (ends.shape[0] - (tiles - 2) * DEPTH) // 2
     if t in (0, tiles - 1):
-        return ends[min(t, 1) * height : (min(t, 1) + 1) * height, :]
-    return jnp.concatenate([low[t - 1], high[t - 1], edge_rows(ends, tiles, t, t + 1)], axis=0)
+        base = min(t, 1) * height
+        return jnp.concatenate([ends[base + a : base + b, :] for a, b in spans], axis=0)
+    rows = [part[t - 1] for part in parts]
+    if edges:
+        rows.append(edge_rows(ends, tiles, t, t + 1))
+    return jnp.concatenate(rows, axis=0)
 
 
 def tiles_of(block, places):
     return jnp.concatenate([tile(block, t) for t in places], axis=0)
 
 
+def whole(parts):
+    low, rest, high, ends = parts
+    return (low, rest, high), ends, ((0, low.shape[1] + rest.shape[1] + high.shape[1] + DEPTH),), True
+
+
+def without_rest(parts):
+    low, rest, high, ends = parts
+    held = low.shape[1] + rest.shape[1]
+    return (low, high), ends, ((0, low.shape[1]), (held, held + high.shape[1] + DEPTH)), True
+
+
+def rest_only(parts):
+    low, rest, _, ends = parts
+    return (rest,), ends, ((low.shape[1], low.shape[1] + rest.shape[1]),), False
+
+
 def own_kernel(*refs):
     parts, (out_ref, sums_ref) = refs[:-2], refs[-2:]
-    blocks = (parts[:3], parts[3:])
+    blocks = (whole(parts[:4]), whole(parts[4:]))
     tiles = parts[0].shape[0] + 2
     for n in range(tiles):
         sums_ref[:, n * TILE : (n + 1) * TILE] = sum(
@@ -465,32 +493,44 @@
     out_ref[...] = fold(sums_ref) + base_ref[...]
 
 
-def late_kernel(scale, odd_ref, *refs):
+def late_kernel(odd_ref, *refs):
     (base_ref, out_ref, sums_ref) = refs[-3:]
     tiles = refs[0].shape[0] + 2
     sums_ref[:, :TILE] = jnp.zeros((TILE, TILE), jnp.float32)
 
     def run(pairs):
+        pairs = [tuple(without_rest(part) for part in pair) for pair in pairs]
         for n in range(1, tiles + 1):
             places = [(tiles - 1, n - 1)] + ([(tiles - n, 0)] if n > 1 else [])
-            inner = n > 2
-            sums_ref[:, n * TILE : (n + 1) * TILE] = sum(
-                gram(
-                    jnp.concatenate(
-                        [tile(left, t) for t, _ in places]
-                        + ([edge_rows(left[2], tiles, tiles + 1 - n, tiles - 1)] if inner else []),
-                        axis=0,
-                    ),
-                    jnp.concatenate(
-                        [tile(right, q) for _, q in places]
-                        + ([edge_rows(right[2], tiles, 1, n - 1)] if inner else []),
-                        axis=0,
-                    ),
-                )
-                for left, right in pairs
+            total = 0.0
+            for left, right in pairs:
+                lefts, rights = [tile(left, t) for t, _ in places], [tile(right, q) for _, q in places]
+                if n > 2:
+                    lefts.append(edge_rows(left[1], tiles, tiles + 1 - n, tiles - 1))
+                    rights.append(edge_rows(right[1], tiles, 1, n - 1))
+                total += gram(jnp.concatenate(lefts, axis=0), jnp.concatenate(rights, axis=0))
+            sums_ref[:, n * TILE : (n + 1) * TILE] = total
+
+    by_side(odd_ref, refs[0:4], refs[4:8], refs[8:12], run)
+    out_ref[...] = fold(sums_ref) + base_ref[...]
+
+
+def last_kernel(scale, odd_ref, *refs):
+    (base_ref, out_ref, sums_ref) = refs[-3:]
+    tiles = refs[0].shape[0] + 2
+    sums_ref[:, :TILE] = jnp.zeros((TILE, TILE), jnp.float32)
+
+    def run(pairs):
+        pairs = [tuple(rest_only(part) for part in pair) for pair in pairs]
+        for n in range(1, tiles + 1):
+            sums_ref[:, n * TILE : (n + 1) * TILE] = gram(
+                jnp.concatenate(
+                    [tiles_of(left, range(tiles - n, tiles)) for left, _ in pairs], axis=0
+                ),
+                jnp.concatenate([tiles_of(right, range(n)) for _, right in pairs], axis=0),
             )
 
-    by_side(odd_ref, refs[0:3], refs[3:6], refs[6:9], run)
+    by_side(odd_ref, refs[0:4], refs[4:8], refs[8:12], run)
     value = fold(sums_ref) + base_ref[...]
     for height in (4, 2, 1):
         value = value + pltpu.roll(pltpu.roll(value, value.shape[1] - height, 1), 8 - height, 0)
@@ -571,11 +611,11 @@
     got = [*exchange(given, kept)]
     above = lax.ppermute(last, "row", ring(row_devices, 1))
     below = lax.ppermute(leading, "row", ring(row_devices, -1))
-    low = message(tiles - 2, side * DEPTH)
-    words, given, kept = call(
+    low, rest = message(tiles - 2, (side - 1) * DEPTH), message(tiles - 2, DEPTH)
+    words, given, kept, given_rest, kept_rest = call(
         outer_kernel,
         [smem, anywhere, anywhere, anywhere, anywhere, vmem],
-        [words_shape, low, low],
+        [words_shape, low, low, rest, rest],
         [
             pltpu.VMEM((remaining, columns), jnp.int32),
             pltpu.VMEM((SWEEPS, remaining, columns), jnp.float32),
@@ -594,9 +634,9 @@
         moments,
         words,
     )
-    own = [given, own[0], kept, own[1]]
     mid, far = exchange(given, kept)
-    got = [mid, got[0], far, got[1]]
+    given, kept = [given, given_rest, own[0]], [kept, kept_rest, own[1]]
+    got = [[mid, got[0]], [far, got[1]]]
     joined, beside, across = call(
         functools.partial(join_kernel, planes=planes),
         [smem, vmem, vmem, vmem],
@@ -614,7 +654,7 @@
     )
     beside = lax.ppermute(beside, "col", [(i, i ^ 1) for i in range(col_devices)])
     ends = jax.ShapeDtypeStruct((2 * half_rows + (tiles - 2) * DEPTH, TILE), jnp.bfloat16)
-    spins, given, kept = call(
+    spins, given_ends, kept_ends = call(
         side_kernel,
         [smem, vmem, vmem, vmem, anywhere],
         [jax.ShapeDtypeStruct((DEPTH, columns), jnp.int32), ends, ends],
@@ -632,8 +672,9 @@
         across,
         moments,
     )
-    own = [own[0], own[1], given, own[2], own[3], kept]
-    mid, far = exchange(given, kept)
+    given, kept = given + [given_ends], kept + [kept_ends]
+    mid_ends, far_ends = exchange(given_ends, kept_ends)
+    mid_rest, far_rest = exchange(given_rest, kept_rest)
 
     spins_out = pl.pallas_call(
         spell_kernel,
@@ -651,7 +692,7 @@
     sums = pltpu.VMEM((TILE, R + TILE), jnp.float32)
     folded = jax.ShapeDtypeStruct((8, R + LANES), jnp.float32)
     work = rows * columns * columns
-    base = call(own_kernel, [vmem] * 6, folded, [sums], work, 2 * rows * columns, *own)
+    base = call(own_kernel, [vmem] * 8, folded, [sums], work, 2 * rows * columns, *given, *kept)
     base = call(
         early_kernel,
         [smem] + [vmem] * 7,
@@ -660,28 +701,48 @@
         work // 2,
         2 * rows * columns,
         odd,
-        own[3],
-        own[4],
-        *got,
+        kept[0],
+        kept[2],
+        *got[0],
+        *got[1],
         base,
     )
-    partial_sums = call(
-        functools.partial(late_kernel, normaliser),
-        [smem] + [vmem] * 10,
-        jax.ShapeDtypeStruct((devices, 1, R // devices), jnp.float32),
+    base = call(
+        late_kernel,
+        [smem] + [vmem] * 13,
+        folded,
         [sums],
         work // 2,
         2 * rows * columns,
         odd,
-        own[3],
-        own[4],
-        own[5],
-        got[0],
-        got[1],
-        mid,
-        got[2],
-        got[3],
-        far,
+        *kept,
+        got[0][0],
+        given_rest,
+        got[0][1],
+        mid_ends,
+        got[1][0],
+        kept_rest,
+        got[1][1],
+        far_ends,
+        base,
+    )
+    partial_sums = call(
+        functools.partial(last_kernel, normaliser),
+        [smem] + [vmem] * 13,
+        jax.ShapeDtypeStruct((devices, 1, R // devices), jnp.float32),
+        [sums],
+        work // 8,
+        rows * columns,
+        odd,
+        *kept,
+        got[0][0],
+        mid_rest,
+        got[0][1],
+        mid_ends,
+        got[1][0],
+        far_rest,
+        got[1][1],
+        far_ends,
         base,
     )
     shares = lax.all_to_all(partial_sums, ("row", "col"), 0, 0, tiled=True)

time: 69.4 us -> 75.1 us (1.082)
  waiting for transfers between devices: 19.8 us -> 26.1 us
  starting transfers between devices: 21.8 us -> 20.7 us
    ppermute x3 -> x4, waiting for transfers between devices: 1.29 us -> 9.31 us  [exchange(): lax.ppermute(kept, 'col', beyond)]
    ppermute x1, starting transfers between devices: 2.7 us -> 0.02 us  [on_device(): lax.ppermute(across, 'col', [(i, (i - 1 + 2 * (i % 2)) % col_devices) for...]
    ppermute x1, waiting for transfers between devices: 10.5 us -> 7.87 us  [on_device(): lax.ppermute(beside, 'col', [(i, i ^ 1) for i in range(col_devices)])]
    ppermute x3 -> x4, starting transfers between devices: 4.98 us -> 6.75 us  [exchange(): lax.ppermute(given, 'col', beside)]
    ppermute x1, waiting for transfers between devices: 1.15 us -> 2.74 us  [on_device(): above = lax.ppermute(last, 'row', ring(row_devices, 1))]
    ppermute x3 -> x4, starting transfers between devices: 5.04 us -> 3.92 us  [exchange(): lax.ppermute(kept, 'col', beyond)]
    pallas_call x7 -> x8, Pallas kernels: 23.8 us -> 24.3 us  [call(): pl.pallas_call(kernel, in_specs=specs, out_specs=jax.tree.map(lambda _: v...]
  transfers between devices with their start and end apart: 11 -> 13, of which waited for: 6 -> 5; matrix products, arithmetic and copies ran while one was open for 0% -> 0% of each run, Pallas kernels for 18% -> 19%
where the time goes in v8:
time: 75.1 us; the launch traced here: 74.9 us
  Pallas kernels  26.8 us (36%)
  waiting for transfers between devices  26.1 us (35%)
  starting transfers between devices  20.7 us (28%)
    pallas_call x8, Pallas kernels, call(): pl.pallas_call(kernel, in_specs=specs, out_specs=jax.tree.map(lambda _: v...  24.3 us
    ppermute x4, waiting for transfers between devices, exchange(): lax.ppermute(kept, 'col', beyond)  9.31 us
    ppermute x1, waiting for transfers between devices, on_device(): lax.ppermute(beside, 'col', [(i, i ^ 1) for i in range(col_devices)])  7.87 us
    ppermute x4, starting transfers between devices, exchange(): lax.ppermute(given, 'col', beside)  6.75 us
    all_to_all x1, starting transfers between devices, on_device(): shares = lax.all_to_all(partial_sums, ('row', 'col'), 0, 0, tiled=True)  4.93 us
    all_to_all x1, waiting for transfers between devices, on_device(): shares = lax.all_to_all(partial_sums, ('row', 'col'), 0, 0, tiled=True)  4.67 us
    ppermute x4, starting transfers between devices, exchange(): lax.ppermute(kept, 'col', beyond)  3.92 us
    ppermute x1, starting transfers between devices, on_device(): below = lax.ppermute(leading, 'row', ring(row_devices, -1))  3.54 us
  transfers between devices with their start and end apart: 13, of which 5 were waited for; matrix products, arithmetic and copies ran while one was open for 0% of the time, Pallas kernels for 19%

profile of v8, /device:TPU:0, one launch (start us, length us, event | category | flops | bytes accessed | tf_op | source)
XLA Modules:
  0.0 74.9 jit_solution(13721673374418520348)
XLA Ops:
  0.6 6.1 %shard_map.59 = (s32[5,32,2048]{2,1,0:T(8,128)S(1)}, bf16[32,2048]{1,0:T(8,128)(2,1)S(1)}, bf16[32,2048]{1,0:T(8,128)(2,1)S(1)}, bf16[6,160,256]{2,1,0:T(8,128)(2,1)S(1)}, bf16[6,160,256]{2,1,0:T(8,128)(2,1)S(1)}) custom-call(s32[1]{0:T(128)} %bitcast.odd_ref, f32[2]{0:T(128)} %bar_hbm.1, s32[640,2048]{1,0:T(8,128)} %spins_hbm.3, f32[2,640,2048]{2,1,0:T(8,128)} %draws_hbm.3, ...), custom_call_target="tpu_custom_call" | custom-call | flops 31457280 | bytes 9437184 | tf_op jit(solution)/shard_map/pallas_call | solution.py:573
  6.7 4.7 %shard_map.60 = (s32[5,32,2048]{2,1,0:T(8,128)S(1)}, bf16[6,96,256]{2,1,0:T(8,128)(2,1)S(1)}, bf16[6,96,256]{2,1,0:T(8,128)(2,1)S(1)}, bf16[6,32,256]{2,1,0:T(8,128)(2,1)S(1)}, bf16[6,32,256]{2,1,0:T(8,128)(2,1)S(1)}) custom-call(s32[1]{0:T(128)} %bitcast.odd_ref, f32[2]{0:T(128)} %bar_hbm.1, s32[640,2048]{1,0:T(8,128)} %spins_hbm.3, ...), custom_call_target="tpu_custom_call" | custom-call | flops 20971520 | bytes 6291456 | tf_op jit(solution)/shard_map/pallas_call | solution.py:573
  11.4 3.0 %collective-permute-start.4 = (bf16[6,96,256]{2,1,0:T(8,128)(2,1)S(1)}, bf16[6,96,256]{2,1,0:T(8,128)(2,1)S(1)}, u32[]{:S(2)}, u32[]{:S(2)}) collective-permute-start(bf16[6,96,256]{2,1,0:T(8,128)(2,1)S(1)} %get-tuple-element.30.refs_0_), channel_id=1, source_target_pairs={{0,1},{1,0},{2,3},{3,2},{4,5},{5,4},{6,7},{7,6},{8,9},{9,8},{10,11... | collective-permute-start | bytes 884744 | tf_op jit(solution)/shard_map/ppermute | solution.py:570
  14.4 1.5 %collective-permute-start.10 = (bf16[6,160,256]{2,1,0:T(8,128)(2,1)S(1)}, bf16[6,160,256]{2,1,0:T(8,128)(2,1)S(1)}, u32[]{:S(2)}, u32[]{:S(2)}) collective-permute-start(bf16[6,160,256]{2,1,0:T(8,128)(2,1)S(1)} %get-tuple-element.28.refs_6_.refs_1_.refs_2_), channel_id=1, source_target_pairs={{0,2},{1,3},{2,0},{3,1},{4,6},{5,7},{6,4},{7,5},{8,10},{9,11},{10,... | collective-permute-start | bytes 1474568 | tf_op jit(solution)/shard_map/ppermute | solution.py:570
  16.0 0.5 collective-permute-start.6
  16.5 3.5 %collective-permute-start.1 = (bf16[32,2048]{1,0:T(8,128)(2,1)S(1)}, bf16[32,2048]{1,0:T(8,128)(2,1)S(1)}, u32[]{:S(2)}, u32[]{:S(2)}) collective-permute-start(bf16[32,2048]{1,0:T(8,128)(2,1)S(1)} %get-tuple-element.21), channel_id=1, source_target_pairs={{0,28},{4,0},{8,4},{12,8},{16,12},{20,16},{24,20},{28,24},{1,29},{... | collective-permute-start | bytes 393224 | tf_op jit(solution)/shard_map/ppermute | solution.py:613
  20.0 2.7 %collective-permute-done.above_ref = bf16[32,2048]{1,0:T(8,128)(2,1)S(1)} collective-permute-done((bf16[32,2048]{1,0:T(8,128)(2,1)S(1)}, bf16[32,2048]{1,0:T(8,128)(2,1)S(1)}, u32[]{:S(2)}, u32[]{:S(2)}) %collective-permute-start) | collective-permute-done | bytes 131104 | tf_op jit(solution)/shard_map/ppermute | solution.py:612
  22.8 0.5 shard_map.61
  23.3 1.6 %collective-permute-start.2 = (bf16[96,128]{1,0:T(8,128)(2,1)S(1)}, bf16[96,128]{1,0:T(8,128)(2,1)S(1)}, u32[]{:S(2)}, u32[]{:S(2)}) collective-permute-start(bf16[96,128]{1,0:T(8,128)(2,1)S(1)} %get-tuple-element.23), channel_id=1, source_target_pairs={{0,1},{1,0},{2,3},{3,2},{4,5},{5,4},{6,7},{7,6},{8,9},{9,8},{10,11... | collective-permute-start | bytes 73736 | tf_op jit(solution)/shard_map/ppermute | solution.py:655
  24.9 7.9 %collective-permute-done.2.beside_ref = bf16[96,128]{1,0:T(8,128)(2,1)S(1)} collective-permute-done((bf16[96,128]{1,0:T(8,128)(2,1)S(1)}, bf16[96,128]{1,0:T(8,128)(2,1)S(1)}, u32[]{:S(2)}, u32[]{:S(2)}) %collective-permute-start.2) | collective-permute-done | bytes 24608 | tf_op jit(solution)/shard_map/ppermute | solution.py:655
  32.8 1.5 %collective-permute-done.3.across_ref = bf16[96,128]{1,0:T(8,128)(2,1)S(1)} collective-permute-done((bf16[96,128]{1,0:T(8,128)(2,1)S(1)}, bf16[96,128]{1,0:T(8,128)(2,1)S(1)}, u32[]{:S(2)}, u32[]{:S(2)}) %collective-permute-start.3) | collective-permute-done | bytes 24608 | tf_op jit(solution)/shard_map/ppermute | solution.py:652
  34.2 2.7 %shard_map.62 = (s32[32,2048]{1,0:T(8,128)S(1)}, bf16[832,256]{1,0:T(8,128)(2,1)S(1)}, bf16[832,256]{1,0:T(8,128)(2,1)S(1)}) custom-call(s32[1]{0:T(128)} %bitcast.odd_ref, s32[5,32,2048]{2,1,0:T(8,128)S(1)} %get-tuple-element.22.joined_ref, bf16[96,128]{1,0:T(8,128)(2,1)S(1)} %collective-permute-done.2.beside_ref, ...), custom_call_target="tpu_custom_call" | custom-call | flops 13107200 | bytes 1310720 | tf_op jit(solution)/shard_map/pallas_call | solution.py:573
  37.3 1.7 %collective-permute-start.7 = (bf16[832,256]{1,0:T(8,128)(2,1)S(1)}, bf16[832,256]{1,0:T(8,128)(2,1)S(1)}, u32[]{:S(2)}, u32[]{:S(2)}) collective-permute-start(bf16[832,256]{1,0:T(8,128)(2,1)S(1)} %get-tuple-element.33.refs_3_), channel_id=1, source_target_pairs={{0,1},{1,0},{2,3},{3,2},{4,5},{5,4},{6,7},{7,6},{8,9},{9,8},{10,11... | collective-permute-start | bytes 1277960 | tf_op jit(solution)/shard_map/ppermute | solution.py:570
  39.0 1.5 %collective-permute-start.8 = (bf16[6,96,256]{2,1,0:T(8,128)(2,1)S(1)}, bf16[6,96,256]{2,1,0:T(8,128)(2,1)S(1)}, u32[]{:S(2)}, u32[]{:S(2)}) collective-permute-start(bf16[6,96,256]{2,1,0:T(8,128)(2,1)S(1)} %get-tuple-element.26.refs_4_.refs_0_), channel_id=1, source_target_pairs={{0,2},{1,3},{2,0},{3,1},{4,6},{5,7},{6,4},{7,5},{8,10},{9,11},{10,... | collective-permute-start | bytes 884744 | tf_op jit(solution)/shard_map/ppermute | solution.py:570
  40.5 3.9 %shard_map.63.refs_6_ = f32[8,2176]{1,0:T(8,128)S(1)} custom-call(bf16[6,96,256]{2,1,0:T(8,128)(2,1)S(1)} %get-tuple-element.30.refs_0_, bf16[6,32,256]{2,1,0:T(8,128)(2,1)S(1)} %get-tuple-element.31.refs_1_.refs_5_, bf16[6,160,256]{2,1,0:T(8,128)(2,1)S(1)} %get-tuple-element.32.refs_2_, bf16[832,256]{1,0:T(8,128)(2,1)S(1)} %get-tuple-element.33.refs_3_, ...), custom_call_target="tpu_custom_call" | custom-call | flops 2684354560 | bytes 2621440 | tf_op jit(solution)/shard_map/pallas_call | solution.py:573
  44.4 9.3 %collective-permute-done.8.refs_4_.refs_8_ = bf16[6,96,256]{2,1,0:T(8,128)(2,1)S(1)} collective-permute-done((bf16[6,96,256]{2,1,0:T(8,128)(2,1)S(1)}, bf16[6,96,256]{2,1,0:T(8,128)(2,1)S(1)}, u32[]{:S(2)}, u32[]{:S(2)}) %collective-permute-start.8) | collective-permute-done | bytes 294944 | tf_op jit(solution)/shard_map/ppermute | solution.py:570
  53.7 1.5 %collective-permute-start.5 = (bf16[6,32,256]{2,1,0:T(8,128)(2,1)S(1)}, bf16[6,32,256]{2,1,0:T(8,128)(2,1)S(1)}, u32[]{:S(2)}, u32[]{:S(2)}) collective-permute-start(bf16[6,32,256]{2,1,0:T(8,128)(2,1)S(1)} %get-tuple-element.31.refs_1_.refs_5_), channel_id=1, source_target_pairs={{0,1},{1,0},{2,3},{3,2},{4,5},{5,4},{6,7},{7,6},{8,9},{9,8},{10,11... | collective-permute-start | bytes 294920 | tf_op jit(solution)/shard_map/ppermute | solution.py:570
  55.7 2.1 %shard_map.64.refs_12_ = f32[8,2176]{1,0:T(8,128)S(1)} custom-call(s32[1]{0:T(128)} %bitcast.odd_ref, bf16[6,96,256]{2,1,0:T(8,128)(2,1)S(1)} %get-tuple-element.26.refs_4_.refs_0_, bf16[6,160,256]{2,1,0:T(8,128)(2,1)S(1)} %get-tuple-element.28.refs_6_.refs_1_.refs_2_, bf16[6,96,256]{2,1,0:T(8,128)(2,1)S(1)} %collective-permute-done.4.refs_2_.refs_4_, ...), custom_call_target="tpu_custom_call" | custom-call | flops 1342177280 | bytes 2621440 | tf_op jit(solution)/shard_map/pallas_call | solution.py:573
  57.9 2.5 %shard_map.65.refs_12_ = f32[8,2176]{1,0:T(8,128)S(1)} custom-call(s32[1]{0:T(128)} %bitcast.odd_ref, bf16[6,96,256]{2,1,0:T(8,128)(2,1)S(1)} %get-tuple-element.26.refs_4_.refs_0_, bf16[6,32,256]{2,1,0:T(8,128)(2,1)S(1)} %get-tuple-element.27.refs_5_.refs_1_.refs_9_, bf16[6,160,256]{2,1,0:T(8,128)(2,1)S(1)} %get-tuple-element.28.refs_6_.refs_1_.refs_2_, ...), custom_call_target="tpu_custom_call" | custom-call | flops 1342177280 | bytes 2621440 | tf_op jit(solution)/shard_map/pallas_call | solution.py:573
  60.3 1.9 %shard_map.66 = f32[32,1,64]{2,1,0:T(1,128)} custom-call(s32[1]{0:T(128)} %bitcast.odd_ref, bf16[6,96,256]{2,1,0:T(8,128)(2,1)S(1)} %get-tuple-element.26.refs_4_.refs_0_, bf16[6,32,256]{2,1,0:T(8,128)(2,1)S(1)} %get-tuple-element.27.refs_5_.refs_1_.refs_9_, bf16[6,160,256]{2,1,0:T(8,128)(2,1)S(1)} %get-tuple-element.28.refs_6_.refs_1_.refs_2_, ...), custom_call_target="tpu_custom_call" | custom-call | flops 335544320 | bytes 1310720 | tf_op jit(solution)/shard_map/pallas_call | solution.py:573
  62.2 4.9 %all-to-all-start = ((f32[32,1,64]{2,1,0:T(1,128)}), f32[32,1,64]{2,1,0:T(1,128)S(1)}, u32[]{:S(2)}, u32[]{:S(2)}) async-start(f32[32,1,64]{2,1,0:T(1,128)} %shard_map.66), calls=%async_computation | async-start | bytes 32768 | tf_op jit(solution)/shard_map/all_to_all | solution.py:748
  67.1 2.5 %spell.1 = f32[640,2048]{1,0:T(8,128)} custom-call(s32[32,2048]{1,0:T(8,128)S(1)} %get-tuple-element.25.spins_ref), custom_call_target="tpu_custom_call" | custom-call | flops 1310720 | bytes 5242880 | tf_op jit(solution)/shard_map/spell/pallas_call | solution.py:679
  69.7 4.7 %all-to-all-done = f32[32,1,64]{2,1,0:T(1,128)S(1)} async-done(((f32[32,1,64]{2,1,0:T(1,128)}), f32[32,1,64]{2,1,0:T(1,128)S(1)}, u32[]{:S(2)}, u32[]{:S(2)}) %all-to-all-start) | async-done | bytes 8224 | tf_op jit(solution)/shard_map/all_to_all | solution.py:748
  74.3 0.6 reduce_sum.9
  (12 shorter events, 0.9 us)
Async XLA Ops:
  11.4 27.6 %collective-permute-start.4 = (bf16[6,96,256]{2,1,0:T(8,128)(2,1)S(1)}, bf16[6,96,256]{2,1,0:T(8,128)(2,1)S(1)}, u32[]{:S(2)}, u32[]{:S(2)}) collective-permute-start(bf16[6,96,256]{2,1,0:T(8,128)(2,1)S(1)} %get-tuple-element.30.refs_0_), channel_id=1, source_target_pairs={{0,1},{1,0},{2,3},{3,2},{4,5},{5,4},{6,7},{7,6},{8,9},{9,8},{10,11... | collective-permute-start | bytes 884744 | tf_op jit(solution)/shard_map/ppermute | solution.py:570
  14.4 40.8 %collective-permute-start.10 = (bf16[6,160,256]{2,1,0:T(8,128)(2,1)S(1)}, bf16[6,160,256]{2,1,0:T(8,128)(2,1)S(1)}, u32[]{:S(2)}, u32[]{:S(2)}) collective-permute-start(bf16[6,160,256]{2,1,0:T(8,128)(2,1)S(1)} %get-tuple-element.28.refs_6_.refs_1_.refs_2_), channel_id=1, source_target_pairs={{0,2},{1,3},{2,0},{3,1},{4,6},{5,7},{6,4},{7,5},{8,10},{9,11},{10,... | collective-permute-start | bytes 1474568 | tf_op jit(solution)/shard_map/ppermute | solution.py:570
  16.0 39.8 %collective-permute-start.6 = (bf16[6,160,256]{2,1,0:T(8,128)(2,1)S(1)}, bf16[6,160,256]{2,1,0:T(8,128)(2,1)S(1)}, u32[]{:S(2)}, u32[]{:S(2)}) collective-permute-start(bf16[6,160,256]{2,1,0:T(8,128)(2,1)S(1)} %get-tuple-element.32.refs_2_), channel_id=1, source_target_pairs={{0,1},{1,0},{2,3},{3,2},{4,5},{5,4},{6,7},{7,6},{8,9},{9,8},{10,11... | collective-permute-start | bytes 1474568 | tf_op jit(solution)/shard_map/ppermute | solution.py:570
  16.5 6.3 %collective-permute-start = (bf16[32,2048]{1,0:T(8,128)(2,1)S(1)}, bf16[32,2048]{1,0:T(8,128)(2,1)S(1)}, u32[]{:S(2)}, u32[]{:S(2)}) collective-permute-start(bf16[32,2048]{1,0:T(8,128)(2,1)S(1)} %get-tuple-element.20), channel_id=1, source_target_pairs={{0,4},{4,8},{8,12},{12,16},{16,20},{20,24},{24,28},{28,0},{1,5},{5... | collective-permute-start | bytes 393224 | tf_op jit(solution)/shard_map/ppermute | solution.py:612
  16.5 6.3 %collective-permute-start.1 = (bf16[32,2048]{1,0:T(8,128)(2,1)S(1)}, bf16[32,2048]{1,0:T(8,128)(2,1)S(1)}, u32[]{:S(2)}, u32[]{:S(2)}) collective-permute-start(bf16[32,2048]{1,0:T(8,128)(2,1)S(1)} %get-tuple-element.21), channel_id=1, source_target_pairs={{0,28},{4,0},{8,4},{12,8},{16,12},{20,16},{24,20},{28,24},{1,29},{... | collective-permute-start | bytes 393224 | tf_op jit(solution)/shard_map/ppermute | solution.py:613
  23.3 9.4 %collective-permute-start.2 = (bf16[96,128]{1,0:T(8,128)(2,1)S(1)}, bf16[96,128]{1,0:T(8,128)(2,1)S(1)}, u32[]{:S(2)}, u32[]{:S(2)}) collective-permute-start(bf16[96,128]{1,0:T(8,128)(2,1)S(1)} %get-tuple-element.23), channel_id=1, source_target_pairs={{0,1},{1,0},{2,3},{3,2},{4,5},{5,4},{6,7},{7,6},{8,9},{9,8},{10,11... | collective-permute-start | bytes 73736 | tf_op jit(solution)/shard_map/ppermute | solution.py:655
  24.9 9.4 %collective-permute-start.3 = (bf16[96,128]{1,0:T(8,128)(2,1)S(1)}, bf16[96,128]{1,0:T(8,128)(2,1)S(1)}, u32[]{:S(2)}, u32[]{:S(2)}) collective-permute-start(bf16[96,128]{1,0:T(8,128)(2,1)S(1)} %get-tuple-element.24), channel_id=1, source_target_pairs={{0,3},{1,2},{2,1},{3,0},{4,7},{5,6},{6,5},{7,4},{8,11},{9,10},{10,... | collective-permute-start | bytes 73736 | tf_op jit(solution)/shard_map/ppermute | solution.py:652
  36.9 20.9 %collective-permute-start.11 = (bf16[832,256]{1,0:T(8,128)(2,1)S(1)}, bf16[832,256]{1,0:T(8,128)(2,1)S(1)}, u32[]{:S(2)}, u32[]{:S(2)}) collective-permute-start(bf16[832,256]{1,0:T(8,128)(2,1)S(1)} %get-tuple-element.29.refs_7_.refs_3_), channel_id=1, source_target_pairs={{0,2},{1,3},{2,0},{3,1},{4,6},{5,7},{6,4},{7,5},{8,10},{9,11},{10,... | collective-permute-start | bytes 1277960 | tf_op jit(solution)/shard_map/ppermute | solution.py:570
  37.3 20.6 %collective-permute-start.7 = (bf16[832,256]{1,0:T(8,128)(2,1)S(1)}, bf16[832,256]{1,0:T(8,128)(2,1)S(1)}, u32[]{:S(2)}, u32[]{:S(2)}) collective-permute-start(bf16[832,256]{1,0:T(8,128)(2,1)S(1)} %get-tuple-element.33.refs_3_), channel_id=1, source_target_pairs={{0,1},{1,0},{2,3},{3,2},{4,5},{5,4},{6,7},{7,6},{8,9},{9,8},{10,11... | collective-permute-start | bytes 1277960 | tf_op jit(solution)/shard_map/ppermute | solution.py:570
  39.0 14.7 %collective-permute-start.8 = (bf16[6,96,256]{2,1,0:T(8,128)(2,1)S(1)}, bf16[6,96,256]{2,1,0:T(8,128)(2,1)S(1)}, u32[]{:S(2)}, u32[]{:S(2)}) collective-permute-start(bf16[6,96,256]{2,1,0:T(8,128)(2,1)S(1)} %get-tuple-element.26.refs_4_.refs_0_), channel_id=1, source_target_pairs={{0,2},{1,3},{2,0},{3,1},{4,6},{5,7},{6,4},{7,5},{8,10},{9,11},{10,... | collective-permute-start | bytes 884744 | tf_op jit(solution)/shard_map/ppermute | solution.py:570
  53.7 6.6 %collective-permute-start.5 = (bf16[6,32,256]{2,1,0:T(8,128)(2,1)S(1)}, bf16[6,32,256]{2,1,0:T(8,128)(2,1)S(1)}, u32[]{:S(2)}, u32[]{:S(2)}) collective-permute-start(bf16[6,32,256]{2,1,0:T(8,128)(2,1)S(1)} %get-tuple-element.31.refs_1_.refs_5_), channel_id=1, source_target_pairs={{0,1},{1,0},{2,3},{3,2},{4,5},{5,4},{6,7},{7,6},{8,9},{9,8},{10,11... | collective-permute-start | bytes 294920 | tf_op jit(solution)/shard_map/ppermute | solution.py:570
  55.2 5.1 %collective-permute-start.9 = (bf16[6,32,256]{2,1,0:T(8,128)(2,1)S(1)}, bf16[6,32,256]{2,1,0:T(8,128)(2,1)S(1)}, u32[]{:S(2)}, u32[]{:S(2)}) collective-permute-start(bf16[6,32,256]{2,1,0:T(8,128)(2,1)S(1)} %get-tuple-element.27.refs_5_.refs_1_.refs_9_), channel_id=1, source_target_pairs={{0,2},{1,3},{2,0},{3,1},{4,6},{5,7},{6,4},{7,5},{8,10},{9,11},{10,... | collective-permute-start | bytes 294920 | tf_op jit(solution)/shard_map/ppermute | solution.py:570
  62.2 12.1 %all-to-all-start = ((f32[32,1,64]{2,1,0:T(1,128)}), f32[32,1,64]{2,1,0:T(1,128)S(1)}, u32[]{:S(2)}, u32[]{:S(2)}) async-start(f32[32,1,64]{2,1,0:T(1,128)} %shard_map.66), calls=%async_computation | async-start | bytes 32768 | tf_op jit(solution)/shard_map/all_to_all | solution.py:748
